TPU v7x, 512 devices: a whole 4x4x16 slice. The times are simulated.
512 devices in a mesh: row: 32 (over y, x, core), col: 16 (over z).
Axes of the slice: x: 4, y: 4, z: 16, core: 2. Of those that a mesh axis runs over, the one named last changes fastest.
Arguments:
- front: float32 [4, 32, 128, 8, 16, 128], P(None, 'row', None, None, 'col'), may hold values from 0 to 1, as said below
- support: float32 [4, 32, 128], P(None, 'row'), may hold values from 0.5 to 2
- mask: int32 [128, 128], replicated, may hold values from 0 to 1, as said below
- rhs: float32 [512, 4, 32, 128], P('col', None, 'row'), may hold values from -6 to 6
Outputs:
- factor: float32 [4, 32, 128, 8, 16, 128], P(None, 'row', None, None, 'col')
- solved: float32 [512, 4, 32, 128], P('col', None, 'row')
Inputs may be any that keep to these rules, and one draw needn't show every extreme that they name: mask[I, J] is 1 exactly when block rows I and J carry the same one of three subtree labels; it is symmetric with ones on the diagonal. front is symmetric and positive semidefinite with ones on its diagonal.
All inputs are finite; a program needn't handle non-finite values.
Results may differ from a plain program's by a relative error of at most 0.000057.
Values sent between devices are 32-bit elements; how exact they have to be, the bound alone decides.
No kernel may reach another device: no remote copies, remote signals or barrier semaphores. Data moves between devices by JAX's collectives and lax.ppermute only.
A program may use at most 64 MiB of HBM per device.

v0:
```python
import jax
import jax.numpy as jnp
from jax import lax
from jax.sharding import PartitionSpec as P

KB = 3


precise = lax.Precision.HIGHEST


def broadcast(x, axis, root):
    mine = lax.axis_index(axis) == root
    return lax.psum(jnp.where(mine, x, jnp.zeros_like(x)), axis)


def factor_panel(matrix, panel_id, row_ids):
    row_count = lax.axis_size("row")
    col_count = lax.axis_size("col")
    col_index = lax.axis_index("col")
    repeats = row_count // col_count
    block_size = matrix.shape[1]
    cols_dev = matrix.shape[2]
    local_col = panel_id // col_count
    local_row = panel_id // row_count
    panel_cols = lax.dynamic_index_in_dim(matrix, local_col, 2, keepdims=False)
    diag_piece = lax.dynamic_index_in_dim(panel_cols, local_row, 0, keepdims=False)
    diag_piece = broadcast(diag_piece, "row", panel_id % row_count)
    diag_factor = jnp.linalg.cholesky(diag_piece)
    flat_rows = panel_cols.reshape(-1, block_size)
    solved = jax.scipy.linalg.solve_triangular(diag_factor, flat_rows.T, lower=True).T.reshape(
        panel_cols.shape
    )
    below_mask = (row_ids > panel_id)[:, None, None]
    at_mask = (row_ids == panel_id)[:, None, None]
    column = jnp.where(below_mask, solved, jnp.where(at_mask, diag_factor[None], 0.0))
    column, diag_factor = (
        broadcast(column, "col", panel_id % col_count),
        broadcast(diag_factor, "col", panel_id % col_count),
    )
    strict = jnp.where(below_mask, column, 0.0)
    pieces = []
    for copy_index in range(repeats):
        pieces.append(broadcast(strict, "row", col_index + copy_index * col_count))
    across = jnp.stack(pieces, axis=1).reshape(cols_dev, block_size, block_size)
    written = jnp.where(col_index == panel_id % col_count, column, panel_cols)
    matrix = lax.dynamic_update_index_in_dim(matrix, written, local_col, 2)
    return (matrix, (strict, across, diag_factor))


def subtract(matrix, strict, across, keep_cols):
    update_term = jnp.einsum(
        "lab,mcb->lamc", strict, across * keep_cols[:, None, None], precision=precise
    )
    return matrix - update_term


def apply_block(values, panel_id, rhs_piece, strict, diag_factor):
    row_count = lax.axis_size("row")
    local_row = panel_id // row_count
    found_rows = jax.scipy.linalg.solve_triangular(diag_factor, rhs_piece.T, lower=True).T
    values = values - jnp.einsum("ab,lcb->alc", found_rows, strict, precision=precise)
    current = lax.dynamic_index_in_dim(values, local_row, 1, keepdims=False)
    placed = jnp.where(lax.axis_index("row") == panel_id % row_count, found_rows, current)
    return lax.dynamic_update_index_in_dim(values, placed, local_row, 1)


def shards(front, support, mask, rhs):
    row_count = lax.axis_size("row")
    col_count = lax.axis_size("col")
    row_index = lax.axis_index("row")
    col_index = lax.axis_index("col")
    rows_dev = front.shape[0]
    block_size = front.shape[2]
    cols_dev = front.shape[3]
    all_ids = jnp.arange(rows_dev * row_count, dtype=jnp.int32)
    row_ids = jnp.arange(rows_dev, dtype=jnp.int32) * row_count + row_index
    col_ids = jnp.arange(cols_dev, dtype=jnp.int32) * col_count + col_index
    pick_rows = (row_ids[:, None] == all_ids[None, :]).astype(jnp.float32)
    pick_cols = (col_ids[:, None] == all_ids[None, :]).astype(jnp.float32)
    pattern = jnp.dot(
        jnp.dot(pick_rows, mask.astype(jnp.float32), precision=precise),
        pick_cols.T,
        precision=precise,
    )
    matrix = front[:, 0, :, :, 0, :] * pattern[:, None, :, None]
    on_diag = (row_ids[:, None] == col_ids[None, :]).astype(jnp.float32)
    identity = jnp.eye(block_size, dtype=jnp.float32)
    diag_add = support[:, 0, :][:, :, None, None] * identity[None, :, None, :]
    matrix = matrix + on_diag[:, None, :, None] * diag_add
    values = rhs[:, :, 0, :]

    def plain_step(panel_id, loop_state):
        matrix, values = loop_state
        matrix, panel_set = factor_panel(matrix, panel_id, row_ids)
        strict, across, diag_factor = panel_set
        matrix = subtract(matrix, strict, across, (col_ids > panel_id).astype(jnp.float32))
        return (matrix, values)

    matrix, values = lax.fori_loop(0, KB, plain_step, (matrix, values))

    def solve_step(panel_id, values):
        local_col = panel_id // col_count
        local_row = panel_id // row_count
        column = lax.dynamic_index_in_dim(matrix, local_col, 2, keepdims=False)
        column = broadcast(column, "col", panel_id % col_count)
        strict = jnp.where((row_ids > panel_id)[:, None, None], column, 0.0)
        rhs_piece = lax.dynamic_index_in_dim(values, local_row, 1, keepdims=False)
        diag_piece = lax.dynamic_index_in_dim(column, local_row, 0, keepdims=False)
        rhs_piece, diag_factor = (
            broadcast(rhs_piece, "row", panel_id % row_count),
            broadcast(diag_piece, "row", panel_id % row_count),
        )
        return apply_block(values, panel_id, rhs_piece, strict, diag_factor)

    values = lax.fori_loop(0, KB, solve_step, values)
    keep_blocks = (col_ids[None, :] < KB) & (row_ids[:, None] >= col_ids[None, :]) | (
        col_ids[None, :] >= KB
    ) & (row_ids[:, None] >= KB)
    result = jnp.where(keep_blocks[:, None, :, None], matrix, 0.0)
    return (result.reshape(front.shape), values.reshape(rhs.shape))


def solution(mesh):
    placed = (
        P(None, "row", None, None, "col", None),
        P(None, "row", None),
        P(),
        P("col", None, "row", None),
    )
    return jax.shard_map(
        shards,
        mesh=mesh,
        in_specs=placed,
        out_specs=(P(None, "row", None, None, "col", None), P("col", None, "row", None)),
        check_vma=False,
    )
```

profile of v0, /device:TPU:1, one launch (start us, length us, event | category | flops | bytes accessed | tf_op | source)
XLA Modules:
  0.0 2161.0 jit_solution(15343242638407862423)
XLA Ops:
  15.8 1301.3 %while.34 = (s32[]{:T(128)}, f32[4,128,8,128]{1,3,2,0:T(8,128)S(1)}, s32[]{:T(128)}, s32[]{:T(128)}, s32[]{:T(128)}, /*index=5*/s32[]{:T(128)}, s32[]{:T(128)}, ...) while((s32[]{:T(128)}, ...), condition=%wide.region_7.8_spmd.clone, body=%wide.region_0.7_spmd.clone.sunk | while | flops 907657408 | bytes 35063672 | solution.py:100
  16.8 135.6 %all-reduce.9.cloned.1.call-done = f32[128,128]{0,1:T(8,128)} async-done(((f32[128,128]{0,1:T(8,128)}), f32[128,128]{0,1:T(8,128)}) %all-reduce.9.cloned.1.call-update) | async-done | bytes 65552 | tf_op jit(solution)/shard_map/while/body/eval_jaxpr/psum | solution.py:14
  154.3 11.7 cholesky.56
  167.3 9.8 custom-call.39
  178.5 125.1 %all-reduce.11.cloned.1.call-done = f32[4,128,128]{2,1,0:T(8,128)} async-done(((f32[4,128,128]{2,1,0:T(8,128)}), f32[4,128,128]{2,1,0:T(8,128)}) %all-reduce.11.cloned.1.call-update) | async-done | bytes 262160 | tf_op jit(solution)/shard_map/while/body/eval_jaxpr/psum | solution.py:14
  307.6 139.6 %all-reduce.13.cloned.1.call-done = (f32[4,1,128,128]{3,2,0,1:T(8,128)}, f32[4,1,128,128]{3,2,0,1:T(8,128)}) async-done(((f32[4,1,128,128]{3,2,0,1:T(8,128)}, f32[4,1,128,128]{3,2,0,1:T(8,128)}), (f32[4,1,128,128]{3,2,0,1:T(8,128)}, f32[4,1,128,128]{3,2,0,1:T(8,128)})) %all-reduce.13.cloned.1.call-update) | async-done | bytes 524304 | tf_op jit(solution)/shard_map/while/body/eval_jaxpr/psum | solution.py:14
  454.5 129.6 %all-reduce.9.cloned.1.call-done = f32[128,128]{0,1:T(8,128)} async-done(((f32[128,128]{0,1:T(8,128)}), f32[128,128]{0,1:T(8,128)}) %all-reduce.9.cloned.1.call-update) | async-done | bytes 65552 | tf_op jit(solution)/shard_map/while/body/eval_jaxpr/psum | solution.py:14
  586.0 11.7 cholesky.56
  599.0 9.8 custom-call.39
  610.2 125.1 %all-reduce.11.cloned.1.call-done = f32[4,128,128]{2,1,0:T(8,128)} async-done(((f32[4,128,128]{2,1,0:T(8,128)}), f32[4,128,128]{2,1,0:T(8,128)}) %all-reduce.11.cloned.1.call-update) | async-done | bytes 262160 | tf_op jit(solution)/shard_map/while/body/eval_jaxpr/psum | solution.py:14
  739.3 139.4 %all-reduce.13.cloned.1.call-done = (f32[4,1,128,128]{3,2,0,1:T(8,128)}, f32[4,1,128,128]{3,2,0,1:T(8,128)}) async-done(((f32[4,1,128,128]{3,2,0,1:T(8,128)}, f32[4,1,128,128]{3,2,0,1:T(8,128)}), (f32[4,1,128,128]{3,2,0,1:T(8,128)}, f32[4,1,128,128]{3,2,0,1:T(8,128)})) %all-reduce.13.cloned.1.call-update) | async-done | bytes 524304 | tf_op jit(solution)/shard_map/while/body/eval_jaxpr/psum | solution.py:14
  886.1 130.0 %all-reduce.9.cloned.1.call-done = f32[128,128]{0,1:T(8,128)} async-done(((f32[128,128]{0,1:T(8,128)}), f32[128,128]{0,1:T(8,128)}) %all-reduce.9.cloned.1.call-update) | async-done | bytes 65552 | tf_op jit(solution)/shard_map/while/body/eval_jaxpr/psum | solution.py:14
  1017.9 11.7 cholesky.56
  1030.9 9.8 custom-call.39
  1042.1 125.1 %all-reduce.11.cloned.1.call-done = f32[4,128,128]{2,1,0:T(8,128)} async-done(((f32[4,128,128]{2,1,0:T(8,128)}), f32[4,128,128]{2,1,0:T(8,128)}) %all-reduce.11.cloned.1.call-update) | async-done | bytes 262160 | tf_op jit(solution)/shard_map/while/body/eval_jaxpr/psum | solution.py:14
  1171.2 139.6 %all-reduce.13.cloned.1.call-done = (f32[4,1,128,128]{3,2,0,1:T(8,128)}, f32[4,1,128,128]{3,2,0,1:T(8,128)}) async-done(((f32[4,1,128,128]{3,2,0,1:T(8,128)}, f32[4,1,128,128]{3,2,0,1:T(8,128)}), (f32[4,1,128,128]{3,2,0,1:T(8,128)}, f32[4,1,128,128]{3,2,0,1:T(8,128)})) %all-reduce.13.cloned.1.call-update) | async-done | bytes 524304 | tf_op jit(solution)/shard_map/while/body/eval_jaxpr/psum | solution.py:14
  1322.1 831.7 %while.35 = (s32[]{:T(128)}, f32[32,4,128]{2,0,1:T(8,128)S(1)}, f32[4,128,8,128]{1,3,2,0:T(8,128)S(1)}, s32[]{:T(128)}, s32[]{:T(128)}, /*index=5*/s32[]{:T(128)...) while((s32[]{:T(128)}, f32[32,4,128]{2,0,1:T(8,128)S(1)}, ...), condition=%wide.region_12.13_spmd.clone, body=%wide.region_8.12_spmd.clone.sunk | while | flops 31748144 | bytes 4457076 | solution.py:116
  1323.4 127.8 %all-reduce.15.cloned.1.call-done = f32[4,128,128]{2,1,0:T(8,128)} async-done(((f32[4,128,128]{2,1,0:T(8,128)}), f32[4,128,128]{2,1,0:T(8,128)}) %all-reduce.15.cloned.1.call-update) | async-done | bytes 262160 | tf_op jit(solution)/shard_map/while/body/eval_jaxpr/psum | solution.py:14
  1452.7 128.1 %psum.120 = f32[32,128]{1,0:T(8,128)S(1)} all-reduce(f32[32,128]{1,0:T(8,128)S(1)} %select_bitcast_fusion.19), channel_id=1, replica_groups=mesh['row'=32,'col'=16] {'row'}, use_global_device_ids=true, to_apply=%region_11.11 | all-reduce | flops 4096 | bytes 32768 | tf_op jit(solution)/shard_map/while/body/eval_jaxpr/psum | solution.py:14
  1588.8 9.8 custom-call.40
  1601.3 126.7 %all-reduce.15.cloned.1.call-done = f32[4,128,128]{2,1,0:T(8,128)} async-done(((f32[4,128,128]{2,1,0:T(8,128)}), f32[4,128,128]{2,1,0:T(8,128)}) %all-reduce.15.cloned.1.call-update) | async-done | bytes 262160 | tf_op jit(solution)/shard_map/while/body/eval_jaxpr/psum | solution.py:14
  1729.5 128.1 %psum.120 = f32[32,128]{1,0:T(8,128)S(1)} all-reduce(f32[32,128]{1,0:T(8,128)S(1)} %select_bitcast_fusion.19), channel_id=1, replica_groups=mesh['row'=32,'col'=16] {'row'}, use_global_device_ids=true, to_apply=%region_11.11 | all-reduce | flops 4096 | bytes 32768 | tf_op jit(solution)/shard_map/while/body/eval_jaxpr/psum | solution.py:14
  1878.2 126.7 %all-reduce.15.cloned.1.call-done = f32[4,128,128]{2,1,0:T(8,128)} async-done(((f32[4,128,128]{2,1,0:T(8,128)}), f32[4,128,128]{2,1,0:T(8,128)}) %all-reduce.15.cloned.1.call-update) | async-done | bytes 262160 | tf_op jit(solution)/shard_map/while/body/eval_jaxpr/psum | solution.py:14
  2006.4 128.1 %psum.120 = f32[32,128]{1,0:T(8,128)S(1)} all-reduce(f32[32,128]{1,0:T(8,128)S(1)} %select_bitcast_fusion.19), channel_id=1, replica_groups=mesh['row'=32,'col'=16] {'row'}, use_global_device_ids=true, to_apply=%region_11.11 | all-reduce | flops 4096 | bytes 32768 | tf_op jit(solution)/shard_map/while/body/eval_jaxpr/psum | solution.py:14
  (158 shorter events, 117.1 us)
Async XLA Ops:
  7.2 6.1 copy-start.4
  7.2 6.3 copy-start.2
  15.8 289.6 %copy-start = (f32[4,128,8,128]{1,3,2,0:T(8,128)}, f32[4,128,8,128]{1,3,2,0:T(8,128)S(1)}, u32[]{:S(2)}) copy-start(f32[4,128,8,128]{1,3,2,0:T(8,128)S(1)} %get-tuple-element.448) | copy-start | bytes 6291460 | tf_op jit(solution)/shard_map/while
  15.8 136.7 %all-reduce.9.cloned.1.call-start = ((), (), s32[]{:S(2)}) async-start(), calls=%async_computation | async-start | bytes 131072 | tf_op jit(solution)/shard_map/while/body/eval_jaxpr/psum | solution.py:14
  16.7 286.8 %all-reduce.11.cloned.1.call-start = ((), (), s32[]{:S(2)}) async-start(), calls=%async_computation.1 | async-start | bytes 524288 | tf_op jit(solution)/shard_map/while/body/eval_jaxpr/psum | solution.py:14
  178.4 268.7 %all-reduce.13.cloned.1.call-start = ((), (), s32[]{:S(2)}) async-start(), calls=%async_computation.2 | async-start | bytes 1048576 | tf_op jit(solution)/shard_map/while/body/eval_jaxpr/psum | solution.py:14
  305.4 2.1 copy-start.1
  453.5 283.6 %copy-start = (f32[4,128,8,128]{1,3,2,0:T(8,128)}, f32[4,128,8,128]{1,3,2,0:T(8,128)S(1)}, u32[]{:S(2)}) copy-start(f32[4,128,8,128]{1,3,2,0:T(8,128)S(1)} %get-tuple-element.448) | copy-start | bytes 6291460 | tf_op jit(solution)/shard_map/while
  453.5 130.7 %all-reduce.9.cloned.1.call-start = ((), (), s32[]{:S(2)}) async-start(), calls=%async_computation | async-start | bytes 131072 | tf_op jit(solution)/shard_map/while/body/eval_jaxpr/psum | solution.py:14
  454.4 280.8 %all-reduce.11.cloned.1.call-start = ((), (), s32[]{:S(2)}) async-start(), calls=%async_computation.1 | async-start | bytes 524288 | tf_op jit(solution)/shard_map/while/body/eval_jaxpr/psum | solution.py:14
  610.1 268.6 %all-reduce.13.cloned.1.call-start = ((), (), s32[]{:S(2)}) async-start(), calls=%async_computation.2 | async-start | bytes 1048576 | tf_op jit(solution)/shard_map/while/body/eval_jaxpr/psum | solution.py:14
  737.1 2.1 copy-start.1
  885.0 284.0 %copy-start = (f32[4,128,8,128]{1,3,2,0:T(8,128)}, f32[4,128,8,128]{1,3,2,0:T(8,128)S(1)}, u32[]{:S(2)}) copy-start(f32[4,128,8,128]{1,3,2,0:T(8,128)S(1)} %get-tuple-element.448) | copy-start | bytes 6291460 | tf_op jit(solution)/shard_map/while
  885.1 131.0 %all-reduce.9.cloned.1.call-start = ((), (), s32[]{:S(2)}) async-start(), calls=%async_computation | async-start | bytes 131072 | tf_op jit(solution)/shard_map/while/body/eval_jaxpr/psum | solution.py:14
  886.0 281.2 %all-reduce.11.cloned.1.call-start = ((), (), s32[]{:S(2)}) async-start(), calls=%async_computation.1 | async-start | bytes 524288 | tf_op jit(solution)/shard_map/while/body/eval_jaxpr/psum | solution.py:14
  1042.1 268.7 %all-reduce.13.cloned.1.call-start = ((), (), s32[]{:S(2)}) async-start(), calls=%async_computation.2 | async-start | bytes 1048576 | tf_op jit(solution)/shard_map/while/body/eval_jaxpr/psum | solution.py:14
  1169.1 2.1 copy-start.1
  1318.9 3.1 copy-start.3
  1322.3 128.9 %all-reduce.15.cloned.1.call-start = ((), (), s32[]{:S(2)}) async-start(), calls=%async_computation.3 | async-start | bytes 524288 | tf_op jit(solution)/shard_map/while/body/eval_jaxpr/psum | solution.py:14
  1323.3 264.7 %all-reduce.17.cloned.1.call-start = ((), (), s32[]{:S(2)}) async-start(), calls=%async_computation.4 | async-start | bytes 131072 | tf_op jit(solution)/shard_map/while/body/eval_jaxpr/psum | solution.py:14
  1600.3 127.8 %all-reduce.15.cloned.1.call-start = ((), (), s32[]{:S(2)}) async-start(), calls=%async_computation.3 | async-start | bytes 524288 | tf_op jit(solution)/shard_map/while/body/eval_jaxpr/psum | solution.py:14
  1601.2 263.6 %all-reduce.17.cloned.1.call-start = ((), (), s32[]{:S(2)}) async-start(), calls=%async_computation.4 | async-start | bytes 131072 | tf_op jit(solution)/shard_map/while/body/eval_jaxpr/psum | solution.py:14
  1877.1 127.8 %all-reduce.15.cloned.1.call-start = ((), (), s32[]{:S(2)}) async-start(), calls=%async_computation.3 | async-start | bytes 524288 | tf_op jit(solution)/shard_map/while/body/eval_jaxpr/psum | solution.py:14
  1878.1 263.4 %all-reduce.17.cloned.1.call-start = ((), (), s32[]{:S(2)}) async-start(), calls=%async_computation.4 | async-start | bytes 131072 | tf_op jit(solution)/shard_map/while/body/eval_jaxpr/psum | solution.py:14
Sparse Core Ops, SparseCore 0:
  20.5 131.9 all-reduce.8
  178.6 124.9 all-reduce.10
  306.8 140.3 all-reduce.12
  457.9 126.2 all-reduce.8
  610.3 124.9 all-reduce.10
  738.3 140.3 all-reduce.12
  889.7 126.3 all-reduce.8
  1042.2 124.9 all-reduce.10
  1170.4 140.3 all-reduce.12
  1325.2 125.8 all-reduce.14
  1455.0 132.9 all-reduce.16
  1603.2 124.7 all-reduce.14
  1731.8 132.9 all-reduce.16
  1880.1 124.7 all-reduce.14
  2008.6 132.9 all-reduce.16
where the time goes:
time: 2160 us
  waiting for transfers between devices  1590 us (74%)
  blocking collectives  384 us (18%)
  other arithmetic  127 us (6%)
  local copies, waits for them, and re-layouts  24.1 us (1%)
    psum x15, waiting for transfers between devices, broadcast(): return lax.psum(jnp.where(mine, x, jnp.zeros_like(x)), axis)  1590 us
    psum x3, blocking collectives, broadcast(): return lax.psum(jnp.where(mine, x, jnp.zeros_like(x)), axis)  384 us
  transfers between devices with their start and end apart: 15, of which 15 were waited for; matrix products, arithmetic and copies ran while one was open for 0% of the time, Pallas kernels for 0%

commit v1 on v0

v1 whole, which is shorter than its diff:
```python
import jax
import jax.numpy as jnp
from jax import lax
from jax.sharding import PartitionSpec as P

KB = 3


precise = lax.Precision.HIGHEST


def mm(a, b):
    return jnp.dot(a, b, precision=precise, preferred_element_type=jnp.float32)


def shards(front, support, mask, rhs):
    n_row = lax.axis_size("row")
    n_col = lax.axis_size("col")
    p = lax.axis_index("row")
    q = lax.axis_index("col")
    rows_dev = front.shape[0]
    blk = front.shape[2]
    cols_dev = front.shape[3]
    halves = n_row // n_col
    sub = blk // n_row
    row_ids = jnp.arange(rows_dev, dtype=jnp.int32) * n_row + p
    col_ids = jnp.arange(cols_dev, dtype=jnp.int32) * n_col + q
    mask_rows = lax.dynamic_index_in_dim(mask.reshape(rows_dev, n_row, -1), p, 1, keepdims=False)
    pattern = lax.dynamic_index_in_dim(
        mask_rows.reshape(rows_dev, cols_dev, n_col), q, 2, keepdims=False
    ).astype(jnp.float32)
    on_diag = (row_ids[:, None] == col_ids[None, :]).astype(jnp.float32)
    x = front[:, 0, :, :, 0, :]
    eye = jnp.eye(blk, dtype=jnp.float32)
    diag_add = support[:, 0, :][:, :, None] * eye[None]
    matrix = x * pattern[:, None, :, None] + on_diag[:, None, :, None] * diag_add[:, :, None, :]
    values = rhs[:, :, 0, :]

    top = matrix[0].reshape(n_row, sub * cols_dev, blk)
    sent = jnp.concatenate([top, values[:, 0, :].reshape(n_row, -1, blk)], axis=1)
    got = lax.all_to_all(sent, "row", 0, 0)[:KB]
    mine = got[:, : sub * cols_dev]
    mine_rhs = got[:, sub * cols_dev :]
    every = lax.all_gather(mine, "col")
    every = every.reshape(n_col, KB, sub, rows_dev, halves, blk)
    to_rows = every.transpose(4, 0, 1, 2, 3, 5).reshape(n_row, KB * sub * rows_dev, blk)
    diag_part = every[:KB, :, :, 0, 0].transpose(1, 2, 0, 3).reshape(KB * sub * KB, blk)
    shared = jnp.concatenate([mine.reshape(-1, blk), diag_part, mine_rhs.reshape(-1, blk)], axis=0)
    sent = jnp.concatenate(
        [to_rows, jnp.broadcast_to(shared[None], (n_row,) + shared.shape)], axis=1
    )
    got = lax.all_to_all(sent, "row", 0, 0)
    size = KB * blk

    def lay(part, wide):
        part = part.reshape(n_row, KB, sub, wide, blk)
        return part.transpose(1, 0, 2, 3, 4).reshape(size, wide * blk)

    ends = [KB * sub * rows_dev, KB * sub * cols_dev, KB * sub * KB, KB * mine_rhs.shape[1]]
    at = [0]
    for e in ends:
        at.append(at[-1] + e)
    row_panel = lay(got[:, at[0] : at[1]], rows_dev)
    col_panel = lay(got[:, at[1] : at[2]], cols_dev)
    diag = lay(got[:, at[2] : at[3]], KB)
    first_rhs = got[:, at[3] : at[4]].reshape(n_row, KB, -1, blk).transpose(0, 2, 1, 3)
    first_rhs = first_rhs.reshape(values.shape[0], size)

    factor = jnp.linalg.cholesky(diag)
    inverse = jax.scipy.linalg.solve_triangular(factor, jnp.eye(size, dtype=jnp.float32), lower=True)
    row_solved = mm(inverse, row_panel)
    col_solved = mm(inverse, col_panel)
    found = lax.dot_general(
        first_rhs, inverse, (((1,), (1,)), ((), ())), precision=precise
    )

    update = lax.dot_general(
        row_solved.reshape(size, rows_dev, blk),
        col_solved.reshape(size, cols_dev, blk),
        (((0,), (0,)), ((), ())),
        precision=precise,
    )
    schur = matrix - update
    own_l11 = lax.dynamic_index_in_dim(
        lax.dynamic_index_in_dim(
            factor.reshape(KB, blk, KB, blk), jnp.minimum(p, KB - 1), 0, keepdims=False
        ),
        jnp.minimum(q, KB - 1),
        1,
        keepdims=False,
    )
    own_l21 = lax.dynamic_index_in_dim(
        row_solved.reshape(KB, blk, rows_dev, blk), jnp.minimum(q, KB - 1), 0, keepdims=False
    ).transpose(1, 2, 0)
    low = (row_ids < KB)[:, None, None, None]
    left = (col_ids < KB)[None, None, :, None]
    panel = jnp.where((row_ids < KB)[:, None, None], own_l11[None], own_l21)[:, :, None, :]
    result = jnp.where(left, panel, jnp.where(low, 0.0, schur))

    rest = values - mm(found, row_solved).reshape(values.shape)
    own_y1 = lax.dynamic_index_in_dim(
        found.reshape(-1, KB, blk), jnp.minimum(p, KB - 1), 1, keepdims=False
    )
    solved = jnp.where((row_ids < KB)[None, :, None], own_y1[:, None, :], rest)
    return (result.reshape(front.shape), solved.reshape(rhs.shape))


def solution(mesh):
    placed = (
        P(None, "row", None, None, "col", None),
        P(None, "row", None),
        P(),
        P("col", None, "row", None),
    )
    return jax.shard_map(
        shards,
        mesh=mesh,
        in_specs=placed,
        out_specs=(P(None, "row", None, None, "col", None), P("col", None, "row", None)),
        check_vma=False,
    )
```

time: 2160 us -> 259 us (0.12)
  waiting for transfers between devices: 1590 us -> 35.4 us
  blocking collectives: 384 us -> 54.3 us
  other arithmetic: 127 us -> 100 us
    psum x15 -> x0, waiting for transfers between devices: 1590 us -> none  [broadcast(): return lax.psum(jnp.where(mine, x, jnp.zeros_like(x)), axis)]
    psum x3 -> x0, blocking collectives: 384 us -> none  [broadcast(): return lax.psum(jnp.where(mine, x, jnp.zeros_like(x)), axis)]
    all_to_all x0 -> x1, waiting for transfers between devices: none -> 35.4 us  [shards(): got = lax.all_to_all(sent, 'row', 0, 0)]
    all_gather x0 -> x1, blocking collectives: none -> 31.7 us  [shards(): every = lax.all_gather(mine, 'col')]
    all_to_all x0 -> x1, blocking collectives: none -> 22.5 us  [shards(): got = lax.all_to_all(sent, 'row', 0, 0)[:KB]]
    another operation x27 -> x13, other arithmetic: 109 us -> 90.9 us  [the longest x10 57.6 us: shards(): factor = jnp.linalg.cholesky(diag)]
  transfers between devices with their start and end apart: 15 -> 1, of which waited for: 15 -> 1; matrix products, arithmetic and copies ran while one was open for 0% -> 1% of each run, Pallas kernels for 0% -> 0%
where the time goes in v1:
time: 259 us; the launch traced here: 255 us
  other arithmetic  100 us (39%)
  blocking collectives  54.3 us (21%)
  waiting for transfers between devices  35.4 us (14%)
  local copies, waits for them, and re-layouts  28.3 us (11%)
  matrix products  21.6 us (8%)
  starting transfers between devices  11.5 us (4%)
  between operations  3.38 us (1%)
    another operation x10, other arithmetic, shards(): factor = jnp.linalg.cholesky(diag)  57.6 us
    all_to_all x1, waiting for transfers between devices, shards(): got = lax.all_to_all(sent, 'row', 0, 0)  35.4 us
    another operation x3, other arithmetic, shards(): jax.scipy.linalg.solve_triangular(factor, jnp.eye(size, dtype=jnp.float32...  33.3 us
    all_gather x1, blocking collectives, shards(): every = lax.all_gather(mine, 'col')  31.7 us
    all_to_all x1, blocking collectives, shards(): got = lax.all_to_all(sent, 'row', 0, 0)[:KB]  22.5 us
    all_to_all x1, starting transfers between devices, shards(): got = lax.all_to_all(sent, 'row', 0, 0)  11.5 us
    another operation x9, local copies, waits for them, and re-layouts  10.5 us
    unnamed x33, local copies, waits for them, and re-layouts  7.7 us
  transfers between devices with their start and end apart: 1, of which 1 were waited for; matrix products, arithmetic and copies ran while one was open for 1% of the time, Pallas kernels for 0%

profile of v1, /device:TPU:1, one launch (start us, length us, event | category | flops | bytes accessed | tf_op | source)
XLA Modules:
  0.0 254.8 jit_solution(8226662271982599624)
XLA Ops:
  2.6 2.3 fusion
  6.3 22.5 %all_to_all.10 = f32[32,33,128]{2,1,0:T(8,128)S(1)} all-to-all(f32[32,33,128]{2,1,0:T(8,128)S(1)} %pad_maximum_fusion.1), channel_id=1, replica_groups=mesh['row'=32,'col'=16] {'row'}, dimensions={0} | all-to-all | bytes 1081344 | tf_op jit(solution)/shard_map/all_to_all | solution.py:41
  28.8 31.7 %all-gather = f32[48,32,128]{2,1,0:T(8,128)S(1)} all-gather(f32[3,32,128]{2,1,0:T(8,128)S(1)} %slice.133), channel_id=2, replica_groups=mesh['row'=32,'col'=16] {'col'}, dimensions={0}, use_global_device_ids=true | all-gather | bytes 835584 | tf_op jit(solution)/shard_map/all_gather | solution.py:44
  61.8 1.8 pad_maximum_fusion
  63.6 11.5 %all-to-all-start.1 = ((f32[32,183,128]{2,1,0:T(8,128)}), f32[32,183,128]{2,1,0:T(8,128)S(1)}, u32[]{:S(2)}, u32[]{:S(2)}) async-start(f32[32,183,128]{2,1,0:T(8,128)} %pad_maximum_fusion), calls=%async_computation.1 | async-start | bytes 6029312 | tf_op jit(solution)/shard_map/all_to_all | solution.py:52
  77.2 35.4 %all-to-all-done.1 = f32[32,183,128]{2,1,0:T(8,128)S(1)} async-done(((f32[32,183,128]{2,1,0:T(8,128)}), f32[32,183,128]{2,1,0:T(8,128)S(1)}, u32[]{:S(2)}, u32[]{:S(2)}) %all-to-all-start.1) | async-done | bytes 2998304 | tf_op jit(solution)/shard_map/all_to_all | solution.py:52
  115.3 2.1 copy.68
  119.6 11.7 %cholesky.80 = f32[128,128]{1,0:T(8,128)S(1)} custom-call(f32[128,128]{1,0:T(8,128)S(1)} %cholesky.198), custom_call_target="Cholesky" | custom-call | tf_op jit(solution)/shard_map/jit(cholesky)/cholesky | solution.py:69
  132.2 9.8 %custom-call.23 = f32[1,128,128]{1,2,0:T(8,128)S(1)} custom-call(f32[1,128,128]{2,1,0:T(8,128)S(1)} %get-tuple-element.38), custom_call_target="InvertDiagBlocksLowerTriangular" | custom-call | tf_op jit(solution)/shard_map/jit(cholesky)/cholesky | solution.py:69
  142.0 1.8 constant_dynamic-update-slice_fusion
  145.1 11.7 %cholesky.168 = f32[128,128]{1,0:T(8,128)S(1)} custom-call(f32[128,128]{1,0:T(8,128)S(1)} %cholesky.202), custom_call_target="Cholesky" | custom-call | tf_op jit(solution)/shard_map/jit(cholesky)/cholesky | solution.py:69
  157.4 10.0 %custom-call.24 = f32[1,128,128]{1,2,0:T(8,128)S(1)} custom-call(f32[1,128,128]{2,1,0:T(8,128)S(1)} %get-tuple-element.35), custom_call_target="InvertDiagBlocksLowerTriangular" | custom-call | tf_op jit(solution)/shard_map/jit(cholesky)/cholesky | solution.py:69
  169.5 11.7 %cholesky.187 = f32[128,128]{1,0:T(8,128)S(1)} custom-call(f32[128,128]{1,0:T(8,128)S(1)} %convolution_subtract_fusion.3), custom_call_target="Cholesky" | custom-call | tf_op jit(solution)/shard_map/jit(cholesky)/cholesky | solution.py:69
  185.1 2.2 fusion.8
  187.3 10.5 %while.1 = (s32[]{:T(128)}, f32[384,384]{1,0:T(8,128)}, s32[3,2]{0,1:T(2,128)S(1)}, f32[3,128,128]{2,1,0:T(8,128)}, s32[]{:T(128)}) while((s32[]{:T(128)}, f32[384,384]{1,0:T(8,128)}, s32[3,2]{0,1:T(2,128)S(1)}, f32[3,128,128]{2,1,0:T(8,128)}, s32[]{:T(128)}) %tuple.35), condition=%wide.while_cond, body=%wide.while_body.sunk | while | flops 2 | bytes 132705 | solution.py:70
  188.0 2.9 %bitcast_dynamic-update-slice_fusion.2 = f32[3,128,128]{2,1,0:T(8,128)} fusion(f32[3,128,128]{2,1,0:T(8,128)} %get-tuple-element.80, s32[]{:T(128)} %get-tuple-element.77, f32[384,384]{1,0:T(8,128)} %get-tuple-element.83, s32[]{:T(128)} %bitcast.117, s32[]{:T(128)} %bitcast.118), kind=kLoop, calls=%fused_computation.clone.1 | loop fusion | bytes 132608 | tf_op jit(solution)/shard_map/jit(_solve_triangular)/triangular_solve
  191.5 2.9 %bitcast_dynamic-update-slice_fusion.2 = f32[3,128,128]{2,1,0:T(8,128)} fusion(f32[3,128,128]{2,1,0:T(8,128)} %get-tuple-element.80, s32[]{:T(128)} %get-tuple-element.77, f32[384,384]{1,0:T(8,128)} %get-tuple-element.83, s32[]{:T(128)} %bitcast.117, s32[]{:T(128)} %bitcast.118), kind=kLoop, calls=%fused_computation.clone.1 | loop fusion | bytes 132608 | tf_op jit(solution)/shard_map/jit(_solve_triangular)/triangular_solve
  195.0 2.8 %bitcast_dynamic-update-slice_fusion.2 = f32[3,128,128]{2,1,0:T(8,128)} fusion(f32[3,128,128]{2,1,0:T(8,128)} %get-tuple-element.80, s32[]{:T(128)} %get-tuple-element.77, f32[384,384]{1,0:T(8,128)} %get-tuple-element.83, s32[]{:T(128)} %bitcast.117, s32[]{:T(128)} %bitcast.118), kind=kLoop, calls=%fused_computation.clone.1 | loop fusion | bytes 132608 | tf_op jit(solution)/shard_map/jit(_solve_triangular)/triangular_solve
  197.8 31.1 %custom-call.25 = f32[3,128,128]{1,2,0:T(8,128)} custom-call(f32[3,128,128]{2,1,0:T(8,128)} %get-tuple-element.9), custom_call_target="InvertDiagBlocksLowerTriangular" | custom-call | tf_op jit(solution)/shard_map/jit(_solve_triangular)/triangular_solve | solution.py:70
  232.6 1.5 convolution_subtract_fusion
  236.2 1.4 fusion.2
  242.7 3.9 %fusion.5 = f32[384,8,128]{2,0,1:T(8,128)S(1)} fusion(f32[8,128,384]{2,1,0:T(8,128)S(1)} %bitcast.123, f32[128,384]{1,0:T(8,128)} %copy-done.8, f32[128,384]{1,0:T(8,128)} %copy-done.5, f32[128,384]{1,0:T(8,128)S(1)} %fusion.14), kind=kOutput, calls=%fused_computation.19 | convolution fusion | flops 1812234240 | bytes 3735552 | tf_op jit(solution)/shard_map/dot_general | solution.py:13
  246.6 3.7 %select_bitcast_fusion = f32[4,1,128,8,1,128]{5,2,3,0,4,1:T(8,128)S(1)} fusion(f32[4,128,8,128]{3,1,2,0:T(8,128)S(1)} %copy-done.3, f32[384,4,128,1]{0,2,3,1:T(8,128)S(1)} %bitcast.131, f32[384,8,128]{2,0,1:T(8,128)S(1)} %fusion.5, f32[4,128,128]{2,1,0:T(8,128)S(1)} %copy-done.10, pred[4]{0:T(512)(128)(4,1)S(1)} %copy-done.12, pred[8]{0:T(512)(128)(4,1)S(1)} %copy-done.13), kind=kOutput, calls=%fused_computation.5 | convolution fusion | flops 2417491968 | bytes 6815756 | tf_op jit(solution)/shard_map/dot_general | solution.py:77
  250.3 3.5 %copy.77 = f32[4,1,128,8,1,128]{5,4,3,2,1,0:T(1,128)} copy(f32[4,1,128,8,1,128]{5,2,3,0,4,1:T(8,128)S(1)} %select_bitcast_fusion) | data formatting | bytes 4194304
  (105 shorter events, 31.5 us)
Async XLA Ops:
  0.6 0.8 copy-start
  4.9 23.9 %copy-start.2 = (f32[4,128,8,128]{3,1,2,0:T(8,128)}, f32[4,128,8,128]{3,1,2,0:T(8,128)S(1)}, u32[]{:S(2)}) copy-start(f32[4,128,8,128]{3,1,2,0:T(8,128)S(1)} %fusion) | copy-start | bytes 6291460
  63.6 48.9 %all-to-all-start.1 = ((f32[32,183,128]{2,1,0:T(8,128)}), f32[32,183,128]{2,1,0:T(8,128)S(1)}, u32[]{:S(2)}, u32[]{:S(2)}) async-start(f32[32,183,128]{2,1,0:T(8,128)} %pad_maximum_fusion), calls=%async_computation.1 | async-start | bytes 6029312 | tf_op jit(solution)/shard_map/all_to_all | solution.py:52
  112.5 122.9 %copy-start.1 = (f32[32,183,128]{2,1,0:T(8,128)}, f32[32,183,128]{2,1,0:T(8,128)S(1)}, u32[]{:S(2)}) copy-start(f32[32,183,128]{2,1,0:T(8,128)S(1)} %all-to-all-done.1) | copy-start | bytes 8994820
  113.1 1.3 copy-start.4
  118.8 0.8 copy-start.9
  232.6 3.6 %copy-start.5 = (f32[128,384]{1,0:T(8,128)}, f32[128,384]{1,0:T(8,128)S(1)}, u32[]{:S(2)}) copy-start(f32[128,384]{1,0:T(8,128)S(1)} %fusion.23) | copy-start | bytes 589828
  235.3 0.9 copy-start.8
  238.2 1.5 copy-start.7
  238.5 1.7 copy-start.12
  240.2 1.5 slice-start
  242.6 3.9 %copy-start.3 = (f32[4,128,8,128]{3,1,2,0:T(8,128)S(1)}, f32[4,128,8,128]{3,1,2,0:T(8,128)}, u32[]{:S(2)}) copy-start(f32[4,128,8,128]{3,1,2,0:T(8,128)} %copy-done.2) | copy-start | bytes 6291460
  242.6 3.9 %copy-start.6 = (f32[384,512]{0,1:T(8,128)S(1)}, f32[384,512]{0,1:T(8,128)}, u32[]{:S(2)}) copy-start(f32[384,512]{0,1:T(8,128)} %copy.79) | copy-start | bytes 2359300
  242.7 3.9 %copy-start.10 = (f32[4,128,128]{2,1,0:T(8,128)S(1)}, f32[4,128,128]{2,1,0:T(8,128)}, u32[]{:S(2)}) copy-start(f32[4,128,128]{2,1,0:T(8,128)} %copy.72) | copy-start | bytes 786436
  242.7 3.9 %copy-start.13 = (pred[8]{0:T(512)(128)(4,1)S(1)}, pred[8]{0:T(512)(128)(4,1)}, u32[]{:S(2)}) copy-start(pred[8]{0:T(512)(128)(4,1)} %broadcast_compare_fusion.1) | copy-start | bytes 28
  250.3 3.5 %copy-start.11 = (f32[32,4,1,128]{3,2,1,0:T(1,128)S(1)}, f32[32,4,1,128]{3,2,1,0:T(1,128)}, u32[]{:S(2)}) copy-start(f32[32,4,1,128]{3,2,1,0:T(1,128)} %param.7) | copy-start | bytes 196612

commit v2 on v1

v2 whole, which is shorter than its diff:
```python
import jax
import jax.numpy as jnp
from jax import lax
from jax.experimental import pallas as pl
from jax.experimental.pallas import tpu as pltpu
from jax.sharding import PartitionSpec as P

KB = 3
SPAN = 32
STEP = 8

precise = lax.Precision.HIGHEST


def tdot(a, b):
    return lax.dot_general(
        a, b, (((0,), (0,)), ((), ())), precision=precise, preferred_element_type=jnp.float32
    )


def ndot(a, b):
    return jnp.dot(a, b, precision=precise, preferred_element_type=jnp.float32)


def rdot(a, b):
    return lax.dot_general(
        a, b, (((1,), (1,)), ((), ())), precision=precise, preferred_element_type=jnp.float32
    )


def spread(x, row):
    return jnp.broadcast_to(x[row : row + 1, :], x.shape)


def eliminate_diagonal(aug_ref):
    blk = aug_ref.shape[0]
    sub = lax.broadcasted_iota(jnp.int32, (STEP, blk), 0)
    parts = SPAN // STEP
    for g in range(blk // SPAN):
        base = g * SPAN
        rows = [slice(base + STEP * j, base + STEP * (j + 1)) for j in range(parts)]
        left = [aug_ref[rows[j], :blk] for j in range(parts)]
        right = [aug_ref[rows[j], blk:] for j in range(parts)]
        for i in range(parts):
            c0 = base + STEP * i
            cols = [
                jnp.broadcast_to(left[i][:, c0 + u : c0 + u + 1], (STEP, blk)) for u in range(STEP)
            ]
            pivots = jnp.ones((STEP, blk), jnp.float32)
            inv = []
            tops = {}
            for t in range(STEP):
                pivot = spread(cols[t], t)
                pivots = jnp.where(sub == t, pivot, pivots)
                inv.append(1.0 / pivot)
                ratio = jnp.where(sub > t, cols[t] * inv[t], 0.0)
                for u in range(t + 1, STEP):
                    tops[t, u] = spread(cols[u], t)
                    cols[u] = cols[u] - ratio * tops[t, u]
                left[i] = left[i] - ratio * spread(left[i], t)
                right[i] = right[i] - ratio * spread(right[i], t)
            for j in range(i + 1, parts):
                below = [
                    jnp.broadcast_to(left[j][:, c0 + u : c0 + u + 1], (STEP, blk))
                    for u in range(STEP)
                ]
                for t in range(STEP):
                    ratio = below[t] * inv[t]
                    for u in range(t + 1, STEP):
                        below[u] = below[u] - ratio * tops[t, u]
                    left[j] = left[j] - ratio * spread(left[i], t)
                    right[j] = right[j] - ratio * spread(right[i], t)
            scale = lax.rsqrt(pivots)
            left[i] = left[i] * scale
            right[i] = right[i] * scale
        for j in range(parts):
            aug_ref[rows[j], :blk] = left[j]
            aug_ref[rows[j], blk:] = right[j]
        end = base + SPAN
        if end < blk:
            done = aug_ref[base:end, :]
            term = tdot(done[:, :blk], done)
            aug_ref[end:, :] = aug_ref[end:, :] - term[end:, :]


def factor_kernel(diag_ref, cols_ref, inv_ref, col_ref, found_ref, a_ref, c_ref, aug_ref):
    blk = aug_ref.shape[0]
    size = inv_ref.shape[0]
    wide = col_ref.shape[1] // blk
    count = found_ref.shape[0]
    pitch = KB * KB + 1
    for k in range(KB):
        for j in range(k, KB):
            a_ref[k * blk : (k + 1) * blk, j * blk : (j + 1) * blk] = diag_ref[
                pl.ds(k * KB + j, blk, stride=pitch), :
            ]
    inv_ref[...] = jnp.zeros(inv_ref.shape, jnp.float32)
    eye = lax.broadcasted_iota(jnp.int32, (blk, blk), 0) == lax.broadcasted_iota(
        jnp.int32, (blk, blk), 1
    )
    for k in range(KB):
        k0, k1 = k * blk, (k + 1) * blk
        aug_ref[:, :blk] = a_ref[k0:k1, k0:k1]
        aug_ref[:, blk:] = eye.astype(jnp.float32)
        eliminate_diagonal(aug_ref)
        own = aug_ref[:, blk:]
        if k > 0:
            inv_ref[k0:k1, :k0] = ndot(own, inv_ref[k0:k1, :k0])
        inv_ref[k0:k1, k0:k1] = own
        if k1 < size:
            up = ndot(own, a_ref[k0:k1, k1:])
            a_ref[k1:, k1:] = a_ref[k1:, k1:] - tdot(up, up)
            inv_ref[k1:, :k1] = inv_ref[k1:, :k1] - tdot(up, inv_ref[k0:k1, :k1])
    for k in range(KB):
        for m in range(wide):
            c_ref[k * blk : (k + 1) * blk, m * blk : (m + 1) * blk] = cols_ref[
                pl.ds(k * wide + m, blk, stride=KB * wide), :
            ]
    for k in range(KB):
        k0, k1 = k * blk, (k + 1) * blk
        col_ref[k0:k1, :] = ndot(inv_ref[k0:k1, :k1], c_ref[:k1, :])
    first = jnp.concatenate(
        [
            diag_ref[pl.ds(k * pitch + pitch - 1, count, stride=diag_ref.shape[0] // count), :]
            for k in range(KB)
        ],
        axis=1,
    )
    found_ref[...] = rdot(first, inv_ref[...])


def finish_kernel(
    where_ref, pattern_ref, x_ref, support_ref, rhs_ref, rows_ref, inv_ref, col_ref, found_ref,
    out_ref, solved_ref, t_ref, s_ref,
):
    step = pl.program_id(0)
    p = where_ref[0]
    q = where_ref[1]
    n_row = where_ref[2]
    n_col = where_ref[3]
    blk = support_ref.shape[1]
    rows_dev = support_ref.shape[0]
    wide = col_ref.shape[1] // blk
    count = found_ref.shape[0]

    @pl.when(step == 0)
    def _():
        for k in range(KB):
            for l in range(rows_dev):
                t_ref[k * blk : (k + 1) * blk, l * blk : (l + 1) * blk] = rows_ref[
                    pl.ds(k * rows_dev + l, blk, stride=KB * rows_dev), :
                ]
        for k in range(KB):
            k0, k1 = k * blk, (k + 1) * blk
            got = ndot(inv_ref[k0:k1, :k1], t_ref[:k1, :])
            for l in range(rows_dev):
                s_ref[l, k0:k1, :] = got[:, l * blk : (l + 1) * blk]
        for l in range(rows_dev):
            rest = rhs_ref[pl.ds(l, count, stride=rows_dev), :] - ndot(found_ref[...], s_ref[l])
            if l == 0:
                for k in range(KB):
                    rest = jnp.where(p == k, found_ref[:, k * blk : (k + 1) * blk], rest)
            solved_ref[pl.ds(l, count, stride=rows_dev), :] = rest

    ri = lax.broadcasted_iota(jnp.int32, (blk, blk), 0)
    ci = lax.broadcasted_iota(jnp.int32, (blk, blk), 1)
    mine = s_ref[step]
    term = tdot(mine, col_ref[...])
    row_id = step * n_row + p
    diag = jnp.where(ri == ci, jnp.broadcast_to(support_ref[pl.ds(step, 1), :], (blk, blk)), 0.0)
    for m in range(wide):
        col_id = m * n_col + q
        got = x_ref[pl.ds(m, blk, stride=wide), :] * pattern_ref[step * wide + m]
        got = got - term[:, m * blk : (m + 1) * blk]
        got = got + jnp.where(row_id == col_id, diag, 0.0)
        if m == 0:
            piece = mine[:blk, :]
            for k in range(1, KB):
                piece = jnp.where(q == k, mine[k * blk : (k + 1) * blk, :], piece)
            piece = piece.T
            piece = jnp.where((row_id == col_id) & (ri < ci), 0.0, piece)
            got = jnp.where(q < KB, piece, got)
        got = jnp.where((row_id < KB) & (col_id > row_id), 0.0, got)
        out_ref[pl.ds(m, blk, stride=wide), :] = got


def factor_call(diag, cols, wide, count):
    blk = diag.shape[1]
    size = KB * blk
    return pl.pallas_call(
        factor_kernel,
        out_shape=(
            jax.ShapeDtypeStruct((size, size), jnp.float32),
            jax.ShapeDtypeStruct((size, wide * blk), jnp.float32),
            jax.ShapeDtypeStruct((count, size), jnp.float32),
        ),
        scratch_shapes=[
            pltpu.VMEM((size, size), jnp.float32),
            pltpu.VMEM((size, wide * blk), jnp.float32),
            pltpu.VMEM((blk, 2 * blk), jnp.float32),
        ],
        compiler_params=pltpu.CompilerParams(vmem_limit_bytes=40 << 20),
        name="factor",
    )(diag, cols)


def finish_call(place, pattern, x, support, rhs, rows, inv, col, found):
    rows_dev, blk = support.shape
    size = inv.shape[0]
    part = x.shape[0] // rows_dev

    def whole(a):
        return pl.BlockSpec(a.shape, lambda i: (0, 0))

    scalars = pl.BlockSpec(memory_space=pltpu.SMEM)
    tile = pl.BlockSpec((part, blk), lambda i: (i, 0))
    return pl.pallas_call(
        finish_kernel,
        grid=(rows_dev,),
        in_specs=[scalars, scalars, tile, whole(support), whole(rhs), whole(rows), whole(inv),
                  whole(col), whole(found)],
        out_specs=(tile, whole(rhs)),
        out_shape=(
            jax.ShapeDtypeStruct(x.shape, jnp.float32),
            jax.ShapeDtypeStruct(rhs.shape, jnp.float32),
        ),
        scratch_shapes=[
            pltpu.VMEM((size, rows_dev * blk), jnp.float32),
            pltpu.VMEM((rows_dev, size, blk), jnp.float32),
        ],
        compiler_params=pltpu.CompilerParams(vmem_limit_bytes=40 << 20),
        name="finish",
    )(place, pattern, x, support, rhs, rows, inv, col, found)


def shards(front, support, mask, rhs):
    n_row = lax.axis_size("row")
    n_col = lax.axis_size("col")
    p = lax.axis_index("row")
    q = lax.axis_index("col")
    rows_dev = front.shape[0]
    blk = front.shape[2]
    cols_dev = front.shape[3]
    halves = n_row // n_col
    sub = blk // n_row
    count = rhs.shape[0]
    mask_rows = lax.dynamic_index_in_dim(mask.reshape(rows_dev, n_row, -1), p, 1, keepdims=False)
    pattern = lax.dynamic_index_in_dim(
        mask_rows.reshape(rows_dev, cols_dev, n_col), q, 2, keepdims=False
    ).astype(jnp.float32)
    place = jnp.stack([p, q, jnp.int32(n_row), jnp.int32(n_col)])
    x = front.reshape(rows_dev * blk * cols_dev, blk)
    values = rhs.reshape(count, rows_dev, blk)

    top = front[0, 0, :, :, 0, :] * pattern[0][None, :, None]
    shape = top.shape
    a_id = lax.broadcasted_iota(jnp.int32, shape, 0)
    m_id = lax.broadcasted_iota(jnp.int32, shape, 1)
    b_id = lax.broadcasted_iota(jnp.int32, shape, 2)
    at_diag = (a_id == b_id) & (m_id * n_col + q == p)
    top = top + jnp.where(at_diag, support[0, 0][None, None, :], 0.0)
    sent = jnp.concatenate(
        [top.reshape(n_row, sub * cols_dev, blk), values[:, 0, :].reshape(n_row, -1, blk)], axis=1
    )
    got = lax.all_to_all(sent, "row", 0, 0)[:KB]
    mine = got[:, : sub * cols_dev].reshape(KB, sub, cols_dev, blk).transpose(1, 0, 2, 3)
    mine = mine.reshape(sub * KB * cols_dev, blk)
    mine_rhs = got[:, sub * cols_dev :].reshape(KB, blk)

    def to_all(part):
        sent = jnp.broadcast_to(part[None], (n_row,) + part.shape)
        return lax.all_to_all(sent, "row", 0, 0).reshape(-1, blk)

    cols_got = to_all(mine)
    every = lax.all_gather(mine, "col").reshape(n_col, sub, KB, rows_dev, halves, blk)
    diag_part = every[:KB, :, :, 0, 0].transpose(1, 2, 0, 3).reshape(sub, KB * KB, blk)
    rhs_part = jnp.concatenate([mine_rhs, jnp.zeros((sub - KB, blk), jnp.float32)], axis=0)
    diag_part = jnp.concatenate([diag_part, rhs_part[:, None, :]], axis=1)
    diag_got = to_all(diag_part.reshape(-1, blk))
    to_rows = every.transpose(4, 0, 1, 2, 3, 5).reshape(n_row, sub * KB * rows_dev, blk)
    rows_got = lax.all_to_all(to_rows, "row", 0, 0).reshape(-1, blk)

    inv, col, found = factor_call(diag_got, cols_got, cols_dev, count)
    factor, solved = finish_call(
        place, pattern.reshape(-1), x, support[:, 0, :], values.reshape(-1, blk), rows_got, inv,
        col, found,
    )
    return (factor.reshape(front.shape), solved.reshape(rhs.shape))


def solution(mesh):
    placed = (
        P(None, "row", None, None, "col", None),
        P(None, "row", None),
        P(),
        P("col", None, "row", None),
    )
    return jax.shard_map(
        shards,
        mesh=mesh,
        in_specs=placed,
        out_specs=(P(None, "row", None, None, "col", None), P("col", None, "row", None)),
        check_vma=False,
    )
```

time: 259 us -> 147 us (0.57); the launches traced: 255 us -> 147 us
  other arithmetic: 100 us -> 0.54 us
  Pallas kernels: 0 us -> 24.4 us
  blocking collectives: 54.3 us -> 77.7 us
  matrix products: 21.6 us -> 0 us
  local copies, waits for them, and re-layouts: 28.3 us -> 12.4 us
  waiting for transfers between devices: 35.4 us -> 20.9 us
    another operation x13 -> x1, other arithmetic: 90.9 us -> 0.08 us  [shards(): place = jnp.stack([p, q, jnp.int32(n_row), jnp.int32(n_col)])]
    pallas_call x0 -> x2, Pallas kernels: none -> 24.4 us  [the longest x1 16.6 us: factor_call(): pl.pallas_call(factor_kernel, out_shape=(jax.ShapeDtypeStruct((size, size...]
    all_to_all x0 -> x1, blocking collectives: none -> 23.4 us  [to_all(): return lax.all_to_all(sent, 'row', 0, 0).reshape(-1, blk)]
    all_to_all x1 -> x2, waiting for transfers between devices: 35.4 us -> 20.9 us  [the longest x1 20.9 us: to_all(): return lax.all_to_all(sent, 'row', 0, 0).reshape(-1, blk)]
    another operation x13 -> x0, local copies, waits for them, and re-layouts: 11.4 us -> none
    another operation x9 -> x0, matrix products: 11.4 us -> none  [the longest x5 6.28 us: shards(): jax.scipy.linalg.solve_triangular(factor, jnp.eye(size, dtype=jnp.float32...]
    dot_general x5 -> x0, matrix products: 10.2 us -> none  [the longest x3 5.84 us: mm(): return jnp.dot(a, b, precision=precise, preferred_element_type=jnp.float32)]
    reshape x10 -> x1, local copies, waits for them, and re-layouts: 4.52 us -> 1.34 us  [shards(): every.transpose(4, 0, 1, 2, 3, 5).reshape(n_row, sub * KB * rows_dev, blk)]
  transfers between devices with their start and end apart: 1 -> 2, of which waited for: 1 -> 1; matrix products, arithmetic and copies ran while one was open for 1% -> 1% of each run, Pallas kernels for 0% -> 11%
where the time goes in v2:
time: 147 us
  blocking collectives  77.7 us (53%)
  Pallas kernels  24.4 us (17%)
  waiting for transfers between devices  20.9 us (14%)
  local copies, waits for them, and re-layouts  12.4 us (8%)
  starting transfers between devices  9.75 us (7%)
    all_gather x1, blocking collectives, shards(): lax.all_gather(mine, 'col').reshape(n_col, sub, KB, rows_dev, halves, blk)  31.7 us
    all_to_all x1, blocking collectives, to_all(): return lax.all_to_all(sent, 'row', 0, 0).reshape(-1, blk)  23.4 us
    all_to_all x1, blocking collectives, shards(): got = lax.all_to_all(sent, 'row', 0, 0)[:KB]  22.5 us
    all_to_all x1, waiting for transfers between devices, to_all(): return lax.all_to_all(sent, 'row', 0, 0).reshape(-1, blk)  20.9 us
    pallas_call x1, Pallas kernels, factor_call(): pl.pallas_call(factor_kernel, out_shape=(jax.ShapeDtypeStruct((size, size...  16.6 us
    pallas_call x1, Pallas kernels, finish_call(): pl.pallas_call(finish_kernel, grid=(rows_dev,), in_specs=[scalars, scalar...  7.76 us
    unnamed x17, local copies, waits for them, and re-layouts  6.08 us
    all_to_all x1, starting transfers between devices, shards(): rows_got = lax.all_to_all(to_rows, 'row', 0, 0).reshape(-1, blk)  5.58 us
  transfers between devices with their start and end apart: 2, of which 1 were waited for; matrix products, arithmetic and copies ran while one was open for 1% of the time, Pallas kernels for 11%

profile of v2, /device:TPU:1, one launch (start us, length us, event | category | flops | bytes accessed | tf_op | source)
XLA Modules:
  0.0 146.5 jit_solution(826294131274048965)
XLA Ops:
  0.7 0.7 slice_bitcast_fusion.2
  1.3 0.1 eq.20
  1.6 0.2 fusion.1
  1.8 0.1 slice_reduce_fusion
  2.0 0.9 slice.34
  2.8 1.1 slice.32
  3.9 0.2 select_add_fusion
  4.2 22.5 %all_to_all.20 = f32[32,33,128]{2,1,0:T(8,128)S(1)} all-to-all(f32[32,33,128]{2,1,0:T(8,128)S(1)} %pad_maximum_fusion), channel_id=1, replica_groups=mesh['row'=32,'col'=16] {'row'}, dimensions={0} | all-to-all | bytes 1081344 | tf_op jit(solution)/shard_map/all_to_all | solution.py:265
  26.8 31.7 %all_gather.3 = f32[16,96,128]{2,1,0:T(8,128)S(1)} all-gather(f32[1,96,128]{2,1,0:T(8,128)S(1)} %bitcast.58), channel_id=1, replica_groups=mesh['row'=32,'col'=16] {'col'}, dimensions={0}, use_global_device_ids=true | all-gather | bytes 835584 | tf_op jit(solution)/shard_map/all_gather | solution.py:275
  58.5 0.5 copy.46
  59.1 23.4 %all_to_all.21 = f32[32,40,128]{2,1,0:T(8,128)S(1)} all-to-all(f32[32,40,128]{2,1,0:T(8,128)S(1)} %broadcast_in_dim.37), channel_id=1, replica_groups=mesh['row'=32,'col'=16] {'row'}, dimensions={0} | all-to-all | bytes 1310720 | tf_op jit(solution)/shard_map/all_to_all | solution.py:272
  82.6 1.3 broadcast_in_dim.39
  83.9 4.2 %all-to-all-start.3 = ((f32[32,96,128]{2,1,0:T(8,128)}), f32[32,96,128]{2,1,0:T(8,128)S(1)}, u32[]{:S(2)}, u32[]{:S(2)}) async-start(f32[32,96,128]{2,1,0:T(8,128)} %broadcast_in_dim.39), calls=%async_computation.3 | async-start | bytes 3145728 | tf_op jit(solution)/shard_map/all_to_all | solution.py:272
  88.1 1.3 copy.47
  89.4 20.9 %all-to-all-done.3 = f32[32,96,128]{2,1,0:T(8,128)S(1)} async-done(((f32[32,96,128]{2,1,0:T(8,128)}), f32[32,96,128]{2,1,0:T(8,128)S(1)}, u32[]{:S(2)}, u32[]{:S(2)}) %all-to-all-start.3) | async-done | bytes 1572896 | tf_op jit(solution)/shard_map/all_to_all | solution.py:272
  110.3 5.6 %all-to-all-start.1 = ((f32[32,48,128]{2,1,0:T(8,128)}), f32[32,48,128]{2,1,0:T(8,128)S(1)}, u32[]{:S(2)}, u32[]{:S(2)}) async-start(f32[32,48,128]{2,1,0:T(8,128)} %copy.47), calls=%async_computation.1 | async-start | bytes 1572864 | tf_op jit(solution)/shard_map/all_to_all | solution.py:281
  115.9 0.1 convert_element_type.9.pattern_ref
  116.1 16.6 %factor.1 = (f32[384,384]{1,0:T(8,128)S(1)}, f32[384,1024]{1,0:T(8,128)S(1)}, f32[32,384]{1,0:T(8,128)S(1)}) custom-call(f32[1280,128]{1,0:T(8,128)S(1)} %bitcast.51, f32[3072,128]{1,0:T(8,128)S(1)} %bitcast.47), custom_call_target="tpu_custom_call" | custom-call | tf_op jit(solution)/shard_map/factor/pallas_call | solution.py:190
  132.7 1.2 copy-done.2
  133.8 0.8 copy-done.4
  134.7 1.6 %copy-done.1 = f32[4,1,128,8,1,128]{5,4,3,2,1,0:T(1,128)S(1)} copy-done((f32[4,1,128,8,1,128]{5,4,3,2,1,0:T(1,128)S(1)}, f32[4,1,128,8,1,128]{5,4,3,2,1,0:T(1,128)}, u32[]{:S(2)}) %copy-start.1) | copy-done | bytes 2097176
  136.3 1.4 copy-done.3
  137.7 1.1 copy-done.5
  138.7 7.8 %finish.1 = (f32[4096,128]{1,0:T(8,128)}, f32[128,128]{1,0:T(8,128)}) custom-call(s32[4]{0:T(128)S(1)} %pad_add_fusion.where_ref, f32[32]{0:T(128)S(1)} %convert_element_type.9.pattern_ref, f32[4096,128]{1,0:T(8,128)S(1)} %bitcast.49, f32[4,128]{1,0:T(4,128)S(1)} %bitcast.54, f32[128,128]{1,0:T(8,128)S(1)} %bitcast.53, f32[1536,128]{1,0:T(8,128)S(1)} %bitcast.50, ...), custom_call_target="tpu_custom_call" | custom-call | tf_op jit(solution)/shard_map/finish/pallas_call | solution.py:217
  (34 shorter events, 0.5 us)
Async XLA Ops:
  0.6 0.9 copy-start
  83.9 26.4 %all-to-all-start.3 = ((f32[32,96,128]{2,1,0:T(8,128)}), f32[32,96,128]{2,1,0:T(8,128)S(1)}, u32[]{:S(2)}, u32[]{:S(2)}) async-start(f32[32,96,128]{2,1,0:T(8,128)} %broadcast_in_dim.39), calls=%async_computation.3 | async-start | bytes 3145728 | tf_op jit(solution)/shard_map/all_to_all | solution.py:272
  89.4 45.3 %copy-start.6 = (f32[32,4,1,128]{3,2,1,0:T(1,128)S(1)}, f32[32,4,1,128]{3,2,1,0:T(1,128)}, u32[]{:S(2)}) copy-start(f32[32,4,1,128]{3,2,1,0:T(1,128)} %param.7) | copy-start | bytes 196612
  89.4 45.3 %copy-start.7 = (f32[4,1,128]{2,1,0:T(1,128)S(1)}, f32[4,1,128]{2,1,0:T(1,128)}, u32[]{:S(2)}) copy-start(f32[4,1,128]{2,1,0:T(1,128)} %param.5) | copy-start | bytes 6148
  110.3 24.3 %all-to-all-start.1 = ((f32[32,48,128]{2,1,0:T(8,128)}), f32[32,48,128]{2,1,0:T(8,128)S(1)}, u32[]{:S(2)}, u32[]{:S(2)}) async-start(f32[32,48,128]{2,1,0:T(8,128)} %copy.47), calls=%async_computation.1 | async-start | bytes 1572864 | tf_op jit(solution)/shard_map/all_to_all | solution.py:281
  132.7 1.2 copy-start.2
  133.8 0.8 copy-start.4
  134.7 1.6 %copy-start.1 = (f32[4,1,128,8,1,128]{5,4,3,2,1,0:T(1,128)S(1)}, f32[4,1,128,8,1,128]{5,4,3,2,1,0:T(1,128)}, u32[]{:S(2)}) copy-start(f32[4,1,128,8,1,128]{5,4,3,2,1,0:T(1,128)} %param.4) | copy-start | bytes 6291460
  136.3 1.4 copy-start.3
  137.7 1.1 copy-start.5

commit v3 on v2

--- a/solution.py
+++ b/solution.py
@@ -83,10 +83,9 @@
             aug_ref[end:, :] = aug_ref[end:, :] - term[end:, :]
 
 
-def factor_kernel(diag_ref, cols_ref, inv_ref, col_ref, found_ref, a_ref, c_ref, aug_ref):
+def factor_kernel(diag_ref, inv_ref, found_ref, a_ref, aug_ref):
     blk = aug_ref.shape[0]
     size = inv_ref.shape[0]
-    wide = col_ref.shape[1] // blk
     count = found_ref.shape[0]
     pitch = KB * KB + 1
     for k in range(KB):
@@ -111,14 +110,6 @@
             up = ndot(own, a_ref[k0:k1, k1:])
             a_ref[k1:, k1:] = a_ref[k1:, k1:] - tdot(up, up)
             inv_ref[k1:, :k1] = inv_ref[k1:, :k1] - tdot(up, inv_ref[k0:k1, :k1])
-    for k in range(KB):
-        for m in range(wide):
-            c_ref[k * blk : (k + 1) * blk, m * blk : (m + 1) * blk] = cols_ref[
-                pl.ds(k * wide + m, blk, stride=KB * wide), :
-            ]
-    for k in range(KB):
-        k0, k1 = k * blk, (k + 1) * blk
-        col_ref[k0:k1, :] = ndot(inv_ref[k0:k1, :k1], c_ref[:k1, :])
     first = jnp.concatenate(
         [
             diag_ref[pl.ds(k * pitch + pitch - 1, count, stride=diag_ref.shape[0] // count), :]
@@ -129,108 +120,131 @@
     found_ref[...] = rdot(first, inv_ref[...])
 
 
+def gather_solve(inv_ref, got_ref, wide, to_ref):
+    blk = got_ref.shape[1]
+    size = KB * blk
+    for k in range(KB):
+        for j in range(wide):
+            to_ref[k * blk : (k + 1) * blk, j * blk : (j + 1) * blk] = got_ref[
+                pl.ds(k * wide + j, blk, stride=KB * wide), :
+            ]
+    for k in reversed(range(KB)):
+        k0, k1 = k * blk, (k + 1) * blk
+        to_ref[k0:k1, :] = ndot(inv_ref[k0:k1, :k1], to_ref[:k1, :])
+
+
 def finish_kernel(
-    where_ref, pattern_ref, x_ref, support_ref, rhs_ref, rows_ref, inv_ref, col_ref, found_ref,
-    out_ref, solved_ref, t_ref, s_ref,
+    where_ref, pattern_ref, x_hbm, cols_hbm, support_ref, rhs_ref, rows_ref, inv_ref, found_ref,
+    out_hbm, solved_ref, x_ref, cols_ref, out_ref, row_ref, col_ref, in_sem, cols_sem, out_sem,
 ):
-    step = pl.program_id(0)
     p = where_ref[0]
     q = where_ref[1]
     n_row = where_ref[2]
     n_col = where_ref[3]
-    blk = support_ref.shape[1]
-    rows_dev = support_ref.shape[0]
+    rows_dev, blk = support_ref.shape
     wide = col_ref.shape[1] // blk
     count = found_ref.shape[0]
-
-    @pl.when(step == 0)
-    def _():
-        for k in range(KB):
-            for l in range(rows_dev):
-                t_ref[k * blk : (k + 1) * blk, l * blk : (l + 1) * blk] = rows_ref[
-                    pl.ds(k * rows_dev + l, blk, stride=KB * rows_dev), :
-                ]
-        for k in range(KB):
-            k0, k1 = k * blk, (k + 1) * blk
-            got = ndot(inv_ref[k0:k1, :k1], t_ref[:k1, :])
-            for l in range(rows_dev):
-                s_ref[l, k0:k1, :] = got[:, l * blk : (l + 1) * blk]
-        for l in range(rows_dev):
-            rest = rhs_ref[pl.ds(l, count, stride=rows_dev), :] - ndot(found_ref[...], s_ref[l])
-            if l == 0:
-                for k in range(KB):
-                    rest = jnp.where(p == k, found_ref[:, k * blk : (k + 1) * blk], rest)
-            solved_ref[pl.ds(l, count, stride=rows_dev), :] = rest
-
+    part = blk * wide
+    load_cols = pltpu.make_async_copy(cols_hbm, cols_ref, cols_sem)
+    load_cols.start()
+    load = pltpu.make_async_copy(x_hbm, x_ref, in_sem)
+    load.start()
+    gather_solve(inv_ref, rows_ref, rows_dev, row_ref)
+    rest = ndot(found_ref[...], row_ref[...])
+    for l in range(rows_dev):
+        got = rhs_ref[pl.ds(l, count, stride=rows_dev), :] - rest[:, l * blk : (l + 1) * blk]
+        if l == 0:
+            for k in range(KB):
+                got = jnp.where(p == k, found_ref[:, k * blk : (k + 1) * blk], got)
+        solved_ref[pl.ds(l, count, stride=rows_dev), :] = got
+
+    load_cols.wait()
+    gather_solve(inv_ref, cols_ref, wide, col_ref)
     ri = lax.broadcasted_iota(jnp.int32, (blk, blk), 0)
     ci = lax.broadcasted_iota(jnp.int32, (blk, blk), 1)
-    mine = s_ref[step]
-    term = tdot(mine, col_ref[...])
-    row_id = step * n_row + p
-    diag = jnp.where(ri == ci, jnp.broadcast_to(support_ref[pl.ds(step, 1), :], (blk, blk)), 0.0)
-    for m in range(wide):
-        col_id = m * n_col + q
-        got = x_ref[pl.ds(m, blk, stride=wide), :] * pattern_ref[step * wide + m]
-        got = got - term[:, m * blk : (m + 1) * blk]
-        got = got + jnp.where(row_id == col_id, diag, 0.0)
-        if m == 0:
-            piece = mine[:blk, :]
-            for k in range(1, KB):
-                piece = jnp.where(q == k, mine[k * blk : (k + 1) * blk, :], piece)
-            piece = piece.T
-            piece = jnp.where((row_id == col_id) & (ri < ci), 0.0, piece)
-            got = jnp.where(q < KB, piece, got)
-        got = jnp.where((row_id < KB) & (col_id > row_id), 0.0, got)
-        out_ref[pl.ds(m, blk, stride=wide), :] = got
-
-
-def factor_call(diag, cols, wide, count):
+    load.wait()
+    stores = []
+    pair = 2
+    for g in range(rows_dev // pair):
+        term = tdot(row_ref[:, g * pair * blk : (g + 1) * pair * blk], col_ref[...])
+        for h in range(pair):
+            l = g * pair + h
+            mine = row_ref[:, l * blk : (l + 1) * blk]
+            row_id = l * n_row + p
+            diag = jnp.where(
+                ri == ci, jnp.broadcast_to(support_ref[l : l + 1, :], (blk, blk)), 0.0
+            )
+            for m in range(wide):
+                col_id = m * n_col + q
+                got = x_ref[pl.ds(l * part + m, blk, stride=wide), :]
+                got = got * pattern_ref[l * wide + m]
+                got = got - term[h * blk : (h + 1) * blk, m * blk : (m + 1) * blk]
+                got = got + jnp.where(row_id == col_id, diag, 0.0)
+                if m == 0:
+                    piece = mine[:blk, :]
+                    for k in range(1, KB):
+                        piece = jnp.where(q == k, mine[k * blk : (k + 1) * blk, :], piece)
+                    piece = piece.T
+                    if l == 0:
+                        piece = jnp.where((row_id == col_id) & (ri < ci), 0.0, piece)
+                    got = jnp.where(q < KB, piece, got)
+                if l == 0:
+                    got = jnp.where((row_id < KB) & (col_id > row_id), 0.0, got)
+                out_ref[pl.ds(l * part + m, blk, stride=wide), :] = got
+        span = pl.ds(g * pair * part, pair * part)
+        store = pltpu.make_async_copy(out_ref.at[span, :], out_hbm.at[span, :], out_sem.at[g])
+        store.start()
+        stores.append(store)
+    for store in stores:
+        store.wait()
+
+
+def factor_call(diag, count):
     blk = diag.shape[1]
     size = KB * blk
     return pl.pallas_call(
         factor_kernel,
         out_shape=(
             jax.ShapeDtypeStruct((size, size), jnp.float32),
-            jax.ShapeDtypeStruct((size, wide * blk), jnp.float32),
             jax.ShapeDtypeStruct((count, size), jnp.float32),
         ),
         scratch_shapes=[
             pltpu.VMEM((size, size), jnp.float32),
-            pltpu.VMEM((size, wide * blk), jnp.float32),
             pltpu.VMEM((blk, 2 * blk), jnp.float32),
         ],
-        compiler_params=pltpu.CompilerParams(vmem_limit_bytes=40 << 20),
+        compiler_params=pltpu.CompilerParams(vmem_limit_bytes=8 << 20),
         name="factor",
-    )(diag, cols)
-
-
-def finish_call(place, pattern, x, support, rhs, rows, inv, col, found):
+    )(diag)
+
+
+def finish_call(place, pattern, x, support, rhs, rows, cols, inv, found):
     rows_dev, blk = support.shape
     size = inv.shape[0]
-    part = x.shape[0] // rows_dev
-
-    def whole(a):
-        return pl.BlockSpec(a.shape, lambda i: (0, 0))
-
+    wide = x.shape[0] // (rows_dev * blk)
     scalars = pl.BlockSpec(memory_space=pltpu.SMEM)
-    tile = pl.BlockSpec((part, blk), lambda i: (i, 0))
+    far = pl.BlockSpec(memory_space=pltpu.HBM)
+    near = pl.BlockSpec(memory_space=pltpu.VMEM)
     return pl.pallas_call(
         finish_kernel,
-        grid=(rows_dev,),
-        in_specs=[scalars, scalars, tile, whole(support), whole(rhs), whole(rows), whole(inv),
-                  whole(col), whole(found)],
-        out_specs=(tile, whole(rhs)),
+        in_specs=[scalars, scalars, far, far] + [near] * 5,
+        out_specs=(far, near),
         out_shape=(
             jax.ShapeDtypeStruct(x.shape, jnp.float32),
             jax.ShapeDtypeStruct(rhs.shape, jnp.float32),
         ),
         scratch_shapes=[
+            pltpu.VMEM(x.shape, jnp.float32),
+            pltpu.VMEM(cols.shape, jnp.float32),
+            pltpu.VMEM(x.shape, jnp.float32),
             pltpu.VMEM((size, rows_dev * blk), jnp.float32),
-            pltpu.VMEM((rows_dev, size, blk), jnp.float32),
+            pltpu.VMEM((size, wide * blk), jnp.float32),
+            pltpu.SemaphoreType.DMA,
+            pltpu.SemaphoreType.DMA,
+            pltpu.SemaphoreType.DMA((rows_dev // 2,)),
         ],
-        compiler_params=pltpu.CompilerParams(vmem_limit_bytes=40 << 20),
+        compiler_params=pltpu.CompilerParams(vmem_limit_bytes=24 << 20),
         name="finish",
-    )(place, pattern, x, support, rhs, rows, inv, col, found)
+    )(place, pattern, x, cols, support, rhs, rows, inv, found)
 
 
 def shards(front, support, mask, rhs):
@@ -271,7 +285,7 @@
         sent = jnp.broadcast_to(part[None], (n_row,) + part.shape)
         return lax.all_to_all(sent, "row", 0, 0).reshape(-1, blk)
 
-    cols_got = to_all(mine)
+    cols_got = lax.all_gather(mine, "row").reshape(-1, blk)
     every = lax.all_gather(mine, "col").reshape(n_col, sub, KB, rows_dev, halves, blk)
     diag_part = every[:KB, :, :, 0, 0].transpose(1, 2, 0, 3).reshape(sub, KB * KB, blk)
     rhs_part = jnp.concatenate([mine_rhs, jnp.zeros((sub - KB, blk), jnp.float32)], axis=0)
@@ -280,10 +294,10 @@
     to_rows = every.transpose(4, 0, 1, 2, 3, 5).reshape(n_row, sub * KB * rows_dev, blk)
     rows_got = lax.all_to_all(to_rows, "row", 0, 0).reshape(-1, blk)
 
-    inv, col, found = factor_call(diag_got, cols_got, cols_dev, count)
+    inv, found = factor_call(diag_got, count)
     factor, solved = finish_call(
-        place, pattern.reshape(-1), x, support[:, 0, :], values.reshape(-1, blk), rows_got, inv,
-        col, found,
+        place, pattern.reshape(-1), x, support[:, 0, :], values.reshape(-1, blk), rows_got,
+        cols_got, inv, found,
     )
     return (factor.reshape(front.shape), solved.reshape(rhs.shape))
 

time: 147 us -> 137 us (0.932)
  blocking collectives: 77.7 us -> 54.9 us
  between operations: 0.81 us -> 14.2 us
  waiting for transfers between devices: 20.9 us -> 12.4 us
  starting transfers between devices: 9.75 us -> 14.6 us
  local copies, waits for them, and re-layouts: 12.4 us -> 14.3 us
    all_to_all x1 -> x0, blocking collectives: 23.4 us -> none  [to_all(): return lax.all_to_all(sent, 'row', 0, 0).reshape(-1, blk)]
    all_to_all x1, waiting for transfers between devices: 20.9 us -> 12.4 us  [to_all(): return lax.all_to_all(sent, 'row', 0, 0).reshape(-1, blk)]
    all_to_all x1, starting transfers between devices: 4.17 us -> 10.6 us  [to_all(): return lax.all_to_all(sent, 'row', 0, 0).reshape(-1, blk)]
    pallas_call x1, Pallas kernels: 7.76 us -> 10.3 us  [finish_call(): pl.pallas_call(finish_kernel, in_specs=[scalars, scalars, far, far] + [ne...]
    all_to_all x1, starting transfers between devices: 5.58 us -> 3.96 us  [shards(): rows_got = lax.all_to_all(to_rows, 'row', 0, 0).reshape(-1, blk)]
    pallas_call x1, Pallas kernels: 16.6 us -> 15 us  [factor_call(): pl.pallas_call(factor_kernel, out_shape=(jax.ShapeDtypeStruct((size, size...]
    unnamed x17 -> x21, local copies, waits for them, and re-layouts: 6.08 us -> 6.5 us
  transfers between devices with their start and end apart: 2 -> 3, of which waited for: 1 -> 1; matrix products, arithmetic and copies ran while one was open for 1% -> 3% of each run, Pallas kernels for 11% -> 11%
where the time goes in v3:
time: 137 us; the launch traced here: 136 us
  blocking collectives  54.9 us (40%)
  Pallas kernels  25.2 us (18%)
  starting transfers between devices  14.6 us (11%)
  local copies, waits for them, and re-layouts  14.3 us (10%)
  between operations  14.2 us (10%)
  waiting for transfers between devices  12.4 us (9%)
    all_gather x1, blocking collectives, shards(): lax.all_gather(mine, 'col').reshape(n_col, sub, KB, rows_dev, halves, blk)  32.3 us
    all_to_all x1, blocking collectives, shards(): got = lax.all_to_all(sent, 'row', 0, 0)[:KB]  22.5 us
    pallas_call x1, Pallas kernels, factor_call(): pl.pallas_call(factor_kernel, out_shape=(jax.ShapeDtypeStruct((size, size...  15 us
    all_to_all x1, waiting for transfers between devices, to_all(): return lax.all_to_all(sent, 'row', 0, 0).reshape(-1, blk)  12.4 us
    all_to_all x1, starting transfers between devices, to_all(): return lax.all_to_all(sent, 'row', 0, 0).reshape(-1, blk)  10.6 us
    pallas_call x1, Pallas kernels, finish_call(): pl.pallas_call(finish_kernel, in_specs=[scalars, scalars, far, far] + [ne...  10.3 us
    unnamed x21, local copies, waits for them, and re-layouts  6.5 us
    all_to_all x1, starting transfers between devices, shards(): rows_got = lax.all_to_all(to_rows, 'row', 0, 0).reshape(-1, blk)  3.96 us
  transfers between devices with their start and end apart: 3, of which 1 were waited for; matrix products, arithmetic and copies ran while one was open for 3% of the time, Pallas kernels for 11%

profile of v3, /device:TPU:1, one launch (start us, length us, event | category | flops | bytes accessed | tf_op | source)
XLA Modules:
  0.0 136.2 jit_solution(8929652472972770903)
XLA Ops:
  7.3 0.7 slice_bitcast_fusion.2
  8.2 0.2 fusion.1
  8.3 0.1 slice_reduce_fusion
  8.6 0.9 slice.34
  9.4 1.1 slice.32
  10.5 0.2 select_add_fusion
  10.8 22.5 %all_to_all.15 = f32[32,33,128]{2,1,0:T(8,128)S(1)} all-to-all(f32[32,33,128]{2,1,0:T(8,128)S(1)} %pad_maximum_fusion), channel_id=1, replica_groups=mesh['row'=32,'col'=16] {'row'}, dimensions={0} | all-to-all | bytes 1081344 | tf_op jit(solution)/shard_map/all_to_all | solution.py:279
  33.3 0.6 copy.32
  34.0 32.3 %all_gather.7 = f32[16,96,128]{2,1,0:T(8,128)S(1)} all-gather(f32[1,96,128]{2,1,0:T(8,128)} %bitcast.58), channel_id=1, replica_groups=mesh['row'=32,'col'=16] {'col'}, dimensions={0}, use_global_device_ids=true | all-gather | bytes 835584 | tf_op jit(solution)/shard_map/all_gather | solution.py:289
  66.4 0.5 copy.33
  66.8 0.9 copy-done.9
  67.8 0.9 broadcast_in_dim.30
  68.7 10.6 %all-to-all-start.2 = ((f32[32,40,128]{2,1,0:T(8,128)}), f32[32,40,128]{2,1,0:T(8,128)S(1)}, u32[]{:S(2)}, u32[]{:S(2)}) async-start(f32[32,40,128]{2,1,0:T(8,128)} %broadcast_in_dim.30), calls=%async_computation.2 | async-start | bytes 1310720 | tf_op jit(solution)/shard_map/all_to_all | solution.py:286
  79.3 2.6 %copy.34 = f32[32,48,128]{2,1,0:T(8,128)} copy(f32[32,48,128]{2,0,1:T(8,128)} %bitcast.55) | data formatting | bytes 1572864 | tf_op jit(solution)/shard_map/reshape | solution.py:294
  81.9 12.4 %all-to-all-done.2 = f32[32,40,128]{2,1,0:T(8,128)S(1)} async-done(((f32[32,40,128]{2,1,0:T(8,128)}), f32[32,40,128]{2,1,0:T(8,128)S(1)}, u32[]{:S(2)}, u32[]{:S(2)}) %all-to-all-start.2) | async-done | bytes 655392 | tf_op jit(solution)/shard_map/all_to_all | solution.py:286
  94.3 0.8 copy-done.2
  95.1 4.0 %all-to-all-start.1 = ((f32[32,48,128]{2,1,0:T(8,128)}), f32[32,48,128]{2,1,0:T(8,128)S(1)}, u32[]{:S(2)}, u32[]{:S(2)}) async-start(f32[32,48,128]{2,1,0:T(8,128)} %copy.34), calls=%async_computation.1 | async-start | bytes 1572864 | tf_op jit(solution)/shard_map/all_to_all | solution.py:295
  99.3 1.1 copy-done.3
  100.3 15.0 %factor.1 = (f32[384,384]{1,0:T(8,128)S(1)}, f32[32,384]{1,0:T(8,128)S(1)}) custom-call(f32[1280,128]{1,0:T(8,128)S(1)} %bitcast.49), custom_call_target="tpu_custom_call" | custom-call | tf_op jit(solution)/shard_map/factor/pallas_call | solution.py:205
  115.3 0.6 copy-done.6
  116.0 1.4 %copy-done.4 = f32[32,96,128]{2,1,0:T(8,128)S(1)} copy-done((f32[32,96,128]{2,1,0:T(8,128)S(1)}, f32[32,96,128]{2,1,0:T(8,128)}, u32[]{:S(2)}) %copy-start.4) | copy-done | bytes 1572888
  117.4 0.8 copy-done.5
  118.2 0.8 copy-done.7
  119.0 10.3 %finish.1 = (f32[4096,128]{1,0:T(8,128)}, f32[128,128]{1,0:T(8,128)}) custom-call(s32[4]{0:T(128)S(1)} %pad_add_fusion.where_ref, f32[32]{0:T(128)S(1)} %convert_element_type.9.pattern_ref, f32[4096,128]{1,0:T(8,128)S(1)} %bitcast.47, f32[3072,128]{1,0:T(8,128)S(1)} %bitcast.50, f32[4,128]{1,0:T(4,128)S(1)} %bitcast.53, f32[128,128]{1,0:T(8,128)S(1)} %bitcast.52, ...), custom_call_target="tpu_custom_call" | custom-call | tf_op jit(solution)/shard_map/finish/pallas_call | solution.py:227
  (39 shorter events, 0.7 us)
Async XLA Ops:
  7.2 0.9 copy-start
  7.2 108.8 %all-gather.2.cloned.1.call-start = ((), (), s32[]{:S(2)}) async-start(), calls=%async_computation.3 | async-start | bytes 1622016 | tf_op jit(solution)/shard_map/all_gather | solution.py:288
  66.8 0.9 copy-start.9
  68.7 25.6 %all-to-all-start.2 = ((f32[32,40,128]{2,1,0:T(8,128)}), f32[32,40,128]{2,1,0:T(8,128)S(1)}, u32[]{:S(2)}, u32[]{:S(2)}) async-start(f32[32,40,128]{2,1,0:T(8,128)} %broadcast_in_dim.30), calls=%async_computation.2 | async-start | bytes 1310720 | tf_op jit(solution)/shard_map/all_to_all | solution.py:286
  79.3 36.7 %copy-start.1 = (f32[4,1,128,8,1,128]{5,4,3,2,1,0:T(1,128)S(1)}, f32[4,1,128,8,1,128]{5,4,3,2,1,0:T(1,128)}, u32[]{:S(2)}) copy-start(f32[4,1,128,8,1,128]{5,4,3,2,1,0:T(1,128)} %param.4) | copy-start | bytes 6291460
  79.3 36.7 %copy-start.8 = (f32[4,1,128]{2,1,0:T(1,128)S(1)}, f32[4,1,128]{2,1,0:T(1,128)}, u32[]{:S(2)}) copy-start(f32[4,1,128]{2,1,0:T(1,128)} %param.5) | copy-start | bytes 6148
  94.3 0.8 copy-start.2
  95.1 20.8 %all-to-all-start.1 = ((f32[32,48,128]{2,1,0:T(8,128)}), f32[32,48,128]{2,1,0:T(8,128)S(1)}, u32[]{:S(2)}, u32[]{:S(2)}) async-start(f32[32,48,128]{2,1,0:T(8,128)} %copy.34), calls=%async_computation.1 | async-start | bytes 1572864 | tf_op jit(solution)/shard_map/all_to_all | solution.py:295
  99.3 1.1 copy-start.3
  115.3 0.6 copy-start.6
  116.0 1.4 %copy-start.4 = (f32[32,96,128]{2,1,0:T(8,128)S(1)}, f32[32,96,128]{2,1,0:T(8,128)}, u32[]{:S(2)}) copy-start(f32[32,96,128]{2,1,0:T(8,128)} %all-gather.2.cloned.1.call-done) | copy-start | bytes 4718596
  117.4 0.8 copy-start.5
  118.2 0.8 copy-start.7
Sparse Core Ops, SparseCore 0:
  34.1 62.4 all-gather.1

commit v4 on v3

--- a/solution.py
+++ b/solution.py
@@ -83,7 +83,7 @@
             aug_ref[end:, :] = aug_ref[end:, :] - term[end:, :]
 
 
-def factor_kernel(diag_ref, inv_ref, found_ref, a_ref, aug_ref):
+def factor_kernel(diag_ref, inv_hbm, found_ref, inv_ref, a_ref, aug_ref, sem):
     blk = aug_ref.shape[0]
     size = inv_ref.shape[0]
     count = found_ref.shape[0]
@@ -97,6 +97,7 @@
     eye = lax.broadcasted_iota(jnp.int32, (blk, blk), 0) == lax.broadcasted_iota(
         jnp.int32, (blk, blk), 1
     )
+    stores = []
     for k in range(KB):
         k0, k1 = k * blk, (k + 1) * blk
         aug_ref[:, :blk] = a_ref[k0:k1, k0:k1]
@@ -106,6 +107,9 @@
         if k > 0:
             inv_ref[k0:k1, :k0] = ndot(own, inv_ref[k0:k1, :k0])
         inv_ref[k0:k1, k0:k1] = own
+        store = pltpu.make_async_copy(inv_ref.at[k0:k1, :], inv_hbm.at[k0:k1, :], sem.at[k])
+        store.start()
+        stores.append(store)
         if k1 < size:
             up = ndot(own, a_ref[k0:k1, k1:])
             a_ref[k1:, k1:] = a_ref[k1:, k1:] - tdot(up, up)
@@ -118,24 +122,29 @@
         axis=1,
     )
     found_ref[...] = rdot(first, inv_ref[...])
-
-
-def gather_solve(inv_ref, got_ref, wide, to_ref):
+    for store in stores:
+        store.wait()
+
+
+def gather(got_ref, wide, to_ref):
     blk = got_ref.shape[1]
-    size = KB * blk
     for k in range(KB):
         for j in range(wide):
             to_ref[k * blk : (k + 1) * blk, j * blk : (j + 1) * blk] = got_ref[
                 pl.ds(k * wide + j, blk, stride=KB * wide), :
             ]
+
+
+def solve(inv_ref, to_ref, blk):
     for k in reversed(range(KB)):
         k0, k1 = k * blk, (k + 1) * blk
         to_ref[k0:k1, :] = ndot(inv_ref[k0:k1, :k1], to_ref[:k1, :])
 
 
 def finish_kernel(
-    where_ref, pattern_ref, x_hbm, cols_hbm, support_ref, rhs_ref, rows_ref, inv_ref, found_ref,
-    out_hbm, solved_ref, x_ref, cols_ref, out_ref, row_ref, col_ref, in_sem, cols_sem, out_sem,
+    where_ref, pattern_ref, x_hbm, cols_hbm, inv_hbm, rhs_hbm, support_ref, rows_ref, found_ref,
+    out_hbm, solved_ref, x_ref, cols_ref, inv_ref, rhs_ref, out_ref, row_ref, col_ref, sems,
+    out_sem,
 ):
     p = where_ref[0]
     q = where_ref[1]
@@ -145,11 +154,18 @@
     wide = col_ref.shape[1] // blk
     count = found_ref.shape[0]
     part = blk * wide
-    load_cols = pltpu.make_async_copy(cols_hbm, cols_ref, cols_sem)
-    load_cols.start()
-    load = pltpu.make_async_copy(x_hbm, x_ref, in_sem)
-    load.start()
-    gather_solve(inv_ref, rows_ref, rows_dev, row_ref)
+    loads = [
+        pltpu.make_async_copy(src, dst, sems.at[i])
+        for i, (src, dst) in enumerate(
+            ((inv_hbm, inv_ref), (cols_hbm, cols_ref), (x_hbm, x_ref), (rhs_hbm, rhs_ref))
+        )
+    ]
+    for load in loads:
+        load.start()
+    gather(rows_ref, rows_dev, row_ref)
+    loads[0].wait()
+    solve(inv_ref, row_ref, blk)
+    loads[3].wait()
     rest = ndot(found_ref[...], row_ref[...])
     for l in range(rows_dev):
         got = rhs_ref[pl.ds(l, count, stride=rows_dev), :] - rest[:, l * blk : (l + 1) * blk]
@@ -158,11 +174,12 @@
                 got = jnp.where(p == k, found_ref[:, k * blk : (k + 1) * blk], got)
         solved_ref[pl.ds(l, count, stride=rows_dev), :] = got
 
-    load_cols.wait()
-    gather_solve(inv_ref, cols_ref, wide, col_ref)
+    loads[1].wait()
+    gather(cols_ref, wide, col_ref)
+    solve(inv_ref, col_ref, blk)
     ri = lax.broadcasted_iota(jnp.int32, (blk, blk), 0)
     ci = lax.broadcasted_iota(jnp.int32, (blk, blk), 1)
-    load.wait()
+    loads[2].wait()
     stores = []
     pair = 2
     for g in range(rows_dev // pair):
@@ -208,11 +225,14 @@
             jax.ShapeDtypeStruct((size, size), jnp.float32),
             jax.ShapeDtypeStruct((count, size), jnp.float32),
         ),
+        out_specs=(pl.BlockSpec(memory_space=pltpu.HBM), pl.BlockSpec(memory_space=pltpu.VMEM)),
         scratch_shapes=[
             pltpu.VMEM((size, size), jnp.float32),
+            pltpu.VMEM((size, size), jnp.float32),
             pltpu.VMEM((blk, 2 * blk), jnp.float32),
+            pltpu.SemaphoreType.DMA((KB,)),
         ],
-        compiler_params=pltpu.CompilerParams(vmem_limit_bytes=8 << 20),
+        compiler_params=pltpu.CompilerParams(vmem_limit_bytes=4 << 20),
         name="factor",
     )(diag)
 
@@ -226,7 +246,7 @@
     near = pl.BlockSpec(memory_space=pltpu.VMEM)
     return pl.pallas_call(
         finish_kernel,
-        in_specs=[scalars, scalars, far, far] + [near] * 5,
+        in_specs=[scalars, scalars, far, far, far, far] + [near] * 3,
         out_specs=(far, near),
         out_shape=(
             jax.ShapeDtypeStruct(x.shape, jnp.float32),
@@ -235,16 +255,80 @@
         scratch_shapes=[
             pltpu.VMEM(x.shape, jnp.float32),
             pltpu.VMEM(cols.shape, jnp.float32),
+            pltpu.VMEM(inv.shape, jnp.float32),
+            pltpu.VMEM(rhs.shape, jnp.float32),
             pltpu.VMEM(x.shape, jnp.float32),
             pltpu.VMEM((size, rows_dev * blk), jnp.float32),
             pltpu.VMEM((size, wide * blk), jnp.float32),
-            pltpu.SemaphoreType.DMA,
-            pltpu.SemaphoreType.DMA,
+            pltpu.SemaphoreType.DMA((4,)),
             pltpu.SemaphoreType.DMA((rows_dev // 2,)),
         ],
-        compiler_params=pltpu.CompilerParams(vmem_limit_bytes=24 << 20),
+        compiler_params=pltpu.CompilerParams(vmem_limit_bytes=14 << 20),
         name="finish",
-    )(place, pattern, x, cols, support, rhs, rows, inv, found)
+    )(
+        place,
+        pattern,
+        x,
+        cols,
+        pltpu.with_memory_space_constraint(inv, pltpu.HBM),
+        rhs,
+        support,
+        rows,
+        found,
+    )
+
+
+def start_kernel(where_ref, x_hbm, rhs_hbm, mask_ref, support_ref, out_ref, x_ref, rhs_ref, sems):
+    p = where_ref[0]
+    q = where_ref[1]
+    n_col = where_ref[3]
+    blk = support_ref.shape[1]
+    n_row, pitch = out_ref.shape[0], out_ref.shape[1]
+    wide = x_ref.shape[0] // blk
+    sub = blk // n_row
+    loads = [
+        pltpu.make_async_copy(x_hbm.at[pl.ds(0, blk * wide), :], x_ref, sems.at[0]),
+        pltpu.make_async_copy(rhs_hbm, rhs_ref, sems.at[1]),
+    ]
+    for load in loads:
+        load.start()
+    lane = lax.broadcasted_iota(jnp.int32, (wide, blk), 1)
+    col_id = lax.broadcasted_iota(jnp.int32, (wide, blk), 0) * n_col + q
+    own = jnp.broadcast_to(mask_ref[pl.ds(p, 1), :], (wide, blk)).astype(jnp.float32)
+    keep = jnp.sum(jnp.where(lane == col_id, own, 0.0), axis=1, keepdims=True)
+    keep = jnp.broadcast_to(keep, (wide, blk))
+    added = jnp.where(col_id == p, jnp.broadcast_to(support_ref[0:1, :], (wide, blk)), 0.0)
+    loads[1].wait()
+    step = rhs_ref.shape[0] // n_row
+    first = rhs_ref[pl.ds(0, n_row, stride=step), :]
+    zero = jnp.zeros((pitch - sub * wide - 1, blk), jnp.float32)
+    loads[0].wait()
+    for r in range(n_row):
+        for s in range(sub):
+            a = r * sub + s
+            got = x_ref[a * wide : (a + 1) * wide, :] * keep + jnp.where(lane == a, added, 0.0)
+            out_ref[r, s * wide : (s + 1) * wide, :] = got
+        out_ref[r, sub * wide :, :] = jnp.concatenate([first[r : r + 1, :], zero], axis=0)
+
+
+def start_call(place, x, rhs, mask, support, n_row, wide):
+    blk = support.shape[1]
+    far = pl.BlockSpec(memory_space=pltpu.HBM)
+    near = pl.BlockSpec(memory_space=pltpu.VMEM)
+    pitch = blk // n_row * wide + 8
+    return pl.pallas_call(
+        start_kernel,
+        in_specs=[pl.BlockSpec(memory_space=pltpu.SMEM), far, far, near, near],
+        out_specs=near,
+        out_shape=jax.ShapeDtypeStruct((n_row, pitch, blk), jnp.float32),
+        scratch_shapes=[
+            pltpu.VMEM((blk * wide, blk), jnp.float32),
+            pltpu.VMEM(rhs.shape, jnp.float32),
+            pltpu.SemaphoreType.DMA((2,)),
+        ],
+        compiler_params=pltpu.CompilerParams(vmem_limit_bytes=4 << 20),
+        name="start",
+    )(place, x, rhs, mask, support)
 
 
 def shards(front, support, mask, rhs):
@@ -263,40 +347,34 @@
         mask_rows.reshape(rows_dev, cols_dev, n_col), q, 2, keepdims=False
     ).astype(jnp.float32)
     place = jnp.stack([p, q, jnp.int32(n_row), jnp.int32(n_col)])
-    x = front.reshape(rows_dev * blk * cols_dev, blk)
-    values = rhs.reshape(count, rows_dev, blk)
-
-    top = front[0, 0, :, :, 0, :] * pattern[0][None, :, None]
-    shape = top.shape
-    a_id = lax.broadcasted_iota(jnp.int32, shape, 0)
-    m_id = lax.broadcasted_iota(jnp.int32, shape, 1)
-    b_id = lax.broadcasted_iota(jnp.int32, shape, 2)
-    at_diag = (a_id == b_id) & (m_id * n_col + q == p)
-    top = top + jnp.where(at_diag, support[0, 0][None, None, :], 0.0)
-    sent = jnp.concatenate(
-        [top.reshape(n_row, sub * cols_dev, blk), values[:, 0, :].reshape(n_row, -1, blk)], axis=1
-    )
+    x = pltpu.with_memory_space_constraint(
+        front.reshape(rows_dev * blk * cols_dev, blk), pltpu.HBM
+    )
+    values = pltpu.with_memory_space_constraint(rhs.reshape(count * rows_dev, blk), pltpu.HBM)
+
+    sent = start_call(place, x, values, mask, support[:, 0, :], n_row, cols_dev)
     got = lax.all_to_all(sent, "row", 0, 0)[:KB]
     mine = got[:, : sub * cols_dev].reshape(KB, sub, cols_dev, blk).transpose(1, 0, 2, 3)
     mine = mine.reshape(sub * KB * cols_dev, blk)
-    mine_rhs = got[:, sub * cols_dev :].reshape(KB, blk)
+    mine_rhs = got[:, sub * cols_dev]
 
     def to_all(part):
         sent = jnp.broadcast_to(part[None], (n_row,) + part.shape)
         return lax.all_to_all(sent, "row", 0, 0).reshape(-1, blk)
 
-    cols_got = lax.all_gather(mine, "row").reshape(-1, blk)
+    cols_got = to_all(mine)
     every = lax.all_gather(mine, "col").reshape(n_col, sub, KB, rows_dev, halves, blk)
     diag_part = every[:KB, :, :, 0, 0].transpose(1, 2, 0, 3).reshape(sub, KB * KB, blk)
     rhs_part = jnp.concatenate([mine_rhs, jnp.zeros((sub - KB, blk), jnp.float32)], axis=0)
     diag_part = jnp.concatenate([diag_part, rhs_part[:, None, :]], axis=1)
+    diag_part, cols_got = lax.optimization_barrier((diag_part, cols_got))
     diag_got = to_all(diag_part.reshape(-1, blk))
     to_rows = every.transpose(4, 0, 1, 2, 3, 5).reshape(n_row, sub * KB * rows_dev, blk)
     rows_got = lax.all_to_all(to_rows, "row", 0, 0).reshape(-1, blk)
 
     inv, found = factor_call(diag_got, count)
     factor, solved = finish_call(
-        place, pattern.reshape(-1), x, support[:, 0, :], values.reshape(-1, blk), rows_got,
+        place, pattern.reshape(-1), x, support[:, 0, :], values, rows_got,
         cols_got, inv, found,
     )
     return (factor.reshape(front.shape), solved.reshape(rhs.shape))

time: 137 us -> 127 us (0.927)
  between operations: 14.2 us -> 0.95 us
  starting transfers between devices: 14.6 us -> 21.8 us
  local copies, waits for them, and re-layouts: 14.3 us -> 7.28 us
  Pallas kernels: 25.2 us -> 28.8 us
    all_to_all x1 -> x2, starting transfers between devices: 10.6 us -> 17.7 us  [to_all(): return lax.all_to_all(sent, 'row', 0, 0).reshape(-1, blk)]
    unnamed x21 -> x9, local copies, waits for them, and re-layouts: 6.5 us -> 2.34 us
    pallas_call x1 -> x2, Pallas kernels: 10.3 us -> 12.6 us  [the longest x1 10.9 us: finish_call(): pl.pallas_call(finish_kernel, in_specs=[scalars, scalars, far, far, far,...]
    slice x4 -> x1, local copies, waits for them, and re-layouts: 2.06 us -> 0.01 us  [shards(): mine_rhs = got[:, sub * cols_dev]]
    all_to_all x1 -> x2, waiting for transfers between devices: 12.4 us -> 11.6 us  [to_all(): return lax.all_to_all(sent, 'row', 0, 0).reshape(-1, blk)]
  transfers between devices with their start and end apart: 3 -> 3, of which waited for: 1 -> 1; matrix products, arithmetic and copies ran while one was open for 3% -> 2% of each run, Pallas kernels for 11% -> 13%
where the time goes in v4:
time: 127 us; the launch traced here: 126 us
  blocking collectives  55.3 us (44%)
  Pallas kernels  28.8 us (23%)
  starting transfers between devices  21.8 us (17%)
  waiting for transfers between devices  11.6 us (9%)
  local copies, waits for them, and re-layouts  7.28 us (6%)
    all_gather x1, blocking collectives, shards(): lax.all_gather(mine, 'col').reshape(n_col, sub, KB, rows_dev, halves, blk)  32.8 us
    all_to_all x1, blocking collectives, shards(): got = lax.all_to_all(sent, 'row', 0, 0)[:KB]  22.5 us
    all_to_all x2, starting transfers between devices, to_all(): return lax.all_to_all(sent, 'row', 0, 0).reshape(-1, blk)  17.7 us
    pallas_call x1, Pallas kernels, factor_call(): pl.pallas_call(factor_kernel, out_shape=(jax.ShapeDtypeStruct((size, size...  16.3 us
    all_to_all x2, waiting for transfers between devices, to_all(): return lax.all_to_all(sent, 'row', 0, 0).reshape(-1, blk)  11.6 us
    pallas_call x1, Pallas kernels, finish_call(): pl.pallas_call(finish_kernel, in_specs=[scalars, scalars, far, far, far,...  10.9 us
    all_to_all x1, starting transfers between devices, shards(): rows_got = lax.all_to_all(to_rows, 'row', 0, 0).reshape(-1, blk)  4.12 us
  transfers between devices with their start and end apart: 3, of which 1 were waited for; matrix products, arithmetic and copies ran while one was open for 2% of the time, Pallas kernels for 13%

profile of v4, /device:TPU:1, one launch (start us, length us, event | category | flops | bytes accessed | tf_op | source)
XLA Modules:
  0.0 126.0 jit_solution(18380267440468663343)
XLA Ops:
  0.6 0.1 pad_add_fusion.where_ref
  0.7 0.8 copy-done.1
  1.6 0.7 copy-done.2
  2.2 1.7 %start.1 = f32[32,40,128]{2,1,0:T(8,128)S(1)} custom-call(s32[4]{0:T(128)S(1)} %pad_add_fusion.where_ref, f32[4096,128]{1,0:T(8,128)} %bitcast.46, f32[128,128]{1,0:T(8,128)} %bitcast.52, s32[128,128]{1,0:T(8,128)S(1)} %copy-done.1, f32[4,128]{1,0:T(4,128)S(1)} %bitcast.44), custom_call_target="tpu_custom_call" | custom-call | tf_op jit(solution)/shard_map/start/pallas_call | solution.py:319
  3.9 22.5 %all_to_all.20 = f32[32,40,128]{2,1,0:T(8,128)S(1)} all-to-all(f32[32,40,128]{2,1,0:T(8,128)S(1)} %start.1), channel_id=1, replica_groups=mesh['row'=32,'col'=16] {'row'}, dimensions={0} | all-to-all | bytes 1310720 | tf_op jit(solution)/shard_map/all_to_all | solution.py:356
  26.5 1.3 %broadcast_in_dim.20 = f32[32,96,128]{2,1,0:T(8,128)} broadcast(f32[96,128]{1,0:T(8,128)S(1)} %bitcast.50), dimensions={1,2} | broadcast | bytes 1622016 | tf_op jit(solution)/shard_map/broadcast_in_dim | solution.py:362
  27.8 4.2 %all-to-all-start.1 = ((f32[32,96,128]{2,1,0:T(8,128)}), f32[32,96,128]{2,1,0:T(8,128)S(1)}, u32[]{:S(2)}, u32[]{:S(2)}) async-start(f32[32,96,128]{2,1,0:T(8,128)} %broadcast_in_dim.20), calls=%async_computation.1 | async-start | bytes 3145728 | tf_op jit(solution)/shard_map/all_to_all | solution.py:363
  32.0 32.8 %all_gather.3 = f32[16,96,128]{2,1,0:T(8,128)S(1)} all-gather(f32[1,96,128]{2,1,0:T(8,128)S(1)} %bitcast.51), channel_id=1, replica_groups=mesh['row'=32,'col'=16] {'col'}, dimensions={0}, use_global_device_ids=true | all-gather | bytes 835584 | tf_op jit(solution)/shard_map/all_gather | solution.py:366
  64.8 0.5 copy.29
  65.3 0.0 all-to-all-done.1
  65.3 0.9 broadcast_in_dim.22
  66.2 13.5 %all-to-all-start.2 = ((f32[32,40,128]{2,1,0:T(8,128)}), f32[32,40,128]{2,1,0:T(8,128)S(1)}, u32[]{:S(2)}, u32[]{:S(2)}) async-start(f32[32,40,128]{2,1,0:T(8,128)} %broadcast_in_dim.22), calls=%async_computation.2 | async-start | bytes 1310720 | tf_op jit(solution)/shard_map/all_to_all | solution.py:363
  79.8 0.0 copy-start.3
  79.8 1.3 %copy.33 = f32[32,48,128]{2,1,0:T(8,128)} copy(f32[32,48,128]{2,0,1:T(8,128)S(1)} %bitcast.49) | data formatting | bytes 1572864 | tf_op jit(solution)/shard_map/reshape | solution.py:372
  81.1 11.6 %all-to-all-done.2 = f32[32,40,128]{2,1,0:T(8,128)S(1)} async-done(((f32[32,40,128]{2,1,0:T(8,128)}), f32[32,40,128]{2,1,0:T(8,128)S(1)}, u32[]{:S(2)}, u32[]{:S(2)}) %all-to-all-start.2) | async-done | bytes 655392 | tf_op jit(solution)/shard_map/all_to_all | solution.py:363
  92.7 4.1 %all-to-all-start.3 = ((f32[32,48,128]{2,1,0:T(8,128)}), f32[32,48,128]{2,1,0:T(8,128)S(1)}, u32[]{:S(2)}, u32[]{:S(2)}) async-start(f32[32,48,128]{2,1,0:T(8,128)} %copy.33), calls=%async_computation.3 | async-start | bytes 1572864 | tf_op jit(solution)/shard_map/all_to_all | solution.py:373
  96.8 0.7 constant_dynamic-slice_fusion
  97.5 0.1 reshape.50
  97.6 0.2 convert_reduce_fusion
  97.8 0.1 convert_element_type.8.pattern_ref
  97.8 16.3 %factor.1 = (f32[384,384]{1,0:T(8,128)S(1)}, f32[32,384]{1,0:T(8,128)S(1)}) custom-call(f32[1280,128]{1,0:T(8,128)S(1)} %bitcast.42), custom_call_target="tpu_custom_call" | custom-call | tf_op jit(solution)/shard_map/factor/pallas_call | solution.py:222
  114.1 0.8 copy-done
  114.9 0.0 all-to-all-done.3
  114.9 10.9 %finish.1 = (f32[4096,128]{1,0:T(8,128)}, f32[128,128]{1,0:T(8,128)}) custom-call(s32[4]{0:T(128)S(1)} %pad_add_fusion.where_ref, f32[32]{0:T(128)S(1)} %convert_element_type.8.pattern_ref, f32[4096,128]{1,0:T(8,128)} %bitcast.47, f32[3072,128]{1,0:T(8,128)S(1)} %bitcast.40, f32[384,384]{1,0:T(8,128)} %copy-done, f32[128,128]{1,0:T(8,128)} %bitcast.53, ...), custom_call_target="tpu_custom_call" | custom-call | tf_op jit(solution)/shard_map/finish/pallas_call | solution.py:247
  (14 shorter events, 0.1 us)
Async XLA Ops:
  0.7 0.8 copy-start.1
  1.6 0.7 copy-start.2
  27.8 37.5 %all-to-all-start.1 = ((f32[32,96,128]{2,1,0:T(8,128)}), f32[32,96,128]{2,1,0:T(8,128)S(1)}, u32[]{:S(2)}, u32[]{:S(2)}) async-start(f32[32,96,128]{2,1,0:T(8,128)} %broadcast_in_dim.20), calls=%async_computation.1 | async-start | bytes 3145728 | tf_op jit(solution)/shard_map/all_to_all | solution.py:363
  66.2 26.4 %all-to-all-start.2 = ((f32[32,40,128]{2,1,0:T(8,128)}), f32[32,40,128]{2,1,0:T(8,128)S(1)}, u32[]{:S(2)}, u32[]{:S(2)}) async-start(f32[32,40,128]{2,1,0:T(8,128)} %broadcast_in_dim.22), calls=%async_computation.2 | async-start | bytes 1310720 | tf_op jit(solution)/shard_map/all_to_all | solution.py:363
  79.8 35.2 %copy-start.3 = (f32[4,1,128]{2,1,0:T(1,128)S(1)}, f32[4,1,128]{2,1,0:T(1,128)}, u32[]{:S(2)}) copy-start(f32[4,1,128]{2,1,0:T(1,128)} %param.5) | copy-start | bytes 6148
  92.7 22.3 %all-to-all-start.3 = ((f32[32,48,128]{2,1,0:T(8,128)}), f32[32,48,128]{2,1,0:T(8,128)S(1)}, u32[]{:S(2)}, u32[]{:S(2)}) async-start(f32[32,48,128]{2,1,0:T(8,128)} %copy.33), calls=%async_computation.3 | async-start | bytes 1572864 | tf_op jit(solution)/shard_map/all_to_all | solution.py:373
  114.1 0.8 copy-start

commit v5 on v4

--- a/solution.py
+++ b/solution.py
@@ -1,3 +1,5 @@
+import functools
+
 import jax
 import jax.numpy as jnp
 from jax import lax
@@ -6,8 +8,9 @@
 from jax.sharding import PartitionSpec as P
 
 KB = 3
-SPAN = 32
+SPAN = 64
 STEP = 8
+UPPER = KB * (KB + 1) // 2
 
 precise = lax.Precision.HIGHEST
 
@@ -43,33 +46,46 @@
         right = [aug_ref[rows[j], blk:] for j in range(parts)]
         for i in range(parts):
             c0 = base + STEP * i
-            cols = [
-                jnp.broadcast_to(left[i][:, c0 + u : c0 + u + 1], (STEP, blk)) for u in range(STEP)
-            ]
-            pivots = jnp.ones((STEP, blk), jnp.float32)
-            inv = []
-            tops = {}
-            for t in range(STEP):
-                pivot = spread(cols[t], t)
-                pivots = jnp.where(sub == t, pivot, pivots)
-                inv.append(1.0 / pivot)
-                ratio = jnp.where(sub > t, cols[t] * inv[t], 0.0)
-                for u in range(t + 1, STEP):
-                    tops[t, u] = spread(cols[u], t)
-                    cols[u] = cols[u] - ratio * tops[t, u]
-                left[i] = left[i] - ratio * spread(left[i], t)
-                right[i] = right[i] - ratio * spread(right[i], t)
-            for j in range(i + 1, parts):
-                below = [
+
+            def columns(j):
+                return [
                     jnp.broadcast_to(left[j][:, c0 + u : c0 + u + 1], (STEP, blk))
                     for u in range(STEP)
                 ]
-                for t in range(STEP):
-                    ratio = below[t] * inv[t]
-                    for u in range(t + 1, STEP):
-                        below[u] = below[u] - ratio * tops[t, u]
-                    left[j] = left[j] - ratio * spread(left[i], t)
-                    right[j] = right[j] - ratio * spread(right[i], t)
+
+            cols = columns(i)
+            pivots = jnp.ones((STEP, blk), jnp.float32)
+            pairs = []
+            for t in range(0, STEP, 2):
+                a, b = spread(cols[t], t), spread(cols[t], t + 1)
+                c = spread(cols[t + 1], t + 1)
+                det = a * c - b * b
+                rdet = 1.0 / det
+                ra = 1.0 / a
+                pivots = jnp.where(sub == t, a, jnp.where(sub == t + 1, det * ra, pivots))
+                below = sub > t + 1
+                m0 = jnp.where(below, (c * cols[t] - b * cols[t + 1]) * rdet, 0.0)
+                m1 = jnp.where(below, (a * cols[t + 1] - b * cols[t]) * rdet, 0.0)
+                tops = {}
+                for u in range(t + 2, STEP):
+                    tops[u] = spread(cols[u], t), spread(cols[u], t + 1)
+                    cols[u] = cols[u] - (m0 * tops[u][0] + m1 * tops[u][1])
+                lt = spread(left[i], t), spread(left[i], t + 1)
+                rt = spread(right[i], t), spread(right[i], t + 1)
+                m0 = jnp.where(sub == t + 1, b * ra, m0)
+                left[i] = left[i] - (m0 * lt[0] + m1 * lt[1])
+                right[i] = right[i] - (m0 * rt[0] + m1 * rt[1])
+                pairs.append((a, b, c, rdet, tops, lt, rt))
+            for j in range(i + 1, parts):
+                cols = columns(j)
+                for n, (a, b, c, rdet, tops, lt, rt) in enumerate(pairs):
+                    t = 2 * n
+                    m0 = (c * cols[t] - b * cols[t + 1]) * rdet
+                    m1 = (a * cols[t + 1] - b * cols[t]) * rdet
+                    for u in range(t + 2, STEP):
+                        cols[u] = cols[u] - (m0 * tops[u][0] + m1 * tops[u][1])
+                    left[j] = left[j] - (m0 * lt[0] + m1 * lt[1])
+                    right[j] = right[j] - (m0 * rt[0] + m1 * rt[1])
             scale = lax.rsqrt(pivots)
             left[i] = left[i] * scale
             right[i] = right[i] * scale
@@ -87,12 +103,14 @@
     blk = aug_ref.shape[0]
     size = inv_ref.shape[0]
     count = found_ref.shape[0]
-    pitch = KB * KB + 1
+    pitch = UPPER + 2
+    t = 0
     for k in range(KB):
         for j in range(k, KB):
             a_ref[k * blk : (k + 1) * blk, j * blk : (j + 1) * blk] = diag_ref[
-                pl.ds(k * KB + j, blk, stride=pitch), :
+                pl.ds(t, blk, stride=pitch), :
             ]
+            t += 1
     inv_ref[...] = jnp.zeros(inv_ref.shape, jnp.float32)
     eye = lax.broadcasted_iota(jnp.int32, (blk, blk), 0) == lax.broadcasted_iota(
         jnp.int32, (blk, blk), 1
@@ -116,7 +134,7 @@
             inv_ref[k1:, :k1] = inv_ref[k1:, :k1] - tdot(up, inv_ref[k0:k1, :k1])
     first = jnp.concatenate(
         [
-            diag_ref[pl.ds(k * pitch + pitch - 1, count, stride=diag_ref.shape[0] // count), :]
+            diag_ref[pl.ds(k * pitch + UPPER, count, stride=diag_ref.shape[0] // count), :]
             for k in range(KB)
         ],
         axis=1,
@@ -142,9 +160,9 @@
 
 
 def finish_kernel(
-    where_ref, pattern_ref, x_hbm, cols_hbm, inv_hbm, rhs_hbm, support_ref, rows_ref, found_ref,
-    out_hbm, solved_ref, x_ref, cols_ref, inv_ref, rhs_ref, out_ref, row_ref, col_ref, sems,
-    out_sem,
+    where_ref, x_hbm, cols_hbm, inv_hbm, rhs_hbm, mask_hbm, support_hbm, rows_ref, found_ref,
+    out_hbm, solved_ref, x_ref, cols_ref, inv_ref, rhs_ref, mask_ref, support_ref, out_ref,
+    row_ref, col_ref, sems, out_sem,
 ):
     p = where_ref[0]
     q = where_ref[1]
@@ -157,7 +175,8 @@
     loads = [
         pltpu.make_async_copy(src, dst, sems.at[i])
         for i, (src, dst) in enumerate(
-            ((inv_hbm, inv_ref), (cols_hbm, cols_ref), (x_hbm, x_ref), (rhs_hbm, rhs_ref))
+            ((inv_hbm, inv_ref), (cols_hbm, cols_ref), (x_hbm, x_ref), (rhs_hbm, rhs_ref),
+             (mask_hbm, mask_ref), (support_hbm, support_ref))
         )
     ]
     for load in loads:
@@ -179,6 +198,8 @@
     solve(inv_ref, col_ref, blk)
     ri = lax.broadcasted_iota(jnp.int32, (blk, blk), 0)
     ci = lax.broadcasted_iota(jnp.int32, (blk, blk), 1)
+    loads[4].wait()
+    loads[5].wait()
     loads[2].wait()
     stores = []
     pair = 2
@@ -188,13 +209,14 @@
             l = g * pair + h
             mine = row_ref[:, l * blk : (l + 1) * blk]
             row_id = l * n_row + p
+            keep = kept(mask_ref, row_id, q, n_col, wide)
             diag = jnp.where(
                 ri == ci, jnp.broadcast_to(support_ref[l : l + 1, :], (blk, blk)), 0.0
             )
             for m in range(wide):
                 col_id = m * n_col + q
                 got = x_ref[pl.ds(l * part + m, blk, stride=wide), :]
-                got = got * pattern_ref[l * wide + m]
+                got = got * jnp.broadcast_to(keep[m : m + 1, :], (blk, blk))
                 got = got - term[h * blk : (h + 1) * blk, m * blk : (m + 1) * blk]
                 got = got + jnp.where(row_id == col_id, diag, 0.0)
                 if m == 0:
@@ -237,7 +259,7 @@
     )(diag)
 
 
-def finish_call(place, pattern, x, support, rhs, rows, cols, inv, found):
+def finish_call(place, x, mask, support, rhs, rows, cols, inv, found):
     rows_dev, blk = support.shape
     size = inv.shape[0]
     wide = x.shape[0] // (rows_dev * blk)
@@ -246,7 +268,7 @@
     near = pl.BlockSpec(memory_space=pltpu.VMEM)
     return pl.pallas_call(
         finish_kernel,
-        in_specs=[scalars, scalars, far, far, far, far] + [near] * 3,
+        in_specs=[scalars] + [far] * 6 + [near] * 2,
         out_specs=(far, near),
         out_shape=(
             jax.ShapeDtypeStruct(x.shape, jnp.float32),
@@ -257,28 +279,42 @@
             pltpu.VMEM(cols.shape, jnp.float32),
             pltpu.VMEM(inv.shape, jnp.float32),
             pltpu.VMEM(rhs.shape, jnp.float32),
+            pltpu.VMEM(mask.shape, jnp.int32),
+            pltpu.VMEM(support.shape, jnp.float32),
             pltpu.VMEM(x.shape, jnp.float32),
             pltpu.VMEM((size, rows_dev * blk), jnp.float32),
             pltpu.VMEM((size, wide * blk), jnp.float32),
-            pltpu.SemaphoreType.DMA((4,)),
+            pltpu.SemaphoreType.DMA((6,)),
             pltpu.SemaphoreType.DMA((rows_dev // 2,)),
         ],
         compiler_params=pltpu.CompilerParams(vmem_limit_bytes=14 << 20),
         name="finish",
     )(
         place,
-        pattern,
         x,
         cols,
         pltpu.with_memory_space_constraint(inv, pltpu.HBM),
         rhs,
+        mask,
         support,
         rows,
         found,
     )
 
 
-def start_kernel(where_ref, x_hbm, rhs_hbm, mask_ref, support_ref, out_ref, x_ref, rhs_ref, sems):
+def kept(mask_ref, row_id, q, n_col, wide):
+    blk = mask_ref.shape[1]
+    lane = lax.broadcasted_iota(jnp.int32, (wide, blk), 1)
+    col_id = lax.broadcasted_iota(jnp.int32, (wide, blk), 0) * n_col + q
+    own = jnp.broadcast_to(mask_ref[pl.ds(row_id, 1), :], (wide, blk)).astype(jnp.float32)
+    keep = jnp.sum(jnp.where(lane == col_id, own, 0.0), axis=1, keepdims=True)
+    return jnp.broadcast_to(keep, (wide, blk))
+
+
+def start_kernel(
+    where_ref, x_hbm, rhs_hbm, mask_hbm, support_hbm, out_ref, x_ref, rhs_ref, mask_ref,
+    support_ref, sems,
+):
     p = where_ref[0]
     q = where_ref[1]
     n_col = where_ref[3]
@@ -286,23 +322,23 @@
     n_row, pitch = out_ref.shape[0], out_ref.shape[1]
     wide = x_ref.shape[0] // blk
     sub = blk // n_row
-    loads = [
-        pltpu.make_async_copy(x_hbm.at[pl.ds(0, blk * wide), :], x_ref, sems.at[0]),
-        pltpu.make_async_copy(rhs_hbm, rhs_ref, sems.at[1]),
-    ]
+    pairs = (
+        (mask_hbm, mask_ref), (support_hbm, support_ref), (rhs_hbm, rhs_ref),
+        (x_hbm.at[pl.ds(0, blk * wide), :], x_ref),
+    )
+    loads = [pltpu.make_async_copy(src, dst, sems.at[i]) for i, (src, dst) in enumerate(pairs)]
     for load in loads:
         load.start()
+    for load in loads[:3]:
+        load.wait()
     lane = lax.broadcasted_iota(jnp.int32, (wide, blk), 1)
     col_id = lax.broadcasted_iota(jnp.int32, (wide, blk), 0) * n_col + q
-    own = jnp.broadcast_to(mask_ref[pl.ds(p, 1), :], (wide, blk)).astype(jnp.float32)
-    keep = jnp.sum(jnp.where(lane == col_id, own, 0.0), axis=1, keepdims=True)
-    keep = jnp.broadcast_to(keep, (wide, blk))
+    keep = kept(mask_ref, p, q, n_col, wide)
     added = jnp.where(col_id == p, jnp.broadcast_to(support_ref[0:1, :], (wide, blk)), 0.0)
-    loads[1].wait()
     step = rhs_ref.shape[0] // n_row
     first = rhs_ref[pl.ds(0, n_row, stride=step), :]
     zero = jnp.zeros((pitch - sub * wide - 1, blk), jnp.float32)
-    loads[0].wait()
+    loads[3].wait()
     for r in range(n_row):
         for s in range(sub):
             a = r * sub + s
@@ -314,21 +350,109 @@
 def start_call(place, x, rhs, mask, support, n_row, wide):
     blk = support.shape[1]
     far = pl.BlockSpec(memory_space=pltpu.HBM)
-    near = pl.BlockSpec(memory_space=pltpu.VMEM)
     pitch = blk // n_row * wide + 8
     return pl.pallas_call(
         start_kernel,
-        in_specs=[pl.BlockSpec(memory_space=pltpu.SMEM), far, far, near, near],
-        out_specs=near,
+        in_specs=[pl.BlockSpec(memory_space=pltpu.SMEM), far, far, far, far],
+        out_specs=pl.BlockSpec(memory_space=pltpu.VMEM),
         out_shape=jax.ShapeDtypeStruct((n_row, pitch, blk), jnp.float32),
         scratch_shapes=[
             pltpu.VMEM((blk * wide, blk), jnp.float32),
             pltpu.VMEM(rhs.shape, jnp.float32),
-            pltpu.SemaphoreType.DMA((2,)),
+            pltpu.VMEM(mask.shape, jnp.int32),
+            pltpu.VMEM(support.shape, jnp.float32),
+            pltpu.SemaphoreType.DMA((4,)),
         ],
         compiler_params=pltpu.CompilerParams(vmem_limit_bytes=4 << 20),
         name="start",
     )(place, x, rhs, mask, support)
+
+
+def send_copies(src_ref, out_hbm, sems):
+    copies = [
+        pltpu.make_async_copy(src_ref, out_hbm.at[r], sems.at[r]) for r in range(out_hbm.shape[0])
+    ]
+    for copy in copies:
+        copy.start()
+    for copy in copies:
+        copy.wait()
+
+
+def slice_kernel(got_hbm, mine_ref, out_hbm, got_ref, sem, sems, *, pitch, sub, wide):
+    load = pltpu.make_async_copy(got_hbm.at[pl.ds(0, KB * pitch), :], got_ref, sem)
+    load.start()
+    load.wait()
+    for a in range(sub):
+        for k in range(KB):
+            at = (a * KB + k) * wide
+            mine_ref[at : at + wide, :] = got_ref[k * pitch + a * wide : k * pitch + (a + 1) * wide, :]
+    send_copies(mine_ref, out_hbm, sems)
+
+
+def slice_call(got, n_row, sub, wide):
+    blk = got.shape[-1]
+    rows = sub * KB * wide
+    near = pl.BlockSpec(memory_space=pltpu.VMEM)
+    return pl.pallas_call(
+        functools.partial(slice_kernel, pitch=got.shape[1], sub=sub, wide=wide),
+        in_specs=[pl.BlockSpec(memory_space=pltpu.HBM)],
+        out_specs=(near, pl.BlockSpec(memory_space=pltpu.HBM)),
+        out_shape=(
+            jax.ShapeDtypeStruct((rows, blk), jnp.float32),
+            jax.ShapeDtypeStruct((n_row, rows, blk), jnp.float32),
+        ),
+        scratch_shapes=[
+            pltpu.VMEM((KB * got.shape[1], blk), jnp.float32),
+            pltpu.SemaphoreType.DMA,
+            pltpu.SemaphoreType.DMA((n_row,)),
+        ],
+        name="slice",
+    )(got.reshape(-1, blk))
+
+
+def diag_kernel(
+    every_hbm, got_hbm, out_hbm, every_ref, got_ref, tile_ref, in_sems, sems, *, pitch, sub, wide
+):
+    rows = sub * KB * wide
+    loads = [
+        pltpu.make_async_copy(every_hbm.at[pl.ds(0, KB * rows), :], every_ref, in_sems.at[0]),
+        pltpu.make_async_copy(got_hbm.at[pl.ds(0, KB * pitch), :], got_ref, in_sems.at[1]),
+    ]
+    for load in loads:
+        load.start()
+    for load in loads:
+        load.wait()
+    for a in range(sub):
+        parts = []
+        for k in range(KB):
+            for j in range(k, KB):
+                at = j * rows + (a * KB + k) * wide
+                parts.append(every_ref[at : at + 1, :])
+        at = min(a, KB - 1) * pitch + sub * wide
+        parts.append(got_ref[at : at + 1, :])
+        parts.append(jnp.zeros_like(parts[0]))
+        tile_ref[a * (UPPER + 2) : (a + 1) * (UPPER + 2), :] = jnp.concatenate(parts, axis=0)
+    send_copies(tile_ref, out_hbm, sems)
+
+
+def diag_call(every, got, n_row, sub, wide):
+    blk = got.shape[-1]
+    rows = sub * (UPPER + 2)
+    far = pl.BlockSpec(memory_space=pltpu.HBM)
+    return pl.pallas_call(
+        functools.partial(diag_kernel, pitch=got.shape[1], sub=sub, wide=wide),
+        in_specs=[far, far],
+        out_specs=far,
+        out_shape=jax.ShapeDtypeStruct((n_row, rows, blk), jnp.float32),
+        scratch_shapes=[
+            pltpu.VMEM((KB * sub * KB * wide, blk), jnp.float32),
+            pltpu.VMEM((KB * got.shape[1], blk), jnp.float32),
+            pltpu.VMEM((rows, blk), jnp.float32),
+            pltpu.SemaphoreType.DMA((2,)),
+            pltpu.SemaphoreType.DMA((n_row,)),
+        ],
+        name="diagonal",
+    )(every.reshape(-1, blk), got.reshape(-1, blk))
 
 
 def shards(front, support, mask, rhs):
@@ -342,40 +466,29 @@
     halves = n_row // n_col
     sub = blk // n_row
     count = rhs.shape[0]
-    mask_rows = lax.dynamic_index_in_dim(mask.reshape(rows_dev, n_row, -1), p, 1, keepdims=False)
-    pattern = lax.dynamic_index_in_dim(
-        mask_rows.reshape(rows_dev, cols_dev, n_col), q, 2, keepdims=False
-    ).astype(jnp.float32)
     place = jnp.stack([p, q, jnp.int32(n_row), jnp.int32(n_col)])
     x = pltpu.with_memory_space_constraint(
         front.reshape(rows_dev * blk * cols_dev, blk), pltpu.HBM
     )
+    mask = pltpu.with_memory_space_constraint(mask, pltpu.HBM)
+    support = pltpu.with_memory_space_constraint(support.reshape(rows_dev, blk), pltpu.HBM)
     values = pltpu.with_memory_space_constraint(rhs.reshape(count * rows_dev, blk), pltpu.HBM)
 
-    sent = start_call(place, x, values, mask, support[:, 0, :], n_row, cols_dev)
-    got = lax.all_to_all(sent, "row", 0, 0)[:KB]
-    mine = got[:, : sub * cols_dev].reshape(KB, sub, cols_dev, blk).transpose(1, 0, 2, 3)
-    mine = mine.reshape(sub * KB * cols_dev, blk)
-    mine_rhs = got[:, sub * cols_dev]
-
-    def to_all(part):
-        sent = jnp.broadcast_to(part[None], (n_row,) + part.shape)
-        return lax.all_to_all(sent, "row", 0, 0).reshape(-1, blk)
-
-    cols_got = to_all(mine)
-    every = lax.all_gather(mine, "col").reshape(n_col, sub, KB, rows_dev, halves, blk)
-    diag_part = every[:KB, :, :, 0, 0].transpose(1, 2, 0, 3).reshape(sub, KB * KB, blk)
-    rhs_part = jnp.concatenate([mine_rhs, jnp.zeros((sub - KB, blk), jnp.float32)], axis=0)
-    diag_part = jnp.concatenate([diag_part, rhs_part[:, None, :]], axis=1)
-    diag_part, cols_got = lax.optimization_barrier((diag_part, cols_got))
-    diag_got = to_all(diag_part.reshape(-1, blk))
+    sent = start_call(place, x, values, mask, support, n_row, cols_dev)
+    got = lax.all_to_all(sent, "row", 0, 0)
+    mine, cols_sent = slice_call(got, n_row, sub, cols_dev)
+    cols_got = lax.all_to_all(cols_sent, "row", 0, 0).reshape(-1, blk)
+    every = lax.all_gather(mine, "col")
+    diag_sent = diag_call(every, got, n_row, sub, cols_dev)
+    diag_sent, cols_got = lax.optimization_barrier((diag_sent, cols_got))
+    diag_got = lax.all_to_all(diag_sent, "row", 0, 0).reshape(-1, blk)
+    every = every.reshape(n_col, sub, KB, rows_dev, halves, blk)
     to_rows = every.transpose(4, 0, 1, 2, 3, 5).reshape(n_row, sub * KB * rows_dev, blk)
     rows_got = lax.all_to_all(to_rows, "row", 0, 0).reshape(-1, blk)
 
     inv, found = factor_call(diag_got, count)
     factor, solved = finish_call(
-        place, pattern.reshape(-1), x, support[:, 0, :], values, rows_got,
-        cols_got, inv, found,
+        place, x, mask, support, values, rows_got, cols_got, inv, found
     )
     return (factor.reshape(front.shape), solved.reshape(rhs.shape))
 

time: 127 us -> 126 us (level)
  local copies, waits for them, and re-layouts: 7.28 us -> 1.89 us
  Pallas kernels: 28.8 us -> 32.1 us
  blocking collectives: 55.3 us -> 57.2 us
    pallas_call x1 -> x3, Pallas kernels: 10.9 us -> 15.9 us  [the longest x1 10.9 us: finish_call(): pl.pallas_call(finish_kernel, in_specs=[scalars] + [far] * 6 + [near] * 2...]
    broadcast_in_dim x4 -> x0, local copies, waits for them, and re-layouts: 2.21 us -> none  [the longest x3 2.2 us: to_all(): sent = jnp.broadcast_to(part[None], (n_row,) + part.shape)]
    pallas_call x1, Pallas kernels: 16.3 us -> 14.5 us  [factor_call(): pl.pallas_call(factor_kernel, out_shape=(jax.ShapeDtypeStruct((size, size...]
    unnamed x9 -> x6, local copies, waits for them, and re-layouts: 2.34 us -> 0.81 us
    reshape x4 -> x0, local copies, waits for them, and re-layouts: 1.43 us -> none  [the longest x1 1.34 us: shards(): every.transpose(4, 0, 1, 2, 3, 5).reshape(n_row, sub * KB * rows_dev, blk)]
  transfers between devices with their start and end apart: 3 -> 3, of which waited for: 1 -> 1; matrix products, arithmetic and copies ran while one was open for 2% -> 1% of each run, Pallas kernels for 13% -> 13%
where the time goes in v5:
time: 126 us; the launch traced here: 125 us
  blocking collectives  57.2 us (45%)
  Pallas kernels  32.1 us (25%)
  starting transfers between devices  22.3 us (18%)
  waiting for transfers between devices  10.5 us (8%)
  local copies, waits for them, and re-layouts  1.89 us (2%)
    all_gather x1, blocking collectives, shards(): every = lax.all_gather(mine, 'col')  34 us
    all_to_all x1, blocking collectives, shards(): got = lax.all_to_all(sent, 'row', 0, 0)  23.2 us
    pallas_call x1, Pallas kernels, factor_call(): pl.pallas_call(factor_kernel, out_shape=(jax.ShapeDtypeStruct((size, size...  14.5 us
    all_to_all x1, starting transfers between devices, shards(): diag_got = lax.all_to_all(diag_sent, 'row', 0, 0).reshape(-1, blk)  14 us
    pallas_call x1, Pallas kernels, finish_call(): pl.pallas_call(finish_kernel, in_specs=[scalars] + [far] * 6 + [near] * 2...  10.9 us
    all_to_all x1, waiting for transfers between devices, shards(): diag_got = lax.all_to_all(diag_sent, 'row', 0, 0).reshape(-1, blk)  10.5 us
    all_to_all x1, starting transfers between devices, shards(): cols_got = lax.all_to_all(cols_sent, 'row', 0, 0).reshape(-1, blk)  4.31 us
    all_to_all x1, starting transfers between devices, shards(): rows_got = lax.all_to_all(to_rows, 'row', 0, 0).reshape(-1, blk)  4.02 us
  transfers between devices with their start and end apart: 3, of which 1 were waited for; matrix products, arithmetic and copies ran while one was open for 1% of the time, Pallas kernels for 13%

profile of v5, /device:TPU:1, one launch (start us, length us, event | category | flops | bytes accessed | tf_op | source)
XLA Modules:
  0.0 125.0 jit_solution(14066231961301854063)
XLA Ops:
  0.6 0.1 pad_add_fusion.where_ref
  0.7 1.8 %start.1 = f32[32,40,128]{2,1,0:T(8,128)S(1)} custom-call(s32[4]{0:T(128)S(1)} %pad_add_fusion.where_ref, f32[4096,128]{1,0:T(8,128)} %bitcast.22, f32[128,128]{1,0:T(8,128)} %bitcast.28, s32[128,128]{1,0:T(8,128)} %mask_hbm.3, f32[4,128]{1,0:T(4,128)} %bitcast.30), custom_call_target="tpu_custom_call" | custom-call | tf_op jit(solution)/shard_map/start/pallas_call | solution.py:354
  2.5 23.2 %all_to_all.20 = f32[32,40,128]{2,1,0:T(8,128)} all-to-all(f32[32,40,128]{2,1,0:T(8,128)S(1)} %start.1), channel_id=1, replica_groups=mesh['row'=32,'col'=16] {'row'}, dimensions={0} | all-to-all | bytes 1310720 | tf_op jit(solution)/shard_map/all_to_all | solution.py:478
  25.7 2.9 %slice.1 = (f32[96,128]{1,0:T(8,128)}, f32[32,96,128]{2,1,0:T(8,128)}) custom-call(f32[1280,128]{1,0:T(8,128)} %bitcast.25), custom_call_target="tpu_custom_call" | custom-call | tf_op jit(solution)/shard_map/slice/pallas_call | solution.py:396
  28.6 0.0 copy-start.2
  28.6 4.3 %all-to-all-start.1 = ((f32[32,96,128]{2,1,0:T(8,128)}), f32[32,96,128]{2,1,0:T(8,128)S(1)}, u32[]{:S(2)}, u32[]{:S(2)}) async-start(f32[32,96,128]{2,1,0:T(8,128)} %get-tuple-element.11), calls=%async_computation.1 | async-start | bytes 3145728 | tf_op jit(solution)/shard_map/all_to_all | solution.py:480
  32.9 0.0 copy-done.2
  32.9 34.0 %all-gather.every_hbm = f32[1536,128]{1,0:T(8,128)} all-gather(f32[96,128]{1,0:T(8,128)S(1)} %copy-done.2), channel_id=2, replica_groups=mesh['row'=32,'col'=16] {'col'}, dimensions={0}, use_global_device_ids=true | all-gather | bytes 835584 | tf_op jit(solution)/shard_map/all_gather | solution.py:481
  66.9 0.0 copy-start.1
  66.9 2.1 %diagonal.1 = f32[32,32,128]{2,1,0:T(8,128)} custom-call(f32[1536,128]{1,0:T(8,128)} %all-gather.every_hbm, f32[1280,128]{1,0:T(8,128)} %bitcast.26), custom_call_target="tpu_custom_call" | custom-call | tf_op jit(solution)/shard_map/diagonal/pallas_call | solution.py:442
  69.0 0.0 all-to-all-done.1
  69.1 14.0 %all-to-all-start.2 = ((f32[32,32,128]{2,1,0:T(8,128)}), f32[32,32,128]{2,1,0:T(8,128)S(1)}, u32[]{:S(2)}, u32[]{:S(2)}) async-start(f32[32,32,128]{2,1,0:T(8,128)} %diagonal.1), calls=%async_computation.2 | async-start | bytes 1048576 | tf_op jit(solution)/shard_map/all_to_all | solution.py:484
  83.0 0.0 copy-done.1
  83.0 1.1 copy.6
  84.1 10.5 %all-to-all-done.2 = f32[32,32,128]{2,1,0:T(8,128)S(1)} async-done(((f32[32,32,128]{2,1,0:T(8,128)}), f32[32,32,128]{2,1,0:T(8,128)S(1)}, u32[]{:S(2)}, u32[]{:S(2)}) %all-to-all-start.2) | async-done | bytes 524320 | tf_op jit(solution)/shard_map/all_to_all | solution.py:484
  94.6 4.0 %all-to-all-start.3 = ((f32[32,48,128]{2,1,0:T(8,128)}), f32[32,48,128]{2,1,0:T(8,128)S(1)}, u32[]{:S(2)}, u32[]{:S(2)}) async-start(f32[32,48,128]{2,1,0:T(8,128)} %bitcast.27), calls=%async_computation.3 | async-start | bytes 1572864 | tf_op jit(solution)/shard_map/all_to_all | solution.py:487
  98.6 14.5 %factor.1 = (f32[384,384]{1,0:T(8,128)S(1)}, f32[32,384]{1,0:T(8,128)S(1)}) custom-call(f32[1024,128]{1,0:T(8,128)S(1)} %bitcast.21), custom_call_target="tpu_custom_call" | custom-call | tf_op jit(solution)/shard_map/factor/pallas_call | solution.py:244
  113.1 0.0 copy-start
  113.1 0.8 copy-done
  113.9 0.0 all-to-all-done.3
  113.9 10.9 %finish.1 = (f32[4096,128]{1,0:T(8,128)}, f32[128,128]{1,0:T(8,128)}) custom-call(s32[4]{0:T(128)S(1)} %pad_add_fusion.where_ref, f32[4096,128]{1,0:T(8,128)} %bitcast.23, f32[3072,128]{1,0:T(8,128)S(1)} %bitcast.19, f32[384,384]{1,0:T(8,128)} %copy-done, f32[128,128]{1,0:T(8,128)} %bitcast.29, s32[128,128]{1,0:T(8,128)} %mask_hbm.3, f32[4,128]{1,0:T(4,128)} %bitcast.31, ...), custom_call_target="tpu_custom_call" | custom-call | tf_op jit(solution)/shard_map/finish/pallas_call | solution.py:269
Async XLA Ops:
  28.6 4.3 %copy-start.2 = (f32[96,128]{1,0:T(8,128)S(1)}, f32[96,128]{1,0:T(8,128)}, u32[]{:S(2)}) copy-start(f32[96,128]{1,0:T(8,128)} %get-tuple-element.10) | copy-start | bytes 147460
  28.6 40.5 %all-to-all-start.1 = ((f32[32,96,128]{2,1,0:T(8,128)}), f32[32,96,128]{2,1,0:T(8,128)S(1)}, u32[]{:S(2)}, u32[]{:S(2)}) async-start(f32[32,96,128]{2,1,0:T(8,128)} %get-tuple-element.11), calls=%async_computation.1 | async-start | bytes 3145728 | tf_op jit(solution)/shard_map/all_to_all | solution.py:480
  66.9 16.1 %copy-start.1 = (f32[1536,128]{1,0:T(8,128)S(1)}, f32[1536,128]{1,0:T(8,128)}, u32[]{:S(2)}) copy-start(f32[1536,128]{1,0:T(8,128)} %all-gather.every_hbm) | copy-start | bytes 2359300
  69.1 25.5 %all-to-all-start.2 = ((f32[32,32,128]{2,1,0:T(8,128)}), f32[32,32,128]{2,1,0:T(8,128)S(1)}, u32[]{:S(2)}, u32[]{:S(2)}) async-start(f32[32,32,128]{2,1,0:T(8,128)} %diagonal.1), calls=%async_computation.2 | async-start | bytes 1048576 | tf_op jit(solution)/shard_map/all_to_all | solution.py:484
  94.6 19.3 %all-to-all-start.3 = ((f32[32,48,128]{2,1,0:T(8,128)}), f32[32,48,128]{2,1,0:T(8,128)S(1)}, u32[]{:S(2)}, u32[]{:S(2)}) async-start(f32[32,48,128]{2,1,0:T(8,128)} %bitcast.27), calls=%async_computation.3 | async-start | bytes 1572864 | tf_op jit(solution)/shard_map/all_to_all | solution.py:487
  113.1 0.8 copy-start

commit v6 on v5

--- a/solution.py
+++ b/solution.py
@@ -1,5 +1,3 @@
-import functools
-
 import jax
 import jax.numpy as jnp
 from jax import lax
@@ -368,93 +366,6 @@
     )(place, x, rhs, mask, support)
 
 
-def send_copies(src_ref, out_hbm, sems):
-    copies = [
-        pltpu.make_async_copy(src_ref, out_hbm.at[r], sems.at[r]) for r in range(out_hbm.shape[0])
-    ]
-    for copy in copies:
-        copy.start()
-    for copy in copies:
-        copy.wait()
-
-
-def slice_kernel(got_hbm, mine_ref, out_hbm, got_ref, sem, sems, *, pitch, sub, wide):
-    load = pltpu.make_async_copy(got_hbm.at[pl.ds(0, KB * pitch), :], got_ref, sem)
-    load.start()
-    load.wait()
-    for a in range(sub):
-        for k in range(KB):
-            at = (a * KB + k) * wide
-            mine_ref[at : at + wide, :] = got_ref[k * pitch + a * wide : k * pitch + (a + 1) * wide, :]
-    send_copies(mine_ref, out_hbm, sems)
-
-
-def slice_call(got, n_row, sub, wide):
-    blk = got.shape[-1]
-    rows = sub * KB * wide
-    near = pl.BlockSpec(memory_space=pltpu.VMEM)
-    return pl.pallas_call(
-        functools.partial(slice_kernel, pitch=got.shape[1], sub=sub, wide=wide),
-        in_specs=[pl.BlockSpec(memory_space=pltpu.HBM)],
-        out_specs=(near, pl.BlockSpec(memory_space=pltpu.HBM)),
-        out_shape=(
-            jax.ShapeDtypeStruct((rows, blk), jnp.float32),
-            jax.ShapeDtypeStruct((n_row, rows, blk), jnp.float32),
-        ),
-        scratch_shapes=[
-            pltpu.VMEM((KB * got.shape[1], blk), jnp.float32),
-            pltpu.SemaphoreType.DMA,
-            pltpu.SemaphoreType.DMA((n_row,)),
-        ],
-        name="slice",
-    )(got.reshape(-1, blk))
-
-
-def diag_kernel(
-    every_hbm, got_hbm, out_hbm, every_ref, got_ref, tile_ref, in_sems, sems, *, pitch, sub, wide
-):
-    rows = sub * KB * wide
-    loads = [
-        pltpu.make_async_copy(every_hbm.at[pl.ds(0, KB * rows), :], every_ref, in_sems.at[0]),
-        pltpu.make_async_copy(got_hbm.at[pl.ds(0, KB * pitch), :], got_ref, in_sems.at[1]),
-    ]
-    for load in loads:
-        load.start()
-    for load in loads:
-        load.wait()
-    for a in range(sub):
-        parts = []
-        for k in range(KB):
-            for j in range(k, KB):
-                at = j * rows + (a * KB + k) * wide
-                parts.append(every_ref[at : at + 1, :])
-        at = min(a, KB - 1) * pitch + sub * wide
-        parts.append(got_ref[at : at + 1, :])
-        parts.append(jnp.zeros_like(parts[0]))
-        tile_ref[a * (UPPER + 2) : (a + 1) * (UPPER + 2), :] = jnp.concatenate(parts, axis=0)
-    send_copies(tile_ref, out_hbm, sems)
-
-
-def diag_call(every, got, n_row, sub, wide):
-    blk = got.shape[-1]
-    rows = sub * (UPPER + 2)
-    far = pl.BlockSpec(memory_space=pltpu.HBM)
-    return pl.pallas_call(
-        functools.partial(diag_kernel, pitch=got.shape[1], sub=sub, wide=wide),
-        in_specs=[far, far],
-        out_specs=far,
-        out_shape=jax.ShapeDtypeStruct((n_row, rows, blk), jnp.float32),
-        scratch_shapes=[
-            pltpu.VMEM((KB * sub * KB * wide, blk), jnp.float32),
-            pltpu.VMEM((KB * got.shape[1], blk), jnp.float32),
-            pltpu.VMEM((rows, blk), jnp.float32),
-            pltpu.SemaphoreType.DMA((2,)),
-            pltpu.SemaphoreType.DMA((n_row,)),
-        ],
-        name="diagonal",
-    )(every.reshape(-1, blk), got.reshape(-1, blk))
-
-
 def shards(front, support, mask, rhs):
     n_row = lax.axis_size("row")
     n_col = lax.axis_size("col")
@@ -475,14 +386,22 @@
     values = pltpu.with_memory_space_constraint(rhs.reshape(count * rows_dev, blk), pltpu.HBM)
 
     sent = start_call(place, x, values, mask, support, n_row, cols_dev)
-    got = lax.all_to_all(sent, "row", 0, 0)
-    mine, cols_sent = slice_call(got, n_row, sub, cols_dev)
-    cols_got = lax.all_to_all(cols_sent, "row", 0, 0).reshape(-1, blk)
-    every = lax.all_gather(mine, "col")
-    diag_sent = diag_call(every, got, n_row, sub, cols_dev)
-    diag_sent, cols_got = lax.optimization_barrier((diag_sent, cols_got))
-    diag_got = lax.all_to_all(diag_sent, "row", 0, 0).reshape(-1, blk)
-    every = every.reshape(n_col, sub, KB, rows_dev, halves, blk)
+    got = lax.all_to_all(sent, "row", 0, 0)[:KB]
+    mine = got[:, : sub * cols_dev].reshape(KB, sub, cols_dev, blk).transpose(1, 0, 2, 3)
+    mine = mine.reshape(sub * KB * cols_dev, blk)
+    mine_rhs = got[:, sub * cols_dev]
+
+    def to_all(part):
+        sent = jnp.broadcast_to(part[None], (n_row,) + part.shape)
+        return lax.all_to_all(sent, "row", 0, 0).reshape(-1, blk)
+
+    cols_got = to_all(mine)
+    every = lax.all_gather(mine, "col").reshape(n_col, sub, KB, rows_dev, halves, blk)
+    pieces = [every[k:KB, :, k, 0, 0].transpose(1, 0, 2) for k in range(KB)]
+    ends = jnp.pad(mine_rhs[:, None, :], ((0, sub - KB), (0, 1), (0, 0)))
+    diag_part = jnp.concatenate(pieces + [ends], axis=1).reshape(-1, blk)
+    diag_part, cols_got = lax.optimization_barrier((diag_part, cols_got))
+    diag_got = to_all(diag_part)
     to_rows = every.transpose(4, 0, 1, 2, 3, 5).reshape(n_row, sub * KB * rows_dev, blk)
     rows_got = lax.all_to_all(to_rows, "row", 0, 0).reshape(-1, blk)
 

time: 126 us -> 121 us (0.960)
  Pallas kernels: 32.1 us -> 27.2 us
  local copies, waits for them, and re-layouts: 1.89 us -> 4.83 us
  blocking collectives: 57.2 us -> 55.3 us
    pallas_call x2 -> x0, Pallas kernels: 4.95 us -> none  [the longest x1 2.85 us: slice_call(): pl.pallas_call(functools.partial(slice_kernel, pitch=got.shape[1], sub=su...]
    broadcast_in_dim x0 -> x2, local copies, waits for them, and re-layouts: none -> 2.19 us  [to_all(): sent = jnp.broadcast_to(part[None], (n_row,) + part.shape)]
    reshape x0 -> x3, local copies, waits for them, and re-layouts: none -> 1.35 us  [the longest x1 1.34 us: shards(): every.transpose(4, 0, 1, 2, 3, 5).reshape(n_row, sub * KB * rows_dev, blk)]
  transfers between devices with their start and end apart: 3 -> 3, of which waited for: 1 -> 1; matrix products, arithmetic and copies ran while one was open for 1% -> 2% of each run, Pallas kernels for 13% -> 12%
where the time goes in v6:
time: 121 us; the launch traced here: 120 us
  blocking collectives  55.3 us (46%)
  Pallas kernels  27.2 us (22%)
  starting transfers between devices  21.7 us (18%)
  waiting for transfers between devices  10.2 us (8%)
  local copies, waits for them, and re-layouts  4.83 us (4%)
    all_gather x1, blocking collectives, shards(): lax.all_gather(mine, 'col').reshape(n_col, sub, KB, rows_dev, halves, blk)  32.8 us
    all_to_all x1, blocking collectives, shards(): got = lax.all_to_all(sent, 'row', 0, 0)[:KB]  22.5 us
    all_to_all x2, starting transfers between devices, to_all(): return lax.all_to_all(sent, 'row', 0, 0).reshape(-1, blk)  17.7 us
    pallas_call x1, Pallas kernels, factor_call(): pl.pallas_call(factor_kernel, out_shape=(jax.ShapeDtypeStruct((size, size...  14.5 us
    pallas_call x1, Pallas kernels, finish_call(): pl.pallas_call(finish_kernel, in_specs=[scalars] + [far] * 6 + [near] * 2...  10.9 us
    all_to_all x2, waiting for transfers between devices, to_all(): return lax.all_to_all(sent, 'row', 0, 0).reshape(-1, blk)  10.2 us
    all_to_all x1, starting transfers between devices, shards(): rows_got = lax.all_to_all(to_rows, 'row', 0, 0).reshape(-1, blk)  4.02 us
  transfers between devices with their start and end apart: 3, of which 1 were waited for; matrix products, arithmetic and copies ran while one was open for 2% of the time, Pallas kernels for 12%

profile of v6, /device:TPU:1, one launch (start us, length us, event | category | flops | bytes accessed | tf_op | source)
XLA Modules:
  0.0 120.3 jit_solution(4524756158056283382)
XLA Ops:
  0.6 0.1 pad_add_fusion.where_ref
  0.7 1.8 %start.1 = f32[32,40,128]{2,1,0:T(8,128)S(1)} custom-call(s32[4]{0:T(128)S(1)} %pad_add_fusion.where_ref, f32[4096,128]{1,0:T(8,128)} %bitcast.43, f32[128,128]{1,0:T(8,128)} %bitcast.51, s32[128,128]{1,0:T(8,128)} %mask_hbm.3, f32[4,128]{1,0:T(4,128)} %bitcast.53), custom_call_target="tpu_custom_call" | custom-call | tf_op jit(solution)/shard_map/start/pallas_call | solution.py:352
  2.5 22.5 %all_to_all.20 = f32[32,40,128]{2,1,0:T(8,128)S(1)} all-to-all(f32[32,40,128]{2,1,0:T(8,128)S(1)} %start.1), channel_id=1, replica_groups=mesh['row'=32,'col'=16] {'row'}, dimensions={0} | all-to-all | bytes 1310720 | tf_op jit(solution)/shard_map/all_to_all | solution.py:389
  25.1 1.3 %broadcast_in_dim.14 = f32[32,96,128]{2,1,0:T(8,128)} broadcast(f32[96,128]{1,0:T(8,128)S(1)} %bitcast.49), dimensions={1,2} | broadcast | bytes 1622016 | tf_op jit(solution)/shard_map/broadcast_in_dim | solution.py:395
  26.4 4.2 %all-to-all-start.1 = ((f32[32,96,128]{2,1,0:T(8,128)}), f32[32,96,128]{2,1,0:T(8,128)S(1)}, u32[]{:S(2)}, u32[]{:S(2)}) async-start(f32[32,96,128]{2,1,0:T(8,128)} %broadcast_in_dim.14), calls=%async_computation.1 | async-start | bytes 3145728 | tf_op jit(solution)/shard_map/all_to_all | solution.py:396
  30.6 32.8 %all_gather.3 = f32[16,96,128]{2,1,0:T(8,128)S(1)} all-gather(f32[1,96,128]{2,1,0:T(8,128)S(1)} %bitcast.50), channel_id=1, replica_groups=mesh['row'=32,'col'=16] {'col'}, dimensions={0}, use_global_device_ids=true | all-gather | bytes 835584 | tf_op jit(solution)/shard_map/all_gather | solution.py:399
  63.4 0.5 copy.16
  63.9 0.0 all-to-all-done.1
  63.9 0.9 broadcast_in_dim.15
  64.8 13.5 %all-to-all-start.2 = ((f32[32,32,128]{2,1,0:T(8,128)}), f32[32,32,128]{2,1,0:T(8,128)S(1)}, u32[]{:S(2)}, u32[]{:S(2)}) async-start(f32[32,32,128]{2,1,0:T(8,128)} %broadcast_in_dim.15), calls=%async_computation.2 | async-start | bytes 1048576 | tf_op jit(solution)/shard_map/all_to_all | solution.py:396
  78.3 1.3 %copy.18 = f32[32,48,128]{2,1,0:T(8,128)} copy(f32[32,48,128]{2,0,1:T(8,128)S(1)} %bitcast.48) | data formatting | bytes 1572864 | tf_op jit(solution)/shard_map/reshape | solution.py:405
  79.6 10.2 %all-to-all-done.2 = f32[32,32,128]{2,1,0:T(8,128)S(1)} async-done(((f32[32,32,128]{2,1,0:T(8,128)}), f32[32,32,128]{2,1,0:T(8,128)S(1)}, u32[]{:S(2)}, u32[]{:S(2)}) %all-to-all-start.2) | async-done | bytes 524320 | tf_op jit(solution)/shard_map/all_to_all | solution.py:396
  89.9 4.0 %all-to-all-start.3 = ((f32[32,48,128]{2,1,0:T(8,128)}), f32[32,48,128]{2,1,0:T(8,128)S(1)}, u32[]{:S(2)}, u32[]{:S(2)}) async-start(f32[32,48,128]{2,1,0:T(8,128)} %copy.18), calls=%async_computation.3 | async-start | bytes 1572864 | tf_op jit(solution)/shard_map/all_to_all | solution.py:406
  93.9 14.5 %factor.1 = (f32[384,384]{1,0:T(8,128)S(1)}, f32[32,384]{1,0:T(8,128)S(1)}) custom-call(f32[1024,128]{1,0:T(8,128)S(1)} %bitcast.42), custom_call_target="tpu_custom_call" | custom-call | tf_op jit(solution)/shard_map/factor/pallas_call | solution.py:242
  108.4 0.0 copy-start
  108.4 0.8 copy-done
  109.2 0.0 all-to-all-done.3
  109.2 10.9 %finish.1 = (f32[4096,128]{1,0:T(8,128)}, f32[128,128]{1,0:T(8,128)}) custom-call(s32[4]{0:T(128)S(1)} %pad_add_fusion.where_ref, f32[4096,128]{1,0:T(8,128)} %bitcast.44, f32[3072,128]{1,0:T(8,128)S(1)} %bitcast.40, f32[384,384]{1,0:T(8,128)} %copy-done, f32[128,128]{1,0:T(8,128)} %bitcast.52, s32[128,128]{1,0:T(8,128)} %mask_hbm.3, f32[4,128]{1,0:T(4,128)} %bitcast.54, ...), custom_call_target="tpu_custom_call" | custom-call | tf_op jit(solution)/shard_map/finish/pallas_call | solution.py:267
  (7 shorter events, 0.0 us)
Async XLA Ops:
  26.4 37.5 %all-to-all-start.1 = ((f32[32,96,128]{2,1,0:T(8,128)}), f32[32,96,128]{2,1,0:T(8,128)S(1)}, u32[]{:S(2)}, u32[]{:S(2)}) async-start(f32[32,96,128]{2,1,0:T(8,128)} %broadcast_in_dim.14), calls=%async_computation.1 | async-start | bytes 3145728 | tf_op jit(solution)/shard_map/all_to_all | solution.py:396
  64.8 25.1 %all-to-all-start.2 = ((f32[32,32,128]{2,1,0:T(8,128)}), f32[32,32,128]{2,1,0:T(8,128)S(1)}, u32[]{:S(2)}, u32[]{:S(2)}) async-start(f32[32,32,128]{2,1,0:T(8,128)} %broadcast_in_dim.15), calls=%async_computation.2 | async-start | bytes 1048576 | tf_op jit(solution)/shard_map/all_to_all | solution.py:396
  89.9 19.3 %all-to-all-start.3 = ((f32[32,48,128]{2,1,0:T(8,128)}), f32[32,48,128]{2,1,0:T(8,128)S(1)}, u32[]{:S(2)}, u32[]{:S(2)}) async-start(f32[32,48,128]{2,1,0:T(8,128)} %copy.18), calls=%async_computation.3 | async-start | bytes 1572864 | tf_op jit(solution)/shard_map/all_to_all | solution.py:406
  108.4 0.8 copy-start

commit v7 on v6

--- a/solution.py
+++ b/solution.py
@@ -9,6 +9,16 @@
 SPAN = 64
 STEP = 8
 UPPER = KB * (KB + 1) // 2
+FIRST = (
+    ((0, 1), (1, 2), (2, 9)),
+    ((0, 2), (1, 9), (2, 0)),
+    ((0, 9), (1, 0), (2, 1)),
+)
+SECOND = (
+    ((2, 3), (9, 8), (0, 15), (1, 6)),
+    ((2, 4), (9, 10), (0, 14), (1, 7)),
+    ((2, 5), (9, 11), (0, 13), (1, 12)),
+)
 
 precise = lax.Precision.HIGHEST
 
@@ -101,8 +111,9 @@
     blk = aug_ref.shape[0]
     size = inv_ref.shape[0]
     count = found_ref.shape[0]
-    pitch = UPPER + 2
-    t = 0
+    pitch = diag_ref.shape[0] // blk
+    base = pitch - UPPER - 2
+    t = base
     for k in range(KB):
         for j in range(k, KB):
             a_ref[k * blk : (k + 1) * blk, j * blk : (j + 1) * blk] = diag_ref[
@@ -132,7 +143,7 @@
             inv_ref[k1:, :k1] = inv_ref[k1:, :k1] - tdot(up, inv_ref[k0:k1, :k1])
     first = jnp.concatenate(
         [
-            diag_ref[pl.ds(k * pitch + UPPER, count, stride=diag_ref.shape[0] // count), :]
+            diag_ref[pl.ds(k * pitch + base + UPPER, count, stride=diag_ref.shape[0] // count), :]
             for k in range(KB)
         ],
         axis=1,
@@ -142,12 +153,12 @@
         store.wait()
 
 
-def gather(got_ref, wide, to_ref):
+def gather(got_ref, wide, pitch, to_ref):
     blk = got_ref.shape[1]
     for k in range(KB):
         for j in range(wide):
             to_ref[k * blk : (k + 1) * blk, j * blk : (j + 1) * blk] = got_ref[
-                pl.ds(k * wide + j, blk, stride=KB * wide), :
+                pl.ds(k * wide + j, blk, stride=pitch), :
             ]
 
 
@@ -179,7 +190,7 @@
     ]
     for load in loads:
         load.start()
-    gather(rows_ref, rows_dev, row_ref)
+    gather(rows_ref, rows_dev, KB * rows_dev, row_ref)
     loads[0].wait()
     solve(inv_ref, row_ref, blk)
     loads[3].wait()
@@ -192,7 +203,7 @@
         solved_ref[pl.ds(l, count, stride=rows_dev), :] = got
 
     loads[1].wait()
-    gather(cols_ref, wide, col_ref)
+    gather(cols_ref, wide, cols_ref.shape[0] // blk, col_ref)
     solve(inv_ref, col_ref, blk)
     ri = lax.broadcasted_iota(jnp.int32, (blk, blk), 0)
     ci = lax.broadcasted_iota(jnp.int32, (blk, blk), 1)
@@ -366,6 +377,10 @@
     )(place, x, rhs, mask, support)
 
 
+def at_col(q, k):
+    return jnp.stack([(q == j).astype(jnp.float32) for j in range(k, KB)])[None, :, None]
+
+
 def shards(front, support, mask, rhs):
     n_row = lax.axis_size("row")
     n_col = lax.axis_size("col")
@@ -391,21 +406,30 @@
     mine = mine.reshape(sub * KB * cols_dev, blk)
     mine_rhs = got[:, sub * cols_dev]
 
-    def to_all(part):
-        sent = jnp.broadcast_to(part[None], (n_row,) + part.shape)
-        return lax.all_to_all(sent, "row", 0, 0).reshape(-1, blk)
-
-    cols_got = to_all(mine)
+    corner = mine.reshape(sub, KB, cols_dev, blk)[:, :, 0]
+    own = jnp.concatenate(
+        [corner[:, k : k + 1] * at_col(q, k) for k in range(KB)], axis=1
+    )
+    own = jnp.pad(own, ((0, 0), (0, 2), (0, 0)))
+    hub = own
+    for pairs in FIRST:
+        hub = hub + lax.ppermute(own, "col", pairs)
+    corner = hub
+    for pairs in SECOND:
+        corner = corner + lax.ppermute(hub, "col", pairs)
+    corner = corner + jnp.pad(mine_rhs[:, None, :], ((0, sub - KB), (UPPER, 1), (0, 0)))
+
+    part = jnp.concatenate([mine.reshape(sub, KB * cols_dev, blk), corner], axis=1)
+    part = part.reshape(-1, blk)
+    mine, part = lax.optimization_barrier((mine, part))
+    sent = jnp.broadcast_to(part[None], (n_row,) + part.shape)
+    cols_got = lax.all_to_all(sent, "row", 0, 0).reshape(-1, blk)
     every = lax.all_gather(mine, "col").reshape(n_col, sub, KB, rows_dev, halves, blk)
-    pieces = [every[k:KB, :, k, 0, 0].transpose(1, 0, 2) for k in range(KB)]
-    ends = jnp.pad(mine_rhs[:, None, :], ((0, sub - KB), (0, 1), (0, 0)))
-    diag_part = jnp.concatenate(pieces + [ends], axis=1).reshape(-1, blk)
-    diag_part, cols_got = lax.optimization_barrier((diag_part, cols_got))
-    diag_got = to_all(diag_part)
     to_rows = every.transpose(4, 0, 1, 2, 3, 5).reshape(n_row, sub * KB * rows_dev, blk)
+    to_rows, cols_got = lax.optimization_barrier((to_rows, cols_got))
     rows_got = lax.all_to_all(to_rows, "row", 0, 0).reshape(-1, blk)
 
-    inv, found = factor_call(diag_got, count)
+    inv, found = factor_call(cols_got, count)
     factor, solved = finish_call(
         place, x, mask, support, values, rows_got, cols_got, inv, found
     )

time: 121 us -> 132 us (1.091)
  starting transfers between devices: 21.7 us -> 51.2 us
  blocking collectives: 55.3 us -> 29.1 us
  waiting for transfers between devices: 10.2 us -> 16.2 us
  Pallas kernels: 27.2 us -> 28.9 us
    all_to_all x1 -> x0, blocking collectives: 22.5 us -> none  [shards(): got = lax.all_to_all(sent, 'row', 0, 0)[:KB]]
    ppermute x0 -> x6, starting transfers between devices: none -> 21.9 us  [the longest x3 18 us: shards(): hub = hub + lax.ppermute(own, 'col', pairs)]
    all_to_all x1, starting transfers between devices: 4.02 us -> 12.3 us  [shards(): rows_got = lax.all_to_all(to_rows, 'row', 0, 0).reshape(-1, blk)]
    all_gather x1, blocking collectives: 32.8 us -> 29.1 us  [shards(): lax.all_gather(mine, 'col').reshape(n_col, sub, KB, rows_dev, halves, blk)]
    ppermute x0 -> x6, waiting for transfers between devices: none -> 3.31 us  [the longest x3 2.54 us: shards(): hub = hub + lax.ppermute(own, 'col', pairs)]
    all_to_all x2, waiting for transfers between devices: 10.2 us -> 12.9 us  [the longest x1 12.9 us: shards(): got = lax.all_to_all(sent, 'row', 0, 0)[:KB]]
    optimization_barrier x0 -> x1, local copies, waits for them, and re-layouts: none -> 1.34 us  [shards(): to_rows, cols_got = lax.optimization_barrier((to_rows, cols_got))]
    reshape x1 -> x0, local copies, waits for them, and re-layouts: 1.34 us -> none  [shards(): every.transpose(4, 0, 1, 2, 3, 5).reshape(n_row, sub * KB * rows_dev, blk)]
  transfers between devices with their start and end apart: 3 -> 9, of which waited for: 1 -> 3; matrix products, arithmetic and copies ran while one was open for 2% -> 0% of each run, Pallas kernels for 12% -> 11%
where the time goes in v7:
time: 132 us; the launch traced here: 131 us
  starting transfers between devices  51.2 us (39%)
  blocking collectives  29.1 us (22%)
  Pallas kernels  28.9 us (22%)
  waiting for transfers between devices  16.2 us (12%)
  local copies, waits for them, and re-layouts  4.25 us (3%)
    all_gather x1, blocking collectives, shards(): lax.all_gather(mine, 'col').reshape(n_col, sub, KB, rows_dev, halves, blk)  29.1 us
    ppermute x3, starting transfers between devices, shards(): hub = hub + lax.ppermute(own, 'col', pairs)  18 us
    pallas_call x1, Pallas kernels, factor_call(): pl.pallas_call(factor_kernel, out_shape=(jax.ShapeDtypeStruct((size, size...  14.7 us
    all_to_all x1, waiting for transfers between devices, shards(): got = lax.all_to_all(sent, 'row', 0, 0)[:KB]  12.9 us
    all_to_all x1, starting transfers between devices, shards(): rows_got = lax.all_to_all(to_rows, 'row', 0, 0).reshape(-1, blk)  12.3 us
    pallas_call x1, Pallas kernels, finish_call(): pl.pallas_call(finish_kernel, in_specs=[scalars] + [far] * 6 + [near] * 2...  11.6 us
    all_to_all x1, starting transfers between devices, shards(): got = lax.all_to_all(sent, 'row', 0, 0)[:KB]  10.4 us
    all_to_all x1, starting transfers between devices, shards(): cols_got = lax.all_to_all(sent, 'row', 0, 0).reshape(-1, blk)  6.49 us
  transfers between devices with their start and end apart: 9, of which 3 were waited for; matrix products, arithmetic and copies ran while one was open for 0% of the time, Pallas kernels for 11%

profile of v7, /device:TPU:1, one launch (start us, length us, event | category | flops | bytes accessed | tf_op | source)
XLA Modules:
  0.0 131.1 jit_solution(4451868356012993033)
XLA Ops:
  0.6 0.1 pad_add_fusion.1.where_ref
  0.7 2.6 %start.1 = f32[32,40,128]{2,1,0:T(8,128)} custom-call(s32[4]{0:T(128)S(1)} %pad_add_fusion.1.where_ref, f32[4096,128]{1,0:T(8,128)} %bitcast.37, f32[128,128]{1,0:T(8,128)} %bitcast.44, s32[128,128]{1,0:T(8,128)} %mask_hbm.3, f32[4,128]{1,0:T(4,128)} %bitcast.51), custom_call_target="tpu_custom_call" | custom-call | tf_op jit(solution)/shard_map/start/pallas_call | solution.py:363
  3.3 10.4 %all-to-all-start = ((f32[32,40,128]{2,1,0:T(8,128)}), f32[32,40,128]{2,1,0:T(8,128)S(1)}, u32[]{:S(2)}, u32[]{:S(2)}) async-start(f32[32,40,128]{2,1,0:T(8,128)} %start.1), calls=%async_computation | async-start | bytes 1310720 | tf_op jit(solution)/shard_map/all_to_all | solution.py:404
  13.8 0.1 pad_maximum_fusion.2
  13.9 0.1 pad_maximum_fusion.1
  14.0 12.9 %all-to-all-done = f32[32,40,128]{2,1,0:T(8,128)S(1)} async-done(((f32[32,40,128]{2,1,0:T(8,128)}), f32[32,40,128]{2,1,0:T(8,128)S(1)}, u32[]{:S(2)}, u32[]{:S(2)}) %all-to-all-start) | async-done | bytes 655392 | tf_op jit(solution)/shard_map/all_to_all | solution.py:404
  26.9 0.1 broadcast_multiply_fusion.1
  27.0 2.9 %collective-permute-start.1 = (f32[4,8,128]{2,1,0:T(8,128)S(1)}, f32[4,8,128]{2,1,0:T(8,128)S(1)}, u32[]{:S(2)}, u32[]{:S(2)}) collective-permute-start(f32[4,8,128]{2,1,0:T(8,128)S(1)} %select_maximum_fusion), channel_id=1, source_target_pairs={{0,2},{1,9},{2,0},{16,18},{17,25},{18,16},{32,34},{33,41},{34,32},... | collective-permute-start | bytes 49160 | tf_op jit(solution)/shard_map/ppermute | solution.py:416
  30.0 13.2 %collective-permute-start = (f32[4,8,128]{2,1,0:T(8,128)S(1)}, f32[4,8,128]{2,1,0:T(8,128)S(1)}, u32[]{:S(2)}, u32[]{:S(2)}) collective-permute-start(f32[4,8,128]{2,1,0:T(8,128)S(1)} %select_maximum_fusion), channel_id=1, source_target_pairs={{0,1},{1,2},{2,9},{16,17},{17,18},{18,25},{32,33},{33,34},{34,41},... | collective-permute-start | bytes 49160 | tf_op jit(solution)/shard_map/ppermute | solution.py:416
  43.2 1.9 %collective-permute-start.2 = (f32[4,8,128]{2,1,0:T(8,128)S(1)}, f32[4,8,128]{2,1,0:T(8,128)S(1)}, u32[]{:S(2)}, u32[]{:S(2)}) collective-permute-start(f32[4,8,128]{2,1,0:T(8,128)S(1)} %select_maximum_fusion), channel_id=1, source_target_pairs={{0,9},{1,0},{2,1},{16,25},{17,16},{18,17},{32,41},{33,32},{34,33},... | collective-permute-start | bytes 49160 | tf_op jit(solution)/shard_map/ppermute | solution.py:416
  45.1 2.5 %collective-permute-done.2 = f32[4,8,128]{2,1,0:T(8,128)S(1)} collective-permute-done((f32[4,8,128]{2,1,0:T(8,128)S(1)}, f32[4,8,128]{2,1,0:T(8,128)S(1)}, u32[]{:S(2)}, u32[]{:S(2)}) %collective-permute-start.2) | collective-permute-done | bytes 16416 | tf_op jit(solution)/shard_map/ppermute | solution.py:416
  47.7 1.3 collective-permute-start.5
  49.0 1.3 collective-permute-start.4
  50.3 1.3 collective-permute-start.3
  51.7 0.8 collective-permute-done.3
  52.5 1.6 %broadcast_in_dim.2 = f32[32,128,128]{2,1,0:T(8,128)} broadcast(f32[128,128]{1,0:T(8,128)S(1)} %bitcast.46), dimensions={1,2} | broadcast | bytes 2162688 | tf_op jit(solution)/shard_map/broadcast_in_dim | solution.py:425
  54.0 6.5 %all-to-all-start.1 = ((f32[32,128,128]{2,1,0:T(8,128)}), f32[32,128,128]{2,1,0:T(8,128)S(1)}, u32[]{:S(2)}, u32[]{:S(2)}) async-start(f32[32,128,128]{2,1,0:T(8,128)} %broadcast_in_dim.2), calls=%async_computation.1 | async-start | bytes 4194304 | tf_op jit(solution)/shard_map/all_to_all | solution.py:426
  60.5 29.1 %all-gather = f32[1536,128]{1,0:T(8,128)S(1)} all-gather(f32[96,128]{1,0:T(8,128)S(1)} %bitcast.47), channel_id=2, replica_groups=mesh['row'=32,'col'=16] {'col'}, dimensions={0}, use_global_device_ids=true | all-gather | bytes 835584 | tf_op jit(solution)/shard_map/all_gather | solution.py:427
  89.6 0.5 copy.23
  90.1 1.3 %copy.24 = f32[32,48,128]{2,1,0:T(8,128)} copy(f32[32,48,128]{2,0,1:T(8,128)S(1)} %bitcast.39) | data formatting | bytes 1572864 | tf_op jit(solution)/shard_map/optimization_barrier | solution.py:429
  91.4 12.3 %all-to-all-start.2 = ((f32[32,48,128]{2,1,0:T(8,128)}), f32[32,48,128]{2,1,0:T(8,128)S(1)}, u32[]{:S(2)}, u32[]{:S(2)}) async-start(f32[32,48,128]{2,1,0:T(8,128)} %copy.24), calls=%async_computation.2 | async-start | bytes 1572864 | tf_op jit(solution)/shard_map/all_to_all | solution.py:430
  103.8 14.7 %factor.1 = (f32[384,384]{1,0:T(8,128)S(1)}, f32[32,384]{1,0:T(8,128)S(1)}) custom-call(f32[4096,128]{1,0:T(8,128)S(1)} %bitcast.34), custom_call_target="tpu_custom_call" | custom-call | tf_op jit(solution)/shard_map/factor/pallas_call | solution.py:253
  118.4 0.8 copy-done
  119.3 11.6 %finish.1 = (f32[4096,128]{1,0:T(8,128)}, f32[128,128]{1,0:T(8,128)}) custom-call(s32[4]{0:T(128)S(1)} %pad_add_fusion.1.where_ref, f32[4096,128]{1,0:T(8,128)} %bitcast.38, f32[4096,128]{1,0:T(8,128)S(1)} %bitcast.35, f32[384,384]{1,0:T(8,128)} %copy-done, f32[128,128]{1,0:T(8,128)} %bitcast.45, s32[128,128]{1,0:T(8,128)} %mask_hbm.3, f32[4,128]{1,0:T(4,128)} %bitcast.52, ...), custom_call_target="tpu_custom_call" | custom-call | tf_op jit(solution)/shard_map/finish/pallas_call | solution.py:278
  (19 shorter events, 0.2 us)
Async XLA Ops:
  3.3 23.5 %all-to-all-start = ((f32[32,40,128]{2,1,0:T(8,128)}), f32[32,40,128]{2,1,0:T(8,128)S(1)}, u32[]{:S(2)}, u32[]{:S(2)}) async-start(f32[32,40,128]{2,1,0:T(8,128)} %start.1), calls=%async_computation | async-start | bytes 1310720 | tf_op jit(solution)/shard_map/all_to_all | solution.py:404
  27.0 18.1 %collective-permute-start.1 = (f32[4,8,128]{2,1,0:T(8,128)S(1)}, f32[4,8,128]{2,1,0:T(8,128)S(1)}, u32[]{:S(2)}, u32[]{:S(2)}) collective-permute-start(f32[4,8,128]{2,1,0:T(8,128)S(1)} %select_maximum_fusion), channel_id=1, source_target_pairs={{0,2},{1,9},{2,0},{16,18},{17,25},{18,16},{32,34},{33,41},{34,32},... | collective-permute-start | bytes 49160 | tf_op jit(solution)/shard_map/ppermute | solution.py:416
  30.0 15.1 %collective-permute-start = (f32[4,8,128]{2,1,0:T(8,128)S(1)}, f32[4,8,128]{2,1,0:T(8,128)S(1)}, u32[]{:S(2)}, u32[]{:S(2)}) collective-permute-start(f32[4,8,128]{2,1,0:T(8,128)S(1)} %select_maximum_fusion), channel_id=1, source_target_pairs={{0,1},{1,2},{2,9},{16,17},{17,18},{18,25},{32,33},{33,34},{34,41},... | collective-permute-start | bytes 49160 | tf_op jit(solution)/shard_map/ppermute | solution.py:416
  43.2 4.5 %collective-permute-start.2 = (f32[4,8,128]{2,1,0:T(8,128)S(1)}, f32[4,8,128]{2,1,0:T(8,128)S(1)}, u32[]{:S(2)}, u32[]{:S(2)}) collective-permute-start(f32[4,8,128]{2,1,0:T(8,128)S(1)} %select_maximum_fusion), channel_id=1, source_target_pairs={{0,9},{1,0},{2,1},{16,25},{17,16},{18,17},{32,41},{33,32},{34,33},... | collective-permute-start | bytes 49160 | tf_op jit(solution)/shard_map/ppermute | solution.py:416
  47.7 4.0 %collective-permute-start.5 = (f32[4,8,128]{2,1,0:T(8,128)S(1)}, f32[4,8,128]{2,1,0:T(8,128)S(1)}, u32[]{:S(2)}, u32[]{:S(2)}) collective-permute-start(f32[4,8,128]{2,1,0:T(8,128)S(1)} %add_add_fusion), channel_id=1, source_target_pairs={{2,5},{9,11},{0,13},{1,12},{18,21},{25,27},{16,29},{17,28},{34,37}... | collective-permute-start | bytes 49160 | tf_op jit(solution)/shard_map/ppermute | solution.py:419
  49.0 2.7 %collective-permute-start.4 = (f32[4,8,128]{2,1,0:T(8,128)S(1)}, f32[4,8,128]{2,1,0:T(8,128)S(1)}, u32[]{:S(2)}, u32[]{:S(2)}) collective-permute-start(f32[4,8,128]{2,1,0:T(8,128)S(1)} %add_add_fusion), channel_id=1, source_target_pairs={{2,4},{9,10},{0,14},{1,7},{18,20},{25,26},{16,30},{17,23},{34,36},... | collective-permute-start | bytes 49160 | tf_op jit(solution)/shard_map/ppermute | solution.py:419
  50.3 2.1 %collective-permute-start.3 = (f32[4,8,128]{2,1,0:T(8,128)S(1)}, f32[4,8,128]{2,1,0:T(8,128)S(1)}, u32[]{:S(2)}, u32[]{:S(2)}) collective-permute-start(f32[4,8,128]{2,1,0:T(8,128)S(1)} %add_add_fusion), channel_id=1, source_target_pairs={{2,3},{9,8},{0,15},{1,6},{18,19},{25,24},{16,31},{17,22},{34,35},{... | collective-permute-start | bytes 49160 | tf_op jit(solution)/shard_map/ppermute | solution.py:419
  54.0 36.0 %all-to-all-start.1 = ((f32[32,128,128]{2,1,0:T(8,128)}), f32[32,128,128]{2,1,0:T(8,128)S(1)}, u32[]{:S(2)}, u32[]{:S(2)}) async-start(f32[32,128,128]{2,1,0:T(8,128)} %broadcast_in_dim.2), calls=%async_computation.1 | async-start | bytes 4194304 | tf_op jit(solution)/shard_map/all_to_all | solution.py:426
  91.4 27.8 %all-to-all-start.2 = ((f32[32,48,128]{2,1,0:T(8,128)}), f32[32,48,128]{2,1,0:T(8,128)S(1)}, u32[]{:S(2)}, u32[]{:S(2)}) async-start(f32[32,48,128]{2,1,0:T(8,128)} %copy.24), calls=%async_computation.2 | async-start | bytes 1572864 | tf_op jit(solution)/shard_map/all_to_all | solution.py:430
  118.4 0.8 copy-start

commit v8 on v6

--- a/solution.py
+++ b/solution.py
@@ -200,7 +200,7 @@
     loads[5].wait()
     loads[2].wait()
     stores = []
-    pair = 2
+    pair = 1
     for g in range(rows_dev // pair):
         term = tdot(row_ref[:, g * pair * blk : (g + 1) * pair * blk], col_ref[...])
         for h in range(pair):
@@ -242,7 +242,7 @@
     return pl.pallas_call(
         factor_kernel,
         out_shape=(
-            jax.ShapeDtypeStruct((size, size), jnp.float32),
+            pltpu.HBM((size, size), jnp.float32),
             jax.ShapeDtypeStruct((count, size), jnp.float32),
         ),
         out_specs=(pl.BlockSpec(memory_space=pltpu.HBM), pl.BlockSpec(memory_space=pltpu.VMEM)),
@@ -283,7 +283,7 @@
             pltpu.VMEM((size, rows_dev * blk), jnp.float32),
             pltpu.VMEM((size, wide * blk), jnp.float32),
             pltpu.SemaphoreType.DMA((6,)),
-            pltpu.SemaphoreType.DMA((rows_dev // 2,)),
+            pltpu.SemaphoreType.DMA((rows_dev,)),
         ],
         compiler_params=pltpu.CompilerParams(vmem_limit_bytes=14 << 20),
         name="finish",

time: 121 us -> 120 us (level)
  Pallas kernels: 27.2 us -> 25.9 us
  transfers between devices with their start and end apart: 3 -> 3, of which waited for: 1 -> 2; matrix products, arithmetic and copies ran while one was open for 2% -> 2% of each run, Pallas kernels for 12% -> 11%
where the time goes in v8:
time: 120 us; the launch traced here: 119 us
  blocking collectives  55.3 us (46%)
  Pallas kernels  25.9 us (22%)
  starting transfers between devices  21.7 us (18%)
  waiting for transfers between devices  11.1 us (9%)
  local copies, waits for them, and re-layouts  4 us (3%)
    all_gather x1, blocking collectives, shards(): lax.all_gather(mine, 'col').reshape(n_col, sub, KB, rows_dev, halves, blk)  32.8 us
    all_to_all x1, blocking collectives, shards(): got = lax.all_to_all(sent, 'row', 0, 0)[:KB]  22.5 us
    all_to_all x2, starting transfers between devices, to_all(): return lax.all_to_all(sent, 'row', 0, 0).reshape(-1, blk)  17.7 us
    pallas_call x1, Pallas kernels, factor_call(): pl.pallas_call(factor_kernel, out_shape=(pltpu.HBM((size, size), jnp.floa...  13.4 us
    pallas_call x1, Pallas kernels, finish_call(): pl.pallas_call(finish_kernel, in_specs=[scalars] + [far] * 6 + [near] * 2...  10.7 us
    all_to_all x2, waiting for transfers between devices, to_all(): return lax.all_to_all(sent, 'row', 0, 0).reshape(-1, blk)  10.2 us
    all_to_all x1, starting transfers between devices, shards(): rows_got = lax.all_to_all(to_rows, 'row', 0, 0).reshape(-1, blk)  4.02 us
  transfers between devices with their start and end apart: 3, of which 2 were waited for; matrix products, arithmetic and copies ran while one was open for 2% of the time, Pallas kernels for 11%

profile of v8, /device:TPU:1, one launch (start us, length us, event | category | flops | bytes accessed | tf_op | source)
XLA Modules:
  0.0 119.1 jit_solution(15221568519378971408)
XLA Ops:
  0.6 0.1 pad_add_fusion.where_ref
  0.7 1.8 %start.1 = f32[32,40,128]{2,1,0:T(8,128)S(1)} custom-call(s32[4]{0:T(128)S(1)} %pad_add_fusion.where_ref, f32[4096,128]{1,0:T(8,128)} %bitcast.43, f32[128,128]{1,0:T(8,128)} %bitcast.51, s32[128,128]{1,0:T(8,128)} %mask_hbm.3, f32[4,128]{1,0:T(4,128)} %bitcast.53), custom_call_target="tpu_custom_call" | custom-call | tf_op jit(solution)/shard_map/start/pallas_call | solution.py:352
  2.5 22.5 %all_to_all.20 = f32[32,40,128]{2,1,0:T(8,128)S(1)} all-to-all(f32[32,40,128]{2,1,0:T(8,128)S(1)} %start.1), channel_id=1, replica_groups=mesh['row'=32,'col'=16] {'row'}, dimensions={0} | all-to-all | bytes 1310720 | tf_op jit(solution)/shard_map/all_to_all | solution.py:389
  25.1 1.3 %broadcast_in_dim.14 = f32[32,96,128]{2,1,0:T(8,128)} broadcast(f32[96,128]{1,0:T(8,128)S(1)} %bitcast.49), dimensions={1,2} | broadcast | bytes 1622016 | tf_op jit(solution)/shard_map/broadcast_in_dim | solution.py:395
  26.4 4.2 %all-to-all-start.1 = ((f32[32,96,128]{2,1,0:T(8,128)}), f32[32,96,128]{2,1,0:T(8,128)S(1)}, u32[]{:S(2)}, u32[]{:S(2)}) async-start(f32[32,96,128]{2,1,0:T(8,128)} %broadcast_in_dim.14), calls=%async_computation.1 | async-start | bytes 3145728 | tf_op jit(solution)/shard_map/all_to_all | solution.py:396
  30.6 32.8 %all_gather.3 = f32[16,96,128]{2,1,0:T(8,128)S(1)} all-gather(f32[1,96,128]{2,1,0:T(8,128)S(1)} %bitcast.50), channel_id=1, replica_groups=mesh['row'=32,'col'=16] {'col'}, dimensions={0}, use_global_device_ids=true | all-gather | bytes 835584 | tf_op jit(solution)/shard_map/all_gather | solution.py:399
  63.4 0.5 copy.16
  63.9 0.0 all-to-all-done.1
  63.9 0.8 broadcast_in_dim.15
  64.8 13.5 %all-to-all-start.2 = ((f32[32,32,128]{2,1,0:T(8,128)}), f32[32,32,128]{2,1,0:T(8,128)S(1)}, u32[]{:S(2)}, u32[]{:S(2)}) async-start(f32[32,32,128]{2,1,0:T(8,128)} %broadcast_in_dim.15), calls=%async_computation.2 | async-start | bytes 1048576 | tf_op jit(solution)/shard_map/all_to_all | solution.py:396
  78.3 1.3 %copy.18 = f32[32,48,128]{2,1,0:T(8,128)} copy(f32[32,48,128]{2,0,1:T(8,128)S(1)} %bitcast.48) | data formatting | bytes 1572864 | tf_op jit(solution)/shard_map/reshape | solution.py:405
  79.6 10.2 %all-to-all-done.2 = f32[32,32,128]{2,1,0:T(8,128)S(1)} async-done(((f32[32,32,128]{2,1,0:T(8,128)}), f32[32,32,128]{2,1,0:T(8,128)S(1)}, u32[]{:S(2)}, u32[]{:S(2)}) %all-to-all-start.2) | async-done | bytes 524320 | tf_op jit(solution)/shard_map/all_to_all | solution.py:396
  89.8 4.0 %all-to-all-start.3 = ((f32[32,48,128]{2,1,0:T(8,128)}), f32[32,48,128]{2,1,0:T(8,128)S(1)}, u32[]{:S(2)}, u32[]{:S(2)}) async-start(f32[32,48,128]{2,1,0:T(8,128)} %copy.18), calls=%async_computation.3 | async-start | bytes 1572864 | tf_op jit(solution)/shard_map/all_to_all | solution.py:406
  93.9 13.4 %factor.1 = (f32[384,384]{1,0:T(8,128)}, f32[32,384]{1,0:T(8,128)S(1)}) custom-call(f32[1024,128]{1,0:T(8,128)S(1)} %bitcast.42), custom_call_target="tpu_custom_call" | custom-call | tf_op jit(solution)/shard_map/factor/pallas_call | solution.py:242
  107.3 0.9 all-to-all-done.3
  108.2 10.7 %finish.1 = (f32[4096,128]{1,0:T(8,128)}, f32[128,128]{1,0:T(8,128)}) custom-call(s32[4]{0:T(128)S(1)} %pad_add_fusion.where_ref, f32[4096,128]{1,0:T(8,128)} %bitcast.44, f32[3072,128]{1,0:T(8,128)S(1)} %bitcast.40, f32[384,384]{1,0:T(8,128)} %get-tuple-element.10.inv_hbm, f32[128,128]{1,0:T(8,128)} %bitcast.52, s32[128,128]{1,0:T(8,128)} %mask_hbm.3, ...), custom_call_target="tpu_custom_call" | custom-call | tf_op jit(solution)/shard_map/finish/pallas_call | solution.py:267
  (7 shorter events, 0.0 us)
Async XLA Ops:
  26.4 37.5 %all-to-all-start.1 = ((f32[32,96,128]{2,1,0:T(8,128)}), f32[32,96,128]{2,1,0:T(8,128)S(1)}, u32[]{:S(2)}, u32[]{:S(2)}) async-start(f32[32,96,128]{2,1,0:T(8,128)} %broadcast_in_dim.14), calls=%async_computation.1 | async-start | bytes 3145728 | tf_op jit(solution)/shard_map/all_to_all | solution.py:396
  64.8 25.1 %all-to-all-start.2 = ((f32[32,32,128]{2,1,0:T(8,128)}), f32[32,32,128]{2,1,0:T(8,128)S(1)}, u32[]{:S(2)}, u32[]{:S(2)}) async-start(f32[32,32,128]{2,1,0:T(8,128)} %broadcast_in_dim.15), calls=%async_computation.2 | async-start | bytes 1048576 | tf_op jit(solution)/shard_map/all_to_all | solution.py:396
  89.8 18.4 %all-to-all-start.3 = ((f32[32,48,128]{2,1,0:T(8,128)}), f32[32,48,128]{2,1,0:T(8,128)S(1)}, u32[]{:S(2)}, u32[]{:S(2)}) async-start(f32[32,48,128]{2,1,0:T(8,128)} %copy.18), calls=%async_computation.3 | async-start | bytes 1572864 | tf_op jit(solution)/shard_map/all_to_all | solution.py:406

commit v9 on v8

--- a/solution.py
+++ b/solution.py
@@ -396,12 +396,13 @@
         return lax.all_to_all(sent, "row", 0, 0).reshape(-1, blk)
 
     cols_got = to_all(mine)
-    every = lax.all_gather(mine, "col").reshape(n_col, sub, KB, rows_dev, halves, blk)
-    pieces = [every[k:KB, :, k, 0, 0].transpose(1, 0, 2) for k in range(KB)]
+    every = lax.all_gather(mine, "col")
+    pieces = [every[k:KB, k * cols_dev :: KB * cols_dev].transpose(1, 0, 2) for k in range(KB)]
     ends = jnp.pad(mine_rhs[:, None, :], ((0, sub - KB), (0, 1), (0, 0)))
     diag_part = jnp.concatenate(pieces + [ends], axis=1).reshape(-1, blk)
-    diag_part, cols_got = lax.optimization_barrier((diag_part, cols_got))
+    diag_part, cols_got, every = lax.optimization_barrier((diag_part, cols_got, every))
     diag_got = to_all(diag_part)
+    every = every.reshape(n_col, sub, KB, rows_dev, halves, blk)
     to_rows = every.transpose(4, 0, 1, 2, 3, 5).reshape(n_row, sub * KB * rows_dev, blk)
     rows_got = lax.all_to_all(to_rows, "row", 0, 0).reshape(-1, blk)
 

time: 120 us -> 119 us (level)
  no operation moved by 1% of the time
where the time goes in v9:
time: 119 us
  blocking collectives  55.3 us (46%)
  Pallas kernels  25.9 us (22%)
  starting transfers between devices  21.7 us (18%)
  waiting for transfers between devices  10.7 us (9%)
  local copies, waits for them, and re-layouts  4.05 us (3%)
    all_gather x1, blocking collectives, shards(): every = lax.all_gather(mine, 'col')  32.8 us
    all_to_all x1, blocking collectives, shards(): got = lax.all_to_all(sent, 'row', 0, 0)[:KB]  22.5 us
    all_to_all x2, starting transfers between devices, to_all(): return lax.all_to_all(sent, 'row', 0, 0).reshape(-1, blk)  17.7 us
    pallas_call x1, Pallas kernels, factor_call(): pl.pallas_call(factor_kernel, out_shape=(pltpu.HBM((size, size), jnp.floa...  13.4 us
    pallas_call x1, Pallas kernels, finish_call(): pl.pallas_call(finish_kernel, in_specs=[scalars] + [far] * 6 + [near] * 2...  10.7 us
    all_to_all x2, waiting for transfers between devices, to_all(): return lax.all_to_all(sent, 'row', 0, 0).reshape(-1, blk)  9.75 us
    all_to_all x1, starting transfers between devices, shards(): rows_got = lax.all_to_all(to_rows, 'row', 0, 0).reshape(-1, blk)  4.02 us
  transfers between devices with their start and end apart: 3, of which 2 were waited for; matrix products, arithmetic and copies ran while one was open for 2% of the time, Pallas kernels for 11%

profile of v9, /device:TPU:1, one launch (start us, length us, event | category | flops | bytes accessed | tf_op | source)
XLA Modules:
  0.0 118.7 jit_solution(18416181406057369267)
XLA Ops:
  0.6 0.1 pad_add_fusion.where_ref
  0.7 1.8 %start.1 = f32[32,40,128]{2,1,0:T(8,128)S(1)} custom-call(s32[4]{0:T(128)S(1)} %pad_add_fusion.where_ref, f32[4096,128]{1,0:T(8,128)} %bitcast.38, f32[128,128]{1,0:T(8,128)} %bitcast.43, s32[128,128]{1,0:T(8,128)} %mask_hbm.3, f32[4,128]{1,0:T(4,128)} %bitcast.47), custom_call_target="tpu_custom_call" | custom-call | tf_op jit(solution)/shard_map/start/pallas_call | solution.py:352
  2.5 22.5 %all_to_all.20 = f32[32,40,128]{2,1,0:T(8,128)S(1)} all-to-all(f32[32,40,128]{2,1,0:T(8,128)S(1)} %start.1), channel_id=1, replica_groups=mesh['row'=32,'col'=16] {'row'}, dimensions={0} | all-to-all | bytes 1310720 | tf_op jit(solution)/shard_map/all_to_all | solution.py:389
  25.1 1.3 %broadcast_in_dim.14 = f32[32,96,128]{2,1,0:T(8,128)} broadcast(f32[96,128]{1,0:T(8,128)S(1)} %bitcast.41), dimensions={1,2} | broadcast | bytes 1622016 | tf_op jit(solution)/shard_map/broadcast_in_dim | solution.py:395
  26.4 4.2 %all-to-all-start.1 = ((f32[32,96,128]{2,1,0:T(8,128)}), f32[32,96,128]{2,1,0:T(8,128)S(1)}, u32[]{:S(2)}, u32[]{:S(2)}) async-start(f32[32,96,128]{2,1,0:T(8,128)} %broadcast_in_dim.14), calls=%async_computation.1 | async-start | bytes 3145728 | tf_op jit(solution)/shard_map/all_to_all | solution.py:396
  30.6 32.8 %all_gather.3 = f32[16,96,128]{2,1,0:T(8,128)S(1)} all-gather(f32[1,96,128]{2,1,0:T(8,128)S(1)} %bitcast.42), channel_id=1, replica_groups=mesh['row'=32,'col'=16] {'col'}, dimensions={0}, use_global_device_ids=true | all-gather | bytes 835584 | tf_op jit(solution)/shard_map/all_gather | solution.py:399
  63.5 0.0 all-to-all-done.1
  63.5 0.8 broadcast_in_dim.15
  64.3 13.5 %all-to-all-start.2 = ((f32[32,32,128]{2,1,0:T(8,128)}), f32[32,32,128]{2,1,0:T(8,128)S(1)}, u32[]{:S(2)}, u32[]{:S(2)}) async-start(f32[32,32,128]{2,1,0:T(8,128)} %broadcast_in_dim.15), calls=%async_computation.2 | async-start | bytes 1048576 | tf_op jit(solution)/shard_map/all_to_all | solution.py:396
  77.9 0.5 copy.26
  78.3 1.3 %copy.27 = f32[32,48,128]{2,1,0:T(8,128)} copy(f32[32,48,128]{2,0,1:T(8,128)S(1)} %bitcast.40) | data formatting | bytes 1572864 | tf_op jit(solution)/shard_map/reshape | solution.py:406
  79.7 9.7 %all-to-all-done.2 = f32[32,32,128]{2,1,0:T(8,128)S(1)} async-done(((f32[32,32,128]{2,1,0:T(8,128)}), f32[32,32,128]{2,1,0:T(8,128)S(1)}, u32[]{:S(2)}, u32[]{:S(2)}) %all-to-all-start.2) | async-done | bytes 524320 | tf_op jit(solution)/shard_map/all_to_all | solution.py:396
  89.4 4.0 %all-to-all-start.3 = ((f32[32,48,128]{2,1,0:T(8,128)}), f32[32,48,128]{2,1,0:T(8,128)S(1)}, u32[]{:S(2)}, u32[]{:S(2)}) async-start(f32[32,48,128]{2,1,0:T(8,128)} %copy.27), calls=%async_computation.3 | async-start | bytes 1572864 | tf_op jit(solution)/shard_map/all_to_all | solution.py:407
  93.4 13.4 %factor.1 = (f32[384,384]{1,0:T(8,128)}, f32[32,384]{1,0:T(8,128)S(1)}) custom-call(f32[1024,128]{1,0:T(8,128)S(1)} %bitcast.37), custom_call_target="tpu_custom_call" | custom-call | tf_op jit(solution)/shard_map/factor/pallas_call | solution.py:242
  106.8 0.9 all-to-all-done.3
  107.8 10.7 %finish.1 = (f32[4096,128]{1,0:T(8,128)}, f32[128,128]{1,0:T(8,128)}) custom-call(s32[4]{0:T(128)S(1)} %pad_add_fusion.where_ref, f32[4096,128]{1,0:T(8,128)} %bitcast.39, f32[3072,128]{1,0:T(8,128)S(1)} %bitcast.35, f32[384,384]{1,0:T(8,128)} %get-tuple-element.11.inv_hbm, f32[128,128]{1,0:T(8,128)} %bitcast.44, s32[128,128]{1,0:T(8,128)} %mask_hbm.3, ...), custom_call_target="tpu_custom_call" | custom-call | tf_op jit(solution)/shard_map/finish/pallas_call | solution.py:267
  (9 shorter events, 0.1 us)
Async XLA Ops:
  26.4 37.1 %all-to-all-start.1 = ((f32[32,96,128]{2,1,0:T(8,128)}), f32[32,96,128]{2,1,0:T(8,128)S(1)}, u32[]{:S(2)}, u32[]{:S(2)}) async-start(f32[32,96,128]{2,1,0:T(8,128)} %broadcast_in_dim.14), calls=%async_computation.1 | async-start | bytes 3145728 | tf_op jit(solution)/shard_map/all_to_all | solution.py:396
  64.3 25.1 %all-to-all-start.2 = ((f32[32,32,128]{2,1,0:T(8,128)}), f32[32,32,128]{2,1,0:T(8,128)S(1)}, u32[]{:S(2)}, u32[]{:S(2)}) async-start(f32[32,32,128]{2,1,0:T(8,128)} %broadcast_in_dim.15), calls=%async_computation.2 | async-start | bytes 1048576 | tf_op jit(solution)/shard_map/all_to_all | solution.py:396
  89.4 18.4 %all-to-all-start.3 = ((f32[32,48,128]{2,1,0:T(8,128)}), f32[32,48,128]{2,1,0:T(8,128)S(1)}, u32[]{:S(2)}, u32[]{:S(2)}) async-start(f32[32,48,128]{2,1,0:T(8,128)} %copy.27), calls=%async_computation.3 | async-start | bytes 1572864 | tf_op jit(solution)/shard_map/all_to_all | solution.py:407
